TPU v7x, 32 devices: a whole 2x2x4 slice. The times are simulated.
32 devices in a mesh: dp: 8 (over z, core), tensor: 4 (over y, x).
Axes of the slice: x: 2, y: 2, z: 4, core: 2. Of those that a mesh axis runs over, the one named last changes fastest.
Arguments:
- image_tokens: bfloat16 [8192, 1536], P(('dp', 'tensor')), may hold values from -6 to 6
- text_tokens: bfloat16 [1024, 1536], P(('dp', 'tensor')), may hold values from -6 to 6
- conditioning: float32 [6, 1536], replicated, may hold values from -6 to 6
- slot_sequence: int32 [8], P('dp'), may hold values from 0 to 5, as said below
- rank_counts: int32 [8], P('dp'), may hold values from 0 to 1, as said below
- projection: bfloat16 [2, 2, 1536, 4608], P(None, None, 'dp', 'tensor'), may hold values from -0.15625 to 0.15625
- recombine: bfloat16 [2, 2, 1536, 1536], P(None, None, 'dp', 'tensor'), may hold values from -1.25 to 1.25
- expansion: bfloat16 [2, 2, 1536, 6144], P(None, None, 'dp', 'tensor'), may hold values from -0.15625 to 0.15625
- contraction: bfloat16 [2, 2, 1536, 6144], P(None, None, 'dp', 'tensor'), may hold values from -0.15625 to 0.15625
- modulation: bfloat16 [2, 2, 1536, 9216], P(None, None, ('dp', 'tensor')), may hold values from -0.15625 to 0.15625
- biases: bfloat16 [2, 2, 21504], P(None, None, ('dp', 'tensor')), may hold values from -1.796875 to 1.796875
- cotangent_image: bfloat16 [8192, 1536], P(('dp', 'tensor')), may hold values from -6 to 6
- cotangent_text: bfloat16 [1024, 1536], P(('dp', 'tensor')), may hold values from -6 to 6
Outputs:
- image_output: bfloat16 [8192, 1536], P(('dp', 'tensor'))
- text_output: bfloat16 [1024, 1536], P(('dp', 'tensor'))
- image_grad: float32 [8192, 1536], P(('dp', 'tensor'))
- text_grad: float32 [1024, 1536], P(('dp', 'tensor'))
- projection_grad: float32 [2, 2, 1536, 4608], P(None, None, 'dp', 'tensor')
- recombine_grad: float32 [2, 2, 1536, 1536], P(None, None, 'dp', 'tensor')
- expansion_grad: float32 [2, 2, 1536, 6144], P(None, None, 'dp', 'tensor')
- contraction_grad: float32 [2, 2, 1536, 6144], P(None, None, 'dp', 'tensor')
- modulation_grad: float32 [2, 2, 1536, 9216], P(None, None, ('dp', 'tensor'))
- biases_grad: float32 [2, 2, 21504], P(None, None, ('dp', 'tensor'))
Inputs may be any that keep to these rules, and one draw needn't show every extreme that they name: `rank_counts`: each dp rank's count is its number of live slots, which come first among its 1; the counts sum to 6 and at least one rank holds 1. `slot_sequence`: each of the 6 sequences is named by exactly one live slot; an empty slot names any sequence.
All inputs are finite; a program needn't handle non-finite values.
Results may differ from a plain program's by a relative error of at most 0.03.
Values may be sent and summed in bfloat16 or wider, within the bound.
A program may use at most 320 MiB of HBM per device.

v0:
```python
import jax
import jax.numpy as jnp
from jax import lax
from jax.sharding import PartitionSpec as P

D = 1536
HEADS = 24
HEAD_DIM = 64
FF = 6144
LAYERS = 2
IMG = 1024
TXT = 128
CAP = 1


highest = lax.Precision.HIGHEST
contract_columns = (((1,), (1,)), ((), ()))
contract_rows = (((0,), (0,)), ((), ()))


def normalize(values):
    average = jnp.mean(values, -1, keepdims=True)
    centred = values - average
    spread = jnp.mean(centred * centred, -1, keepdims=True)
    return centred * lax.rsqrt(spread + 1e-06)


def modulate(values, shifts, scales):
    return normalize(values) * (1.0 + scales) + shifts


def gelu_tanh(values):
    return jax.nn.gelu(values, approximate=True)


def slot_select(count_rows, length, offset):
    places = offset + jnp.arange(count_rows, dtype=jnp.int32)
    return (places[:, None] // length == jnp.arange(CAP, dtype=jnp.int32)[None, :]).astype(
        jnp.float32
    )


def spread_rows(select, per_slot):
    return jnp.dot(select, per_slot, precision=highest)


def slot_totals(select, per_row):
    return lax.dot_general(select, per_row, contract_rows, precision=highest)


def to_items(image_part, text_part, heads_local):
    joined = jnp.concatenate(
        [
            image_part.reshape(CAP, IMG, heads_local, HEAD_DIM),
            text_part.reshape(CAP, TXT, heads_local, HEAD_DIM),
        ],
        axis=1,
    )
    return joined.transpose(0, 2, 1, 3).reshape(CAP * heads_local, IMG + TXT, HEAD_DIM)


def from_items(head_items, heads_local):
    joined = head_items.reshape(CAP, heads_local, IMG + TXT, HEAD_DIM).transpose(0, 2, 1, 3)
    return (
        joined[:, :IMG].reshape(CAP * IMG, heads_local * HEAD_DIM),
        joined[:, IMG:].reshape(CAP * TXT, heads_local * HEAD_DIM),
    )


def attend_item(entries):
    queries, key_rows, values = entries
    scores = jnp.einsum(
        "qe,ke->qk", queries, key_rows, preferred_element_type=jnp.float32
    ) * HEAD_DIM ** (-0.5)
    row_max = jnp.max(scores, -1, keepdims=True)
    weights = jnp.exp(scores - row_max)
    totals = jnp.sum(weights, -1, keepdims=True)
    output = jnp.einsum(
        "qk,ke->qe",
        (weights / totals).astype(jnp.bfloat16),
        values,
        preferred_element_type=jnp.float32,
    )
    return (output.astype(jnp.bfloat16), row_max[:, 0] + jnp.log(totals[:, 0]))


def attend_back(entries):
    queries, key_rows, values, logsum, grad_output = entries
    scores = jnp.einsum(
        "qe,ke->qk", queries, key_rows, preferred_element_type=jnp.float32
    ) * HEAD_DIM ** (-0.5)
    weights = jnp.exp(scores - logsum[:, None])
    grad_weights = jnp.einsum("qe,ke->qk", grad_output, values, preferred_element_type=jnp.float32)
    row_inner = jnp.sum(weights * grad_weights, -1, keepdims=True)
    grad_scores = (weights * (grad_weights - row_inner)).astype(jnp.bfloat16)
    grad_query = jnp.einsum(
        "qk,ke->qe", grad_scores, key_rows, preferred_element_type=jnp.float32
    ) * HEAD_DIM ** (-0.5)
    grad_key = jnp.einsum(
        "qk,qe->ke", grad_scores, queries, preferred_element_type=jnp.float32
    ) * HEAD_DIM ** (-0.5)
    grad_value = jnp.einsum(
        "qk,qe->ke", weights.astype(jnp.bfloat16), grad_output, preferred_element_type=jnp.float32
    )
    return (
        grad_query.astype(jnp.bfloat16),
        grad_key.astype(jnp.bfloat16),
        grad_value.astype(jnp.bfloat16),
    )


def layer_biases(bias_layer, tensor_rank, width_local, hidden_local):
    query_bias = lax.dynamic_slice_in_dim(
        bias_layer, 6 * D + tensor_rank * width_local, width_local, 1
    )
    value_bias = lax.dynamic_slice_in_dim(
        bias_layer, 7 * D + tensor_rank * width_local, width_local, 1
    )
    out_bias = bias_layer[:, 8 * D : 9 * D]
    hidden_bias = lax.dynamic_slice_in_dim(
        bias_layer, 9 * D + tensor_rank * hidden_local, hidden_local, 1
    )
    last_bias = bias_layer[:, 9 * D + FF :]
    return (query_bias, value_bias, out_bias, hidden_bias, last_bias)


def forward_layer(states, gathered, pieces, row_shifts, heads_local):
    query_bias, value_bias, out_bias, hidden_bias, last_bias = pieces
    normed = [
        modulate(states[stream], row_shifts[stream][0], row_shifts[stream][1]).astype(jnp.bfloat16)
        for stream in range(2)
    ]
    joined = (
        lax.all_gather(normed[0], "tensor", axis=0, tiled=True),
        lax.all_gather(normed[1], "tensor", axis=0, tiled=True),
    )
    projected = []
    for stream in range(2):
        columns = jnp.dot(
            joined[stream], gathered[0][stream], preferred_element_type=jnp.float32
        ).reshape(-1, heads_local, 3, HEAD_DIM)
        queries = (columns[:, :, 0] + query_bias[stream].reshape(heads_local, HEAD_DIM)).astype(
            jnp.bfloat16
        )
        key_rows = columns[:, :, 1].astype(jnp.bfloat16)
        values = (columns[:, :, 2] + value_bias[stream].reshape(heads_local, HEAD_DIM)).astype(
            jnp.bfloat16
        )
        projected.append((queries, key_rows, values))
    head_items = tuple(
        (
            to_items(projected[0][kind_index], projected[1][kind_index], heads_local)
            for kind_index in range(3)
        )
    )
    attended, logsum = lax.map(attend_item, head_items)
    out_rows = from_items(attended, heads_local)
    summed = (
        lax.psum_scatter(
            lax.dot_general(
                out_rows[0], gathered[1][0], contract_columns, preferred_element_type=jnp.float32
            ).astype(jnp.bfloat16),
            "tensor",
            scatter_dimension=0,
            tiled=True,
        ).astype(jnp.float32),
        lax.psum_scatter(
            lax.dot_general(
                out_rows[1], gathered[1][1], contract_columns, preferred_element_type=jnp.float32
            ).astype(jnp.bfloat16),
            "tensor",
            scatter_dimension=0,
            tiled=True,
        ).astype(jnp.float32),
    )
    branch_attend = [summed[stream] + out_bias[stream] for stream in range(2)]
    middle = [states[stream] + row_shifts[stream][2] * branch_attend[stream] for stream in range(2)]
    normed_feed = [
        modulate(middle[stream], row_shifts[stream][3], row_shifts[stream][4]).astype(jnp.bfloat16)
        for stream in range(2)
    ]
    joined_feed = (
        lax.all_gather(normed_feed[0], "tensor", axis=0, tiled=True),
        lax.all_gather(normed_feed[1], "tensor", axis=0, tiled=True),
    )
    preact = [
        jnp.dot(joined_feed[stream], gathered[2][stream], preferred_element_type=jnp.float32)
        + hidden_bias[stream]
        for stream in range(2)
    ]
    feed_terms = [
        lax.dot_general(
            gelu_tanh(preact[stream]).astype(jnp.bfloat16),
            gathered[3][stream],
            contract_columns,
            preferred_element_type=jnp.float32,
        )
        for stream in range(2)
    ]
    summed_feed = (
        lax.psum_scatter(
            feed_terms[0].astype(jnp.bfloat16), "tensor", scatter_dimension=0, tiled=True
        ).astype(jnp.float32),
        lax.psum_scatter(
            feed_terms[1].astype(jnp.bfloat16), "tensor", scatter_dimension=0, tiled=True
        ).astype(jnp.float32),
    )
    branch_feed = [summed_feed[stream] + last_bias[stream] for stream in range(2)]
    result = [middle[stream] + row_shifts[stream][5] * branch_feed[stream] for stream in range(2)]
    record = (
        states,
        joined,
        head_items,
        logsum,
        out_rows,
        branch_attend,
        middle,
        joined_feed,
        preact,
        branch_feed,
    )
    return (record, result)


def backward_layer(gradients, record, gathered, row_shifts, selects, heads_local, tensor_rank):
    (
        states,
        joined,
        head_items,
        logsum,
        out_rows,
        branch_attend,
        middle,
        joined_feed,
        preact,
        branch_feed,
    ) = record
    width_local = heads_local * HEAD_DIM
    hidden_local = preact[0].shape[1]
    grad_branch = [row_shifts[stream][5] * gradients[stream] for stream in range(2)]
    gate_feed = [
        slot_totals(selects[stream], gradients[stream] * branch_feed[stream]) for stream in range(2)
    ]
    branch_rows = (
        lax.all_gather(grad_branch[0].astype(jnp.bfloat16), "tensor", axis=0, tiled=True),
        lax.all_gather(grad_branch[1].astype(jnp.bfloat16), "tensor", axis=0, tiled=True),
    )
    grad_expansion, grad_contraction, hidden_sums, partials = ([], [], [], [])
    for stream in range(2):
        activated, gelu_back = jax.vjp(gelu_tanh, preact[stream])
        grad_activated = jnp.dot(
            branch_rows[stream], gathered[3][stream], preferred_element_type=jnp.float32
        )
        grad_contraction.append(
            lax.dot_general(
                branch_rows[stream],
                activated.astype(jnp.bfloat16),
                contract_rows,
                preferred_element_type=jnp.float32,
            )
        )
        grad_preact = gelu_back(grad_activated)[0].astype(jnp.bfloat16)
        hidden_sums.append(jnp.sum(grad_preact, 0, dtype=jnp.float32))
        grad_expansion.append(
            lax.dot_general(
                joined_feed[stream], grad_preact, contract_rows, preferred_element_type=jnp.float32
            )
        )
        partials.append(
            lax.dot_general(
                grad_preact,
                gathered[2][stream],
                contract_columns,
                preferred_element_type=jnp.float32,
            )
        )
    summed = (
        lax.psum_scatter(
            partials[0].astype(jnp.bfloat16), "tensor", scatter_dimension=0, tiled=True
        ).astype(jnp.float32),
        lax.psum_scatter(
            partials[1].astype(jnp.bfloat16), "tensor", scatter_dimension=0, tiled=True
        ).astype(jnp.float32),
    )
    grad_middle, shift_feed, scale_feed = ([], [], [])
    for stream in range(2):
        normed_value, shift_back = jax.vjp(
            modulate, middle[stream], row_shifts[stream][3], row_shifts[stream][4]
        )
        back_rows, back_shift, back_scale = shift_back(summed[stream])
        grad_middle.append(gradients[stream] + back_rows)
        shift_feed.append(slot_totals(selects[stream], back_shift))
        scale_feed.append(slot_totals(selects[stream], back_scale))
    grad_attend = [row_shifts[stream][2] * grad_middle[stream] for stream in range(2)]
    gate_attend = [
        slot_totals(selects[stream], grad_middle[stream] * branch_attend[stream])
        for stream in range(2)
    ]
    attend_rows = (
        lax.all_gather(grad_attend[0].astype(jnp.bfloat16), "tensor", axis=0, tiled=True),
        lax.all_gather(grad_attend[1].astype(jnp.bfloat16), "tensor", axis=0, tiled=True),
    )
    grad_recombine = [
        lax.dot_general(
            attend_rows[stream], out_rows[stream], contract_rows, preferred_element_type=jnp.float32
        )
        for stream in range(2)
    ]
    grad_heads = [
        jnp.dot(
            attend_rows[stream], gathered[1][stream], preferred_element_type=jnp.float32
        ).astype(jnp.bfloat16)
        for stream in range(2)
    ]
    grad_query, grad_key, grad_value = lax.map(
        attend_back,
        (
            head_items[0],
            head_items[1],
            head_items[2],
            logsum,
            to_items(grad_heads[0], grad_heads[1], heads_local),
        ),
    )
    query_rows = from_items(grad_query, heads_local)
    key_rows = from_items(grad_key, heads_local)
    value_rows = from_items(grad_value, heads_local)
    grad_projection, partials, query_sums, value_sums = ([], [], [], [])
    for stream in range(2):
        stacked = jnp.stack(
            [
                query_rows[stream].reshape(-1, heads_local, HEAD_DIM),
                key_rows[stream].reshape(-1, heads_local, HEAD_DIM),
                value_rows[stream].reshape(-1, heads_local, HEAD_DIM),
            ],
            axis=2,
        ).reshape(-1, 3 * width_local)
        query_sums.append(jnp.sum(query_rows[stream], 0, dtype=jnp.float32))
        value_sums.append(jnp.sum(value_rows[stream], 0, dtype=jnp.float32))
        grad_projection.append(
            lax.dot_general(
                joined[stream], stacked, contract_rows, preferred_element_type=jnp.float32
            )
        )
        partials.append(
            lax.dot_general(
                stacked, gathered[0][stream], contract_columns, preferred_element_type=jnp.float32
            )
        )
    summed = (
        lax.psum_scatter(
            partials[0].astype(jnp.bfloat16), "tensor", scatter_dimension=0, tiled=True
        ).astype(jnp.float32),
        lax.psum_scatter(
            partials[1].astype(jnp.bfloat16), "tensor", scatter_dimension=0, tiled=True
        ).astype(jnp.float32),
    )
    new_grads, shift_grads, bias_grads = ([], [], [])
    for stream in range(2):
        normed_value, shift_back = jax.vjp(
            modulate, states[stream], row_shifts[stream][0], row_shifts[stream][1]
        )
        back_rows, back_shift, back_scale = shift_back(summed[stream])
        new_grads.append(grad_middle[stream] + back_rows)
        slot_grad = jnp.concatenate(
            [
                slot_totals(selects[stream], back_shift),
                slot_totals(selects[stream], back_scale),
                gate_attend[stream],
                shift_feed[stream],
                scale_feed[stream],
                gate_feed[stream],
            ],
            axis=1,
        )
        shift_grads.append(slot_grad)
        bias_grads.append(
            jnp.concatenate(
                [
                    jnp.sum(slot_grad, 0),
                    lax.dynamic_update_slice_in_dim(
                        jnp.zeros((D,), jnp.float32),
                        query_sums[stream],
                        tensor_rank * width_local,
                        0,
                    ),
                    lax.dynamic_update_slice_in_dim(
                        jnp.zeros((D,), jnp.float32),
                        value_sums[stream],
                        tensor_rank * width_local,
                        0,
                    ),
                    jnp.sum(grad_attend[stream], 0),
                    lax.dynamic_update_slice_in_dim(
                        jnp.zeros((FF,), jnp.float32),
                        hidden_sums[stream],
                        tensor_rank * hidden_local,
                        0,
                    ),
                    jnp.sum(grad_branch[stream], 0),
                ]
            )
        )
    weight_grads = (
        jnp.stack(grad_projection),
        jnp.stack(grad_recombine),
        jnp.stack(grad_expansion),
        jnp.stack(grad_contraction),
    )
    return (new_grads, weight_grads, jnp.stack(bias_grads), jnp.stack(shift_grads))


def on_device(
    image_tokens,
    text_tokens,
    conditioning,
    slot_sequence,
    rank_counts,
    projection,
    recombine,
    expansion,
    contraction,
    modulation,
    biases,
    cotangent_image,
    cotangent_text,
):
    tensor_rank = lax.axis_index("tensor")
    flat_rank = lax.axis_index(("dp", "tensor"))
    heads_local = HEADS // lax.axis_size("tensor")
    width_local = heads_local * HEAD_DIM
    hidden_local = FF // lax.axis_size("tensor")
    bias_all = lax.all_gather(biases, ("dp", "tensor"), axis=2, tiled=True).astype(jnp.float32)
    shard_rows = modulation.shape[2]
    silu_values = jax.nn.silu(conditioning)
    owned_rows = lax.dynamic_slice_in_dim(silu_values, flat_rank * shard_rows, shard_rows, 1)
    partial_table = jnp.einsum(
        "nd,lsdm->lsnm", owned_rows, modulation.astype(jnp.float32), precision=highest
    )
    shift_table = lax.psum(partial_table, ("dp", "tensor")) + bias_all[:, :, None, : 6 * D]
    onehot = (
        slot_sequence[:, None] == jnp.arange(conditioning.shape[0], dtype=jnp.int32)[None, :]
    ).astype(jnp.float32)
    slot_shifts = jnp.einsum("pn,lsnm->lspm", onehot, shift_table, precision=highest)
    live_slots = (jnp.arange(CAP, dtype=jnp.int32) < rank_counts[0]).astype(jnp.float32)
    image_count = image_tokens.shape[0]
    text_count = text_tokens.shape[0]
    selects = (
        slot_select(image_count, IMG, tensor_rank * image_count),
        slot_select(text_count, TXT, tensor_rank * text_count),
    )
    live_rows = [jnp.dot(selects[stream], live_slots, precision=highest) for stream in range(2)]
    states = [image_tokens.astype(jnp.float32), text_tokens.astype(jnp.float32)]
    stored = []
    for tier_index in range(LAYERS):
        gathered = (
            lax.all_gather(projection[tier_index], "dp", axis=1, tiled=True),
            lax.all_gather(recombine[tier_index], "dp", axis=1, tiled=True),
            lax.all_gather(expansion[tier_index], "dp", axis=1, tiled=True),
            lax.all_gather(contraction[tier_index], "dp", axis=1, tiled=True),
        )
        pieces = layer_biases(bias_all[tier_index], tensor_rank, width_local, hidden_local)
        row_shifts = [
            [
                spread_rows(
                    selects[stream],
                    slot_shifts[tier_index, stream, :, component * D : (component + 1) * D],
                )
                for component in range(6)
            ]
            for stream in range(2)
        ]
        record, states = forward_layer(states, gathered, pieces, row_shifts, heads_local)
        stored.append((None, row_shifts, record))
    gradients = [
        cotangent_image.astype(jnp.float32) * live_rows[0][:, None],
        cotangent_text.astype(jnp.float32) * live_rows[1][:, None],
    ]
    weight_store, bias_store, shift_store = ([], [], [])
    for tier_index in reversed(range(LAYERS)):
        kept_weights, row_shifts, record = stored[tier_index]
        layer_weights = (
            lax.all_gather(projection[tier_index], "dp", axis=1, tiled=True),
            lax.all_gather(recombine[tier_index], "dp", axis=1, tiled=True),
            lax.all_gather(expansion[tier_index], "dp", axis=1, tiled=True),
            lax.all_gather(contraction[tier_index], "dp", axis=1, tiled=True),
        )
        gradients, layer_grads, bias_part, shift_part = backward_layer(
            gradients, record, layer_weights, row_shifts, selects, heads_local, tensor_rank
        )
        reduced = (
            lax.psum_scatter(
                layer_grads[0].astype(jnp.bfloat16), "dp", scatter_dimension=1, tiled=True
            ).astype(jnp.float32),
            lax.psum_scatter(
                layer_grads[1].astype(jnp.bfloat16), "dp", scatter_dimension=1, tiled=True
            ).astype(jnp.float32),
            lax.psum_scatter(
                layer_grads[2].astype(jnp.bfloat16), "dp", scatter_dimension=1, tiled=True
            ).astype(jnp.float32),
            lax.psum_scatter(
                layer_grads[3].astype(jnp.bfloat16), "dp", scatter_dimension=1, tiled=True
            ).astype(jnp.float32),
        )
        weight_store.insert(0, reduced)
        bias_store.insert(0, bias_part)
        shift_store.insert(0, shift_part)
    stacked_grads = tuple(
        (jnp.stack([entry[kind_index] for entry in weight_store]) for kind_index in range(4))
    )
    grad_table = jnp.einsum("pn,lspm->lsnm", onehot, jnp.stack(shift_store), precision=highest)
    table_sum, bias_sum = lax.psum((grad_table, jnp.stack(bias_store)), ("dp", "tensor"))
    modulation_grad = jnp.einsum("nd,lsnm->lsdm", owned_rows, table_sum, precision=highest)
    bias_rows = biases.shape[2]
    biases_grad = lax.dynamic_slice_in_dim(bias_sum, flat_rank * bias_rows, bias_rows, 2)
    image_output = (states[0] * live_rows[0][:, None]).astype(jnp.bfloat16)
    text_output = (states[1] * live_rows[1][:, None]).astype(jnp.bfloat16)
    return (
        image_output,
        text_output,
        gradients[0],
        gradients[1],
        stacked_grads[0],
        stacked_grads[1],
        stacked_grads[2],
        stacked_grads[3],
        modulation_grad,
        biases_grad,
    )


def solution(mesh):
    in_specs = (
        P(("dp", "tensor"), None),
        P(("dp", "tensor"), None),
        P(),
        P("dp"),
        P("dp"),
        P(None, None, "dp", "tensor"),
        P(None, None, "dp", "tensor"),
        P(None, None, "dp", "tensor"),
        P(None, None, "dp", "tensor"),
        P(None, None, ("dp", "tensor"), None),
        P(None, None, ("dp", "tensor")),
        P(("dp", "tensor"), None),
        P(("dp", "tensor"), None),
    )
    out_specs = (
        P(("dp", "tensor"), None),
        P(("dp", "tensor"), None),
        P(("dp", "tensor"), None),
        P(("dp", "tensor"), None),
        P(None, None, "dp", "tensor"),
        P(None, None, "dp", "tensor"),
        P(None, None, "dp", "tensor"),
        P(None, None, "dp", "tensor"),
        P(None, None, ("dp", "tensor"), None),
        P(None, None, ("dp", "tensor")),
    )
    return jax.shard_map(
        on_device, mesh=mesh, in_specs=in_specs, out_specs=out_specs, check_vma=False
    )
```

profile of v0, /device:TPU:0, one launch (start us, length us, event | category | flops | bytes accessed | tf_op | source)
XLA Modules:
  0.0 2688.0 jit_solution(6506075270106945531)
XLA Ops:
  16.5 260.6 %all_gather.83 = bf16[2,2,21504]{1,0,2:T(2,128)(2,1)S(1)} all-gather(bf16[2,2,672]{1,0,2:T(2,128)(2,1)S(1)} %copy.119), channel_id=1, replica_groups=mesh['dp'=8,'tensor'=4] {'dp','tensor'}, dimensions={2}, use_global_device_ids=true | all-gather | bytes 177408 | tf_op jit(solution)/shard_map/all_gather | solution.py:433
  286.0 10.6 copy.120
  302.6 22.0 fusion.378
  332.0 14.3 all_gather.86
  367.8 7.0 fusion.162
  385.4 32.5 %while.52 = (s32[]{:T(128)}, bf16[6,1152,64]{1,2,0:T(8,128)(2,1)}, f32[6,1152]{1,0:T(8,128)S(1)}, bf16[6,1152,64]{2,1,0:T(8,128)(2,1)}, bf16[6,1152,64]{2,1,0:T(...) while((s32[]{:T(128)}, bf16[6,1152,64]{1,2,0:T(8,128)(2,1)}, ...), condition=%wide.region_8.9_spmd, body=%wide.region_5.8_spmd.sunk | while | flops 349100928 | bytes 17014880 | solution.py:156
  434.0 34.6 %reduce-scatter.25.cloned.1.call-done = bf16[256,1536]{1,0:T(8,128)(2,1)} async-done(((bf16[1024,1536]{1,0:T(8,128)(2,1)}), bf16[256,1536]{1,0:T(8,128)(2,1)}) %reduce-scatter.25.cloned.1.call-update) | async-done | bytes 786448 | tf_op jit(solution)/shard_map/reduce_scatter | solution.py:159
  477.1 26.8 dynamic-slice_reduce_fusion.4
  507.7 53.8 %all-gather.45.cloned.1.call-done = bf16[1,2,1536,1536]{3,2,1,0:T(8,128)(2,1)} async-done(((bf16[1,2,192,1536]{3,2,1,0:T(8,128)(2,1)}), bf16[1,2,1536,1536]{3,2,1,0:T(8,128)(2,1)}) %all-gather.45.cloned.1.call-update) | async-done | bytes 9437200 | tf_op jit(solution)/shard_map/all_gather | solution.py:459
  561.5 44.9 %all-gather.27.cloned.1.call-done = bf16[1024,1536]{1,0:T(8,128)(2,1)} async-done(((bf16[256,1536]{1,0:T(8,128)(2,1)}), bf16[1024,1536]{1,0:T(8,128)(2,1)}) %all-gather.27.cloned.1.call-update) | async-done | bytes 3145744 | tf_op jit(solution)/shard_map/all_gather | solution.py:183
  606.4 9.7 fusion.131
  616.1 83.0 %all-gather.47.cloned.1.call-done = bf16[1,2,1536,1536]{3,2,1,0:T(8,128)(2,1)} async-done(((bf16[1,2,192,1536]{3,2,1,0:T(8,128)(2,1)}), bf16[1,2,1536,1536]{3,2,1,0:T(8,128)(2,1)}) %all-gather.47.cloned.1.call-update) | async-done | bytes 9437200 | tf_op jit(solution)/shard_map/all_gather | solution.py:460
  699.1 10.3 fusion.148
  710.9 14.6 reduce-scatter.29.cloned.1.call-done
  729.3 11.7 all_gather.93
  749.8 24.3 reduce-scatter.27.cloned.1.call-done
  785.8 61.0 %all-gather.49.cloned.1.call-done = bf16[1,2,1536,1152]{3,2,1,0:T(8,128)(2,1)} async-done(((bf16[1,2,192,1152]{3,2,1,0:T(8,128)(2,1)}), bf16[1,2,1536,1152]{3,2,1,0:T(8,128)(2,1)}) %all-gather.49.cloned.1.call-update) | async-done | bytes 7077904 | tf_op jit(solution)/shard_map/all_gather | solution.py:457
  865.1 7.7 reduce-scatter.31.cloned.1.call-done
  875.6 10.0 all_gather.94
  890.3 28.9 %all-gather.29.cloned.1.call-done = bf16[1024,1536]{1,0:T(8,128)(2,1)} async-done(((bf16[256,1536]{1,0:T(8,128)(2,1)}), bf16[1024,1536]{1,0:T(8,128)(2,1)}) %all-gather.29.cloned.1.call-update) | async-done | bytes 3145744 | tf_op jit(solution)/shard_map/all_gather | solution.py:134
  934.5 29.3 %while.53 = (s32[]{:T(128)}, bf16[6,1152,64]{1,2,0:T(8,128)(2,1)S(1)}, f32[6,1152]{1,0:T(8,128)S(1)}, bf16[6,1152,64]{2,1,0:T(8,128)(2,1)}, bf16[6,1152,64]{2,1,...) while((s32[]{:T(128)}, bf16[6,1152,64]{1,2,0:T(8,128)(2,1)S(1)}, ...), condition=%wide.region_24.25_spmd, body=%wide.region_21.24_spmd.sunk | while | flops 349100928 | bytes 17022048 | solution.py:156
  973.8 39.2 %reduce-scatter.33.cloned.1.call-done = bf16[256,1536]{1,0:T(8,128)(2,1)} async-done(((bf16[1024,1536]{1,0:T(8,128)(2,1)}), bf16[256,1536]{1,0:T(8,128)(2,1)}) %reduce-scatter.33.cloned.1.call-update) | async-done | bytes 786448 | tf_op jit(solution)/shard_map/reduce_scatter | solution.py:159
  1019.1 27.4 %dynamic-slice_reduce_fusion.2 = (f32[1536]{0:T(1024)}, f32[1536]{0:T(1024)S(1)}) fusion(f32[1,2,21504]{1,0,2:T(1,128)} %get-tuple-element.458, s32[]{:T(128)S(6)} %add.935, s32[]{:T(128)S(6)} %select_n.103), kind=kLoop, calls=%fused_computation.407 | loop fusion | bytes 24584 | tf_op jit(solution)/shard_map/slice | solution.py:188
  1048.1 57.2 %all-gather.53.cloned.1.call-done = bf16[1,2,1536,1536]{3,2,1,0:T(8,128)(2,1)} async-done(((bf16[1,2,192,1536]{3,2,1,0:T(8,128)(2,1)}), bf16[1,2,1536,1536]{3,2,1,0:T(8,128)(2,1)}) %all-gather.53.cloned.1.call-update) | async-done | bytes 9437200 | tf_op jit(solution)/shard_map/all_gather | solution.py:459
  1105.3 44.9 %all-gather.31.cloned.1.call-done = bf16[1024,1536]{1,0:T(8,128)(2,1)} async-done(((bf16[256,1536]{1,0:T(8,128)(2,1)}), bf16[1024,1536]{1,0:T(8,128)(2,1)}) %all-gather.31.cloned.1.call-update) | async-done | bytes 3145744 | tf_op jit(solution)/shard_map/all_gather | solution.py:183
  1150.2 9.7 fusion.139
  1159.9 83.2 %all-gather.55.cloned.1.call-done = bf16[1,2,1536,1536]{3,2,1,0:T(8,128)(2,1)} async-done(((bf16[1,2,192,1536]{3,2,1,0:T(8,128)(2,1)}), bf16[1,2,1536,1536]{3,2,1,0:T(8,128)(2,1)}) %all-gather.55.cloned.1.call-update) | async-done | bytes 9437200 | tf_op jit(solution)/shard_map/all_gather | solution.py:460
  1243.1 44.9 %all-gather.33.cloned.1.call-done = bf16[1024,1536]{1,0:T(8,128)(2,1)} async-done(((bf16[256,1536]{1,0:T(8,128)(2,1)}), bf16[1024,1536]{1,0:T(8,128)(2,1)}) %all-gather.33.cloned.1.call-update) | async-done | bytes 3145744 | tf_op jit(solution)/shard_map/all_gather | solution.py:245
  1287.9 12.7 convert_reduce_fusion
  1307.2 10.3 fusion.146
  1318.4 10.0 all_gather.102
  1330.0 12.5 all_gather.99
  1368.0 45.9 %reduce-scatter.35.cloned.1.call-done = bf16[256,1536]{1,0:T(8,128)(2,1)} async-done(((bf16[1024,1536]{1,0:T(8,128)(2,1)}), bf16[256,1536]{1,0:T(8,128)(2,1)}) %reduce-scatter.35.cloned.1.call-update) | async-done | bytes 786448 | tf_op jit(solution)/shard_map/reduce_scatter | solution.py:201
  1418.7 22.4 reduce-scatter.43.cloned.1.call-done
  1442.3 26.2 reduce-scatter.39.cloned.1.call-done
  1470.5 9.8 all_gather.103
  1482.4 32.5 %all-gather.35.cloned.1.call-done = bf16[1024,1536]{1,0:T(8,128)(2,1)} async-done(((bf16[256,1536]{1,0:T(8,128)(2,1)}), bf16[1024,1536]{1,0:T(8,128)(2,1)}) %all-gather.35.cloned.1.call-update) | async-done | bytes 3145744 | tf_op jit(solution)/shard_map/all_gather | solution.py:300
  1525.1 80.0 %while.54 = (s32[]{:T(128)}, bf16[6,1152,64]{1,2,0:T(8,128)(2,1)}, bf16[6,1152,64]{1,2,0:T(8,128)(2,1)}, bf16[6,1152,64]{1,2,0:T(8,128)(2,1)}, bf16[6,1152,64]{2...) while((s32[]{:T(128)}, bf16[6,1152,64]{1,2,0:T(8,128)(2,1)}, ...), condition=%wide.region_41.42_spmd, body=%wide.region_39.41_spmd.sunk | while | flops 860330880 | bytes 49426088 | solution.py:315
  1609.4 7.7 convolution_convert_fusion.15
  1617.2 43.9 %reduce-scatter.45.cloned.1.call-done = bf16[256,1536]{1,0:T(8,128)(2,1)} async-done(((bf16[1024,1536]{1,0:T(8,128)(2,1)}), bf16[256,1536]{1,0:T(8,128)(2,1)}) %reduce-scatter.45.cloned.1.call-update) | async-done | bytes 786448 | tf_op jit(solution)/shard_map/reduce_scatter | solution.py:351
  1673.6 36.7 %all-gather.37.cloned.1.call-done = bf16[1024,1536]{1,0:T(8,128)(2,1)} async-done(((bf16[256,1536]{1,0:T(8,128)(2,1)}), bf16[1024,1536]{1,0:T(8,128)(2,1)}) %all-gather.37.cloned.1.call-update) | async-done | bytes 3145744 | tf_op jit(solution)/shard_map/all_gather | solution.py:245
  1710.3 12.6 convert_reduce_fusion.1
  1724.5 8.8 fusion.149
  1740.8 9.8 all_gather.106
  1760.2 25.7 reduce-scatter.47.cloned.1.call-done
  1791.3 22.5 reduce-scatter.51.cloned.1.call-done
  1817.0 10.8 all_gather.107
  1829.9 30.3 %all-gather.39.cloned.1.call-done = bf16[1024,1536]{1,0:T(8,128)(2,1)} async-done(((bf16[256,1536]{1,0:T(8,128)(2,1)}), bf16[1024,1536]{1,0:T(8,128)(2,1)}) %all-gather.39.cloned.1.call-update) | async-done | bytes 3145744 | tf_op jit(solution)/shard_map/all_gather | solution.py:300
  1870.2 80.0 %while.55 = (s32[]{:T(128)}, bf16[6,1152,64]{1,2,0:T(8,128)(2,1)}, bf16[6,1152,64]{1,2,0:T(8,128)(2,1)}, bf16[6,1152,64]{1,2,0:T(8,128)(2,1)}, bf16[6,1152,64]{2...) while((s32[]{:T(128)}, bf16[6,1152,64]{1,2,0:T(8,128)(2,1)}, ...), condition=%wide.region_56.57_spmd, body=%wide.region_54.56_spmd.sunk | while | flops 860330880 | bytes 49426088 | solution.py:315
  1962.3 7.7 convolution_convert_fusion.14
  1980.8 9.3 fusion.111
  2058.9 8.4 pad_maximum_fusion.1
  2072.0 8.6 fusion.110
  2080.6 8.2 pad_maximum_fusion
  2093.8 10.1 fusion.113
  2103.9 8.3 pad_maximum_fusion.3
  2117.1 11.0 fusion.112
  2128.1 8.4 pad_maximum_fusion.2
  2170.9 141.9 %all-reduce.6.cloned.1.call-done = (f32[2,2,6,9216]{3,2,1,0:T(8,128)}, f32[2,2,21504]{2,1,0:T(2,128)}) async-done(((f32[2,2,6,9216]{3,2,1,0:T(8,128)}, f32[2,2,21504]{2,1,0:T(2,128)}), (f32[2,2,6,9216]{3,2,1,0:T(8,128)}, f32[2,2,21504]{2,1,0:T(2,128)})) %all-reduce.6.cloned.1.call-update) | async-done | bytes 1228816 | tf_op jit(solution)/shard_map/psum | solution.py:512
  2314.2 9.4 convolution_bitcast_fusion
  2327.8 93.1 %reduce-scatter.71.cloned.1.call-done = bf16[2,192,1536]{2,1,0:T(8,128)(2,1)} async-done(((bf16[2,1536,1536]{2,1,0:T(8,128)(2,1)}), bf16[2,192,1536]{2,1,0:T(8,128)(2,1)}) %reduce-scatter.71.cloned.1.call-update) | async-done | bytes 1179664 | tf_op jit(solution)/shard_map/reduce_scatter | solution.py:501
  2420.8 100.1 %reduce-scatter.69.cloned.1.call-done = bf16[2,192,1536]{2,1,0:T(8,128)(2,1)} async-done(((bf16[2,1536,1536]{2,1,0:T(8,128)(2,1)}), bf16[2,192,1536]{2,1,0:T(8,128)(2,1)}) %reduce-scatter.69.cloned.1.call-update) | async-done | bytes 1179664 | tf_op jit(solution)/shard_map/reduce_scatter | solution.py:501
  2525.0 73.8 %reduce-scatter.59.cloned.1.call-done = bf16[2,192,1152]{2,1,0:T(8,128)(2,1)} async-done(((bf16[2,1536,1152]{2,1,0:T(8,128)(2,1)}), bf16[2,192,1152]{2,1,0:T(8,128)(2,1)}) %reduce-scatter.59.cloned.1.call-update) | async-done | bytes 884752 | tf_op jit(solution)/shard_map/reduce_scatter | solution.py:492
  2598.9 77.8 %reduce-scatter.57.cloned.1.call-done = bf16[2,192,1152]{2,1,0:T(8,128)(2,1)} async-done(((bf16[2,1536,1152]{2,1,0:T(8,128)(2,1)}), bf16[2,192,1152]{2,1,0:T(8,128)(2,1)}) %reduce-scatter.57.cloned.1.call-update) | async-done | bytes 884752 | tf_op jit(solution)/shard_map/reduce_scatter | solution.py:492
  (1224 shorter events, 656.5 us)
Async XLA Ops:
  8.0 290.0 %all-reduce.4.cloned.1.call-start = ((), (), s32[]{:S(2)}) async-start(), calls=%async_computation.24 | async-start | bytes 2359296 | tf_op jit(solution)/shard_map/psum | solution.py:440
  13.3 333.0 %all-gather.41.cloned.1.call-start = ((), (), s32[]{:S(2)}) async-start(), calls=%async_computation.57 | async-start | bytes 7962624 | tf_op jit(solution)/shard_map/all_gather | solution.py:457
  16.2 351.6 %all-gather.25.cloned.1.call-start = ((), (), s32[]{:S(2)}) async-start(), calls=%async_computation.25 | async-start | bytes 3932160 | tf_op jit(solution)/shard_map/all_gather | solution.py:134
  297.4 480.3 %copy-start.119 = (f32[256]{0:T(256)}, f32[256]{0:T(256)S(1)}, u32[]{:S(2)}) copy-start(f32[256]{0:T(256)S(1)} %fusion.346) | copy-start | bytes 3076
  300.2 473.9 %copy-start.107 = (f32[1536]{0:T(1024)}, f32[1536]{0:T(1024)S(1)}, u32[]{:S(2)}) copy-start(f32[1536]{0:T(1024)S(1)} %get-tuple-element.345) | copy-start | bytes 18436
  301.6 119.0 %all-gather.43.cloned.1.call-start = ((), (), s32[]{:S(2)}) async-start(), calls=%async_computation.58 | async-start | bytes 2654208 | tf_op jit(solution)/shard_map/all_gather | solution.py:458
  302.6 166.0 %reduce-scatter.25.cloned.1.call-start = ((), (), s32[]{:S(2)}) async-start(), calls=%async_computation.26 | async-start | bytes 3932160 | tf_op jit(solution)/shard_map/reduce_scatter | solution.py:159
  324.7 403.5 %copy-start.137 = (f32[32]{0:T(128)}, f32[32]{0:T(128)S(1)}, u32[]{:S(2)}) copy-start(f32[32]{0:T(128)S(1)} %fusion.359) | copy-start | bytes 388
  425.7 135.8 %all-gather.45.cloned.1.call-start = ((), (), s32[]{:S(2)}) async-start(), calls=%async_computation.59 | async-start | bytes 10616832 | tf_op jit(solution)/shard_map/all_gather | solution.py:459
  428.9 177.5 %all-gather.27.cloned.1.call-start = ((), (), s32[]{:S(2)}) async-start(), calls=%async_computation.27 | async-start | bytes 3932160 | tf_op jit(solution)/shard_map/all_gather | solution.py:183
  433.1 340.9 %copy-start.113 = (f32[1536]{0:T(1024)}, f32[1536]{0:T(1024)S(1)}, u32[]{:S(2)}) copy-start(f32[1536]{0:T(1024)S(1)} %get-tuple-element.317) | copy-start | bytes 18436
  433.2 439.6 %copy-start.116 = (f32[1536]{0:T(1024)}, f32[1536]{0:T(1024)S(1)}, u32[]{:S(2)}) copy-start(f32[1536]{0:T(1024)S(1)} %get-tuple-element.315) | copy-start | bytes 18436
  434.0 294.2 %copy-start.176 = (f32[1536]{0:T(1024)}, f32[1536]{0:T(1024)S(1)}, u32[]{:S(2)}) copy-start(f32[1536]{0:T(1024)S(1)} %get-tuple-element.336) | copy-start | bytes 18436
  434.0 340.0 %copy-start.153 = (f32[1536]{0:T(1024)}, f32[1536]{0:T(1024)S(1)}, u32[]{:S(2)}) copy-start(f32[1536]{0:T(1024)S(1)} %get-tuple-element.332) | copy-start | bytes 18436
  434.0 340.0 %copy-start.159 = (f32[1536]{0:T(1024)}, f32[1536]{0:T(1024)S(1)}, u32[]{:S(2)}) copy-start(f32[1536]{0:T(1024)S(1)} %get-tuple-element.344) | copy-start | bytes 18436
  434.0 438.8 %copy-start.109 = (f32[1536]{0:T(1024)}, f32[1536]{0:T(1024)S(1)}, u32[]{:S(2)}) copy-start(f32[1536]{0:T(1024)S(1)} %get-tuple-element.338) | copy-start | bytes 18436
  473.8 225.3 %all-gather.47.cloned.1.call-start = ((), (), s32[]{:S(2)}) async-start(), calls=%async_computation.60 | async-start | bytes 10616832 | tf_op jit(solution)/shard_map/all_gather | solution.py:460
  477.1 248.4 %reduce-scatter.29.cloned.1.call-start = ((), (), s32[]{:S(2)}) async-start(), calls=%async_computation.30 | async-start | bytes 491520 | tf_op jit(solution)/shard_map/reduce_scatter | solution.py:167
  503.9 195.2 %copy-start.265 = (f32[1536]{0:T(1024)}, f32[1536]{0:T(1024)S(1)}, u32[]{:S(2)}) copy-start(f32[1536]{0:T(1024)S(1)} %get-tuple-element.319) | copy-start | bytes 18436
  504.9 111.2 %copy-start.95 = (bf16[1,128,6,64]{1,3,2,0:T(8,128)(2,1)}, bf16[1,128,6,64]{1,3,2,0:T(8,128)(2,1)S(1)}, u32[]{:S(2)}) copy-start(bf16[1,128,6,64]{1,3,2,0:T(8,128)(2,1)S(1)} %slice.495) | copy-start | bytes 294916
  507.5 266.6 %reduce-scatter.27.cloned.1.call-start = ((), (), s32[]{:S(2)}) async-start(), calls=%async_computation.28 | async-start | bytes 3932160 | tf_op jit(solution)/shard_map/reduce_scatter | solution.py:201
  709.4 137.4 %all-gather.49.cloned.1.call-start = ((), (), s32[]{:S(2)}) async-start(), calls=%async_computation.61 | async-start | bytes 7962624 | tf_op jit(solution)/shard_map/all_gather | solution.py:457
  710.2 162.6 %reduce-scatter.31.cloned.1.call-start = ((), (), s32[]{:S(2)}) async-start(), calls=%async_computation.31 | async-start | bytes 491520 | tf_op jit(solution)/shard_map/reduce_scatter | solution.py:204
  749.7 169.5 %all-gather.29.cloned.1.call-start = ((), (), s32[]{:S(2)}) async-start(), calls=%async_computation.29 | async-start | bytes 3932160 | tf_op jit(solution)/shard_map/all_gather | solution.py:134
  777.3 235.7 %copy-start.5 = (f32[256,1536]{1,0:T(8,128)}, f32[256,1536]{1,0:T(8,128)S(1)}, u32[]{:S(2)}) copy-start(f32[256,1536]{1,0:T(8,128)S(1)} %get-tuple-element.447) | copy-start | bytes 4718596
  777.6 75.8 %copy-start.256 = (f32[256]{0:T(256)}, f32[256]{0:T(256)S(1)}, u32[]{:S(2)}) copy-start(f32[256]{0:T(256)S(1)} %multiply_reduce_fusion.6) | copy-start | bytes 3076
  777.6 75.8 %copy-start.237 = (f32[256]{0:T(256)}, f32[256]{0:T(256)S(1)}, u32[]{:S(2)}) copy-start(f32[256]{0:T(256)S(1)} %fusion.334) | copy-start | bytes 3076
  779.0 184.9 %all-gather.51.cloned.1.call-start = ((), (), s32[]{:S(2)}) async-start(), calls=%async_computation.62 | async-start | bytes 2654208 | tf_op jit(solution)/shard_map/all_gather | solution.py:458
  779.6 233.3 %reduce-scatter.33.cloned.1.call-start = ((), (), s32[]{:S(2)}) async-start(), calls=%async_computation.32 | async-start | bytes 3932160 | tf_op jit(solution)/shard_map/reduce_scatter | solution.py:159
  779.7 93.1 %copy-start.232 = (f32[32]{0:T(128)}, f32[32]{0:T(128)S(1)}, u32[]{:S(2)}) copy-start(f32[32]{0:T(128)S(1)} %broadcast_select_fusion.1) | copy-start | bytes 388
  874.6 864.9 %copy-start.38 = (f32[32,1536]{1,0:T(8,128)}, f32[32,1536]{1,0:T(8,128)S(1)}, u32[]{:S(2)}) copy-start(f32[32,1536]{1,0:T(8,128)S(1)} %get-tuple-element.449) | copy-start | bytes 589828
  969.0 136.3 %all-gather.53.cloned.1.call-start = ((), (), s32[]{:S(2)}) async-start(), calls=%async_computation.63 | async-start | bytes 10616832 | tf_op jit(solution)/shard_map/all_gather | solution.py:459
  969.8 180.4 %all-gather.31.cloned.1.call-start = ((), (), s32[]{:S(2)}) async-start(), calls=%async_computation.33 | async-start | bytes 3932160 | tf_op jit(solution)/shard_map/all_gather | solution.py:183
  1014.6 399.3 %copy-start.202 = (f32[256]{0:T(256)}, f32[256]{0:T(256)S(1)}, u32[]{:S(2)}) copy-start(f32[256]{0:T(256)S(1)} %broadcast_multiply_fusion) | copy-start | bytes 3076
  1017.2 225.9 %all-gather.55.cloned.1.call-start = ((), (), s32[]{:S(2)}) async-start(), calls=%async_computation.64 | async-start | bytes 10616832 | tf_op jit(solution)/shard_map/all_gather | solution.py:460
  1017.9 270.0 %all-gather.33.cloned.1.call-start = ((), (), s32[]{:S(2)}) async-start(), calls=%async_computation.37 | async-start | bytes 3932160 | tf_op jit(solution)/shard_map/all_gather | solution.py:245
  1018.7 309.7 %reduce-scatter.37.cloned.1.call-start = ((), (), s32[]{:S(2)}) async-start(), calls=%async_computation.35 | async-start | bytes 491520 | tf_op jit(solution)/shard_map/reduce_scatter | solution.py:167
  1046.5 260.6 %copy-start.268 = (f32[1536]{0:T(1024)}, f32[1536]{0:T(1024)S(1)}, u32[]{:S(2)}) copy-start(f32[1536]{0:T(1024)S(1)} %get-tuple-element.309) | copy-start | bytes 18436
  1046.6 113.4 %copy-start.96 = (bf16[1,128,6,64]{1,3,2,0:T(8,128)(2,1)}, bf16[1,128,6,64]{1,3,2,0:T(8,128)(2,1)S(1)}, u32[]{:S(2)}) copy-start(bf16[1,128,6,64]{1,3,2,0:T(8,128)(2,1)S(1)} %slice.522) | copy-start | bytes 294916
  1047.9 318.5 %reduce-scatter.41.cloned.1.call-start = ((), (), s32[]{:S(2)}) async-start(), calls=%async_computation.38 | async-start | bytes 3932160 | tf_op jit(solution)/shard_map/reduce_scatter | solution.py:278
  1307.1 106.8 %reduce-scatter.35.cloned.1.call-start = ((), (), s32[]{:S(2)}) async-start(), calls=%async_computation.34 | async-start | bytes 3932160 | tf_op jit(solution)/shard_map/reduce_scatter | solution.py:201
  1317.5 123.6 %reduce-scatter.43.cloned.1.call-start = ((), (), s32[]{:S(2)}) async-start(), calls=%async_computation.40 | async-start | bytes 491520 | tf_op jit(solution)/shard_map/reduce_scatter | solution.py:281
  1329.6 138.8 %copy-start.249 = (f32[32]{0:T(128)}, f32[32]{0:T(128)S(1)}, u32[]{:S(2)}) copy-start(f32[32]{0:T(128)S(1)} %broadcast_multiply_fusion.4) | copy-start | bytes 388
  1329.8 138.6 %copy-start.289 = (f32[32]{0:T(128)}, f32[32]{0:T(128)S(1)}, u32[]{:S(2)}) copy-start(f32[32]{0:T(128)S(1)} %fusion.343) | copy-start | bytes 388
  1353.6 114.8 %reduce-scatter.39.cloned.1.call-start = ((), (), s32[]{:S(2)}) async-start(), calls=%async_computation.36 | async-start | bytes 491520 | tf_op jit(solution)/shard_map/reduce_scatter | solution.py:204
  1359.4 155.5 %all-gather.35.cloned.1.call-start = ((), (), s32[]{:S(2)}) async-start(), calls=%async_computation.39 | async-start | bytes 3932160 | tf_op jit(solution)/shard_map/all_gather | solution.py:300
  1417.3 246.2 %copy-start.229 = (f32[256]{0:T(256)}, f32[256]{0:T(256)S(1)}, u32[]{:S(2)}) copy-start(f32[256]{0:T(256)S(1)} %negate_multiply_fusion.3) | copy-start | bytes 3076
  1418.7 242.3 %reduce-scatter.45.cloned.1.call-start = ((), (), s32[]{:S(2)}) async-start(), calls=%async_computation.41 | async-start | bytes 3932160 | tf_op jit(solution)/shard_map/reduce_scatter | solution.py:351
  1617.1 93.2 %all-gather.37.cloned.1.call-start = ((), (), s32[]{:S(2)}) async-start(), calls=%async_computation.42 | async-start | bytes 3932160 | tf_op jit(solution)/shard_map/all_gather | solution.py:245
  1666.4 72.0 %reduce-scatter.49.cloned.1.call-start = ((), (), s32[]{:S(2)}) async-start(), calls=%async_computation.45 | async-start | bytes 491520 | tf_op jit(solution)/shard_map/reduce_scatter | solution.py:354
  1673.5 112.4 %reduce-scatter.47.cloned.1.call-start = ((), (), s32[]{:S(2)}) async-start(), calls=%async_computation.43 | async-start | bytes 3932160 | tf_op jit(solution)/shard_map/reduce_scatter | solution.py:278
  1733.4 80.4 %reduce-scatter.51.cloned.1.call-start = ((), (), s32[]{:S(2)}) async-start(), calls=%async_computation.46 | async-start | bytes 491520 | tf_op jit(solution)/shard_map/reduce_scatter | solution.py:281
  1760.1 100.1 %all-gather.39.cloned.1.call-start = ((), (), s32[]{:S(2)}) async-start(), calls=%async_computation.44 | async-start | bytes 3932160 | tf_op jit(solution)/shard_map/all_gather | solution.py:300
  1791.2 241.7 %reduce-scatter.55.cloned.1.call-start = ((), (), s32[]{:S(2)}) async-start(), calls=%async_computation.48 | async-start | bytes 491520 | tf_op jit(solution)/shard_map/reduce_scatter | solution.py:354
  1960.5 83.1 %reduce-scatter.53.cloned.1.call-start = ((), (), s32[]{:S(2)}) async-start(), calls=%async_computation.47 | async-start | bytes 3932160 | tf_op jit(solution)/shard_map/reduce_scatter | solution.py:351
  1970.0 195.5 %reduce-scatter.63.cloned.1.call-start = ((), (), s32[]{:S(2)}) async-start(), calls=%async_computation.52 | async-start | bytes 2654208 | tf_op jit(solution)/shard_map/reduce_scatter | solution.py:495
  1999.5 166.0 %reduce-scatter.61.cloned.1.call-start = ((), (), s32[]{:S(2)}) async-start(), calls=%async_computation.51 | async-start | bytes 2654208 | tf_op jit(solution)/shard_map/reduce_scatter | solution.py:495
  2030.4 282.5 %all-reduce.6.cloned.1.call-start = ((), (), s32[]{:S(2)}) async-start(), calls=%async_computation.65 | async-start | bytes 3047424 | tf_op jit(solution)/shard_map/psum | solution.py:512
  2058.8 264.8 %reduce-scatter.67.cloned.1.call-start = ((), (), s32[]{:S(2)}) async-start(), calls=%async_computation.54 | async-start | bytes 10616832 | tf_op jit(solution)/shard_map/reduce_scatter | solution.py:498
  2067.3 256.3 %reduce-scatter.65.cloned.1.call-start = ((), (), s32[]{:S(2)}) async-start(), calls=%async_computation.53 | async-start | bytes 10616832 | tf_op jit(solution)/shard_map/reduce_scatter | solution.py:498
  2088.9 331.9 %reduce-scatter.71.cloned.1.call-start = ((), (), s32[]{:S(2)}) async-start(), calls=%async_computation.56 | async-start | bytes 10616832 | tf_op jit(solution)/shard_map/reduce_scatter | solution.py:501
  2112.3 408.6 %reduce-scatter.69.cloned.1.call-start = ((), (), s32[]{:S(2)}) async-start(), calls=%async_computation.55 | async-start | bytes 10616832 | tf_op jit(solution)/shard_map/reduce_scatter | solution.py:501
  2136.5 462.3 %reduce-scatter.59.cloned.1.call-start = ((), (), s32[]{:S(2)}) async-start(), calls=%async_computation.50 | async-start | bytes 7962624 | tf_op jit(solution)/shard_map/reduce_scatter | solution.py:492
  2149.3 527.4 %reduce-scatter.57.cloned.1.call-start = ((), (), s32[]{:S(2)}) async-start(), calls=%async_computation.49 | async-start | bytes 7962624 | tf_op jit(solution)/shard_map/reduce_scatter | solution.py:492
  (306 other events, 3053.6 us)
Sparse Core Ops, SparseCore 0:
  14.8 209.1 all-reduce.3
  2059.0 253.8 all-reduce.5
Sparse Core Ops, SparseCore 1:
  16.3 86.0 all-gather.40
  301.7 47.1 all-gather.24
  351.0 31.3 all-gather.42
  425.8 42.8 reduce-scatter.24
  470.9 90.5 all-gather.44
  564.1 42.2 all-gather.26
  608.5 90.5 all-gather.46
  702.6 22.8 reduce-scatter.28
  729.2 44.8 reduce-scatter.26
  775.8 71.0 all-gather.48
  849.7 23.0 reduce-scatter.30
  875.4 43.8 all-gather.28
  920.8 31.3 all-gather.50
  969.1 43.8 reduce-scatter.32
  1014.7 90.5 all-gather.52
  1107.9 42.2 all-gather.30
  1152.5 90.5 all-gather.54
  1245.7 42.2 all-gather.32
  1290.8 24.4 reduce-scatter.36
  1319.1 47.2 reduce-scatter.40
  1370.1 43.8 reduce-scatter.34
  1416.8 24.3 reduce-scatter.42
  1444.0 24.3 reduce-scatter.38
  1471.0 43.8 all-gather.34
  1617.2 43.8 reduce-scatter.44
  1666.4 43.8 all-gather.36
  1713.9 24.4 reduce-scatter.48
  1742.0 43.8 reduce-scatter.46
  1789.4 24.3 reduce-scatter.50
  1816.4 43.8 all-gather.38
  1960.6 24.4 reduce-scatter.54
  1988.7 43.8 reduce-scatter.52
  2035.0 36.7 reduce-scatter.62
  2074.1 36.6 reduce-scatter.60
  2113.1 100.0 reduce-scatter.66
  2215.5 105.3 reduce-scatter.64
  2323.3 97.4 reduce-scatter.70
  2423.1 97.8 reduce-scatter.68
  2523.4 75.5 reduce-scatter.58
  2601.2 75.5 reduce-scatter.56
where the time goes:
time: 2700 us; the launch traced here: 2690 us
  waiting for transfers between devices  1410 us (52%)
  matrix products  493 us (18%)
  blocking collectives  350 us (13%)
  local copies, waits for them, and re-layouts  255 us (9%)
  other arithmetic  152 us (6%)
    all_gather x1, blocking collectives, on_device(): lax.all_gather(biases, ('dp', 'tensor'), axis=2, tiled=True)  261 us
    reduce_scatter x2, waiting for transfers between devices, on_device(): lax.psum_scatter(layer_grads[3].astype(jnp.bfloat16), 'dp', scatter_dimen...  193 us
    all_gather x2, waiting for transfers between devices, on_device(): lax.all_gather(contraction[tier_index], 'dp', axis=1, tiled=True)  166 us
    reduce_scatter x2, waiting for transfers between devices, on_device(): lax.psum_scatter(layer_grads[0].astype(jnp.bfloat16), 'dp', scatter_dimen...  152 us
    psum x1, waiting for transfers between devices, on_device(): lax.psum((grad_table, jnp.stack(bias_store)), ('dp', 'tensor'))  142 us
    all_gather x2, waiting for transfers between devices, on_device(): lax.all_gather(expansion[tier_index], 'dp', axis=1, tiled=True)  111 us
    all_gather x2, waiting for transfers between devices, forward_layer(): lax.all_gather(normed_feed[0], 'tensor', axis=0, tiled=True)  89.7 us
    all_gather x2, waiting for transfers between devices, backward_layer(): lax.all_gather(grad_branch[0].astype(jnp.bfloat16), 'tensor', axis=0, til...  81.6 us
  transfers between devices with their start and end apart: 42, of which 30 were waited for; matrix products, arithmetic and copies ran while one was open for 24% of the time, Pallas kernels for 0%

commit v1 on v0

v1 whole, which is shorter than its diff:
```python
import functools
import math

import jax
import jax.numpy as jnp
from jax import lax
from jax.experimental import pallas as pl
from jax.experimental.pallas import tpu as pltpu
from jax.sharding import PartitionSpec as P

D = 1536
HEADS = 24
HEAD_DIM = 64
FF = 6144
LAYERS = 2

highest = lax.Precision.HIGHEST
contract_columns = (((1,), (1,)), ((), ()))
contract_rows = (((0,), (0,)), ((), ()))
SCALE = HEAD_DIM ** (-0.5)
EXPONENT = SCALE * math.log2(math.e)


def normalize(values):
    average = jnp.mean(values, -1, keepdims=True)
    centred = values - average
    spread = jnp.mean(centred * centred, -1, keepdims=True)
    return centred * lax.rsqrt(spread + 1e-06)


def modulate(values, shifts, scales):
    return normalize(values) * (1.0 + scales) + shifts


def gelu_tanh(values):
    return jax.nn.gelu(values, approximate=True)


def exchange(values, axis, step):
    size = lax.axis_size(axis)
    return lax.ppermute(values, axis, [(rank, rank ^ step) for rank in range(size)])


def gather_parts(values, axis):
    return [values] + [exchange(values, axis, step) for step in range(1, lax.axis_size(axis))]


def gather_rows(values, axis):
    return jnp.concatenate(gather_parts(values, axis), axis=0)


def scatter_rows(values, axis):
    size = lax.axis_size(axis)
    rows = values.shape[0] // size
    total = values[:rows].astype(jnp.float32)
    for step in range(1, size):
        total = total + exchange(values[step * rows : (step + 1) * rows], axis, step).astype(
            jnp.float32
        )
    return total


def sum_over(values, axis):
    total = values
    for step in range(1, lax.axis_size(axis)):
        total = total + exchange(values, axis, step)
    return total


def row_block(rows):
    for block in (384, 256, 128):
        if rows % block == 0:
            return block
    return rows


def attend_kernel(heads, block, columns_ref, out_ref, log_ref):
    rows = columns_ref.shape[0]
    for head in range(heads):
        base = head * 3 * HEAD_DIM
        keys = columns_ref[:, base + HEAD_DIM : base + 2 * HEAD_DIM]
        values = columns_ref[:, base + 2 * HEAD_DIM : base + 3 * HEAD_DIM]

        def step(index, carry):
            place = pl.ds(pl.multiple_of(index * block, block), block)
            queries = columns_ref[place, base : base + HEAD_DIM]
            scores = lax.dot_general(
                queries, keys, contract_columns, preferred_element_type=jnp.float32
            )
            row_max = jnp.max(scores, -1, keepdims=True)
            weights = jnp.exp2((scores - row_max) * EXPONENT)
            totals = jnp.sum(weights, -1, keepdims=True)
            output = jnp.dot(
                weights.astype(jnp.bfloat16), values, preferred_element_type=jnp.float32
            )
            out_ref[place, head * HEAD_DIM : (head + 1) * HEAD_DIM] = (output / totals).astype(
                jnp.bfloat16
            )
            log_ref[place, head : head + 1] = row_max * EXPONENT + jnp.log2(totals)
            return carry

        lax.fori_loop(0, rows // block, step, 0)


def attend(columns, heads):
    rows = columns.shape[0]
    return pl.pallas_call(
        functools.partial(attend_kernel, heads, row_block(rows)),
        out_shape=(
            jax.ShapeDtypeStruct((rows, heads * HEAD_DIM), jnp.bfloat16),
            jax.ShapeDtypeStruct((rows, 128), jnp.float32),
        ),
        cost_estimate=pl.CostEstimate(
            flops=heads * rows * rows * HEAD_DIM * 4,
            bytes_accessed=columns.size * 3,
            transcendentals=heads * rows * rows,
        ),
        name="attend",
    )(columns)


def attend_back_kernel(
    heads, block, columns_ref, out_ref, log_ref, grad_ref, result_ref, key_acc, value_acc
):
    rows = columns_ref.shape[0]
    for head in range(heads):
        base = head * 3 * HEAD_DIM
        part = slice(head * HEAD_DIM, (head + 1) * HEAD_DIM)
        keys = columns_ref[:, base + HEAD_DIM : base + 2 * HEAD_DIM]
        values = columns_ref[:, base + 2 * HEAD_DIM : base + 3 * HEAD_DIM]
        key_acc[...] = jnp.zeros_like(key_acc)
        value_acc[...] = jnp.zeros_like(value_acc)

        def step(index, carry):
            place = pl.ds(pl.multiple_of(index * block, block), block)
            queries = columns_ref[place, base : base + HEAD_DIM]
            grad_out = grad_ref[place, part]
            inner = jnp.sum(
                grad_out.astype(jnp.float32) * out_ref[place, part].astype(jnp.float32),
                -1,
                keepdims=True,
            )
            scores = lax.dot_general(
                queries, keys, contract_columns, preferred_element_type=jnp.float32
            )
            weights = jnp.exp2(scores * EXPONENT - log_ref[place, head : head + 1])
            grad_weights = lax.dot_general(
                grad_out, values, contract_columns, preferred_element_type=jnp.float32
            )
            grad_scores = (weights * (grad_weights - inner)).astype(jnp.bfloat16)
            result_ref[place, base : base + HEAD_DIM] = (
                jnp.dot(grad_scores, keys, preferred_element_type=jnp.float32) * SCALE
            ).astype(jnp.bfloat16)
            key_acc[...] += lax.dot_general(
                grad_scores, queries, contract_rows, preferred_element_type=jnp.float32
            )
            value_acc[...] += lax.dot_general(
                weights.astype(jnp.bfloat16),
                grad_out,
                contract_rows,
                preferred_element_type=jnp.float32,
            )
            return carry

        lax.fori_loop(0, rows // block, step, 0)
        result_ref[:, base + HEAD_DIM : base + 2 * HEAD_DIM] = (key_acc[...] * SCALE).astype(
            jnp.bfloat16
        )
        result_ref[:, base + 2 * HEAD_DIM : base + 3 * HEAD_DIM] = value_acc[...].astype(
            jnp.bfloat16
        )


def attend_back(columns, output, logsum, grad_output, heads):
    rows = columns.shape[0]
    return pl.pallas_call(
        functools.partial(attend_back_kernel, heads, row_block(rows)),
        out_shape=jax.ShapeDtypeStruct(columns.shape, jnp.bfloat16),
        scratch_shapes=[
            pltpu.VMEM((rows, HEAD_DIM), jnp.float32),
            pltpu.VMEM((rows, HEAD_DIM), jnp.float32),
        ],
        cost_estimate=pl.CostEstimate(
            flops=heads * rows * rows * HEAD_DIM * 10,
            bytes_accessed=columns.size * 6,
            transcendentals=heads * rows * rows,
        ),
        name="attend_back",
    )(columns, output, logsum, grad_output)


def column_bias(query_bias, value_bias, heads):
    query_part = query_bias.reshape(heads, HEAD_DIM)
    value_part = value_bias.reshape(heads, HEAD_DIM)
    return jnp.stack([query_part, jnp.zeros_like(query_part), value_part], axis=1).reshape(-1)


def layer_biases(bias_layer, tensor_rank, width_local, hidden_local):
    query_bias = lax.dynamic_slice_in_dim(
        bias_layer, 6 * D + tensor_rank * width_local, width_local, 1
    )
    value_bias = lax.dynamic_slice_in_dim(
        bias_layer, 7 * D + tensor_rank * width_local, width_local, 1
    )
    out_bias = bias_layer[:, 8 * D : 9 * D]
    hidden_bias = lax.dynamic_slice_in_dim(
        bias_layer, 9 * D + tensor_rank * hidden_local, hidden_local, 1
    )
    last_bias = bias_layer[:, 9 * D + FF :]
    return (query_bias, value_bias, out_bias, hidden_bias, last_bias)


def forward_layer(states, weights, pieces, shifts, heads_local):
    query_bias, value_bias, out_bias, hidden_bias, last_bias = pieces
    joined = [
        gather_rows(
            modulate(states[stream], shifts[stream][0], shifts[stream][1]).astype(jnp.bfloat16),
            "tensor",
        )
        for stream in range(2)
    ]
    columns = jnp.concatenate(
        [
            (
                jnp.dot(joined[stream], weights[0][stream], preferred_element_type=jnp.float32)
                + column_bias(query_bias[stream], value_bias[stream], heads_local)
            ).astype(jnp.bfloat16)
            for stream in range(2)
        ]
    )
    attended, logsum = attend(columns, heads_local)
    split = joined[0].shape[0]
    out_rows = [attended[:split], attended[split:]]
    branch_attend = [
        scatter_rows(
            lax.dot_general(
                out_rows[stream],
                weights[1][stream],
                contract_columns,
                preferred_element_type=jnp.float32,
            ).astype(jnp.bfloat16),
            "tensor",
        )
        + out_bias[stream]
        for stream in range(2)
    ]
    middle = [states[stream] + shifts[stream][2] * branch_attend[stream] for stream in range(2)]
    joined_feed = [
        gather_rows(
            modulate(middle[stream], shifts[stream][3], shifts[stream][4]).astype(jnp.bfloat16),
            "tensor",
        )
        for stream in range(2)
    ]
    preact = [
        jnp.dot(joined_feed[stream], weights[2][stream], preferred_element_type=jnp.float32)
        + hidden_bias[stream]
        for stream in range(2)
    ]
    activated = [gelu_tanh(preact[stream]).astype(jnp.bfloat16) for stream in range(2)]
    branch_feed = [
        scatter_rows(
            lax.dot_general(
                activated[stream],
                weights[3][stream],
                contract_columns,
                preferred_element_type=jnp.float32,
            ).astype(jnp.bfloat16),
            "tensor",
        )
        + last_bias[stream]
        for stream in range(2)
    ]
    result = [middle[stream] + shifts[stream][5] * branch_feed[stream] for stream in range(2)]
    record = (
        states,
        joined,
        columns,
        attended,
        logsum,
        branch_attend,
        middle,
        joined_feed,
        preact,
        activated,
        branch_feed,
    )
    return (record, result)


def scatter_weights(grads):
    return [
        lax.psum_scatter(grad.astype(jnp.bfloat16), "dp", scatter_dimension=0, tiled=True).astype(
            jnp.float32
        )
        for grad in grads
    ]


def backward_layer(gradients, record, weights, shifts, heads_local):
    (
        states,
        joined,
        columns,
        attended,
        logsum,
        branch_attend,
        middle,
        joined_feed,
        preact,
        activated,
        branch_feed,
    ) = record
    split = joined[0].shape[0]
    out_rows = [attended[:split], attended[split:]]
    grad_branch = [shifts[stream][5] * gradients[stream] for stream in range(2)]
    gate_feed = [jnp.sum(gradients[stream] * branch_feed[stream], 0) for stream in range(2)]
    branch_rows = [
        gather_rows(grad_branch[stream].astype(jnp.bfloat16), "tensor") for stream in range(2)
    ]
    grad_contraction = scatter_weights(
        [
            lax.dot_general(
                branch_rows[stream],
                activated[stream],
                contract_rows,
                preferred_element_type=jnp.float32,
            )
            for stream in range(2)
        ]
    )
    grad_preact = []
    for stream in range(2):
        grad_activated = jnp.dot(
            branch_rows[stream], weights[3][stream], preferred_element_type=jnp.float32
        )
        gelu_back = jax.vjp(gelu_tanh, preact[stream])[1]
        grad_preact.append(gelu_back(grad_activated)[0].astype(jnp.bfloat16))
    hidden_sums = [jnp.sum(grad_preact[stream], 0, dtype=jnp.float32) for stream in range(2)]
    summed = [
        scatter_rows(
            lax.dot_general(
                grad_preact[stream],
                weights[2][stream],
                contract_columns,
                preferred_element_type=jnp.float32,
            ).astype(jnp.bfloat16),
            "tensor",
        )
        for stream in range(2)
    ]
    grad_expansion = scatter_weights(
        [
            lax.dot_general(
                joined_feed[stream],
                grad_preact[stream],
                contract_rows,
                preferred_element_type=jnp.float32,
            )
            for stream in range(2)
        ]
    )
    grad_middle, shift_feed, scale_feed = ([], [], [])
    for stream in range(2):
        shift_back = jax.vjp(modulate, middle[stream], shifts[stream][3], shifts[stream][4])[1]
        back_rows, back_shift, back_scale = shift_back(summed[stream])
        grad_middle.append(gradients[stream] + back_rows)
        shift_feed.append(back_shift)
        scale_feed.append(back_scale)
    grad_attend = [shifts[stream][2] * grad_middle[stream] for stream in range(2)]
    gate_attend = [jnp.sum(grad_middle[stream] * branch_attend[stream], 0) for stream in range(2)]
    attend_rows = [
        gather_rows(grad_attend[stream].astype(jnp.bfloat16), "tensor") for stream in range(2)
    ]
    grad_heads = jnp.concatenate(
        [
            jnp.dot(
                attend_rows[stream], weights[1][stream], preferred_element_type=jnp.float32
            ).astype(jnp.bfloat16)
            for stream in range(2)
        ]
    )
    grad_recombine = scatter_weights(
        [
            lax.dot_general(
                attend_rows[stream],
                out_rows[stream],
                contract_rows,
                preferred_element_type=jnp.float32,
            )
            for stream in range(2)
        ]
    )
    grad_columns = attend_back(columns, attended, logsum, grad_heads, heads_local)
    column_rows = [grad_columns[:split], grad_columns[split:]]
    column_sums = [
        jnp.sum(column_rows[stream], 0, dtype=jnp.float32).reshape(heads_local, 3, HEAD_DIM)
        for stream in range(2)
    ]
    summed = [
        scatter_rows(
            lax.dot_general(
                column_rows[stream],
                weights[0][stream],
                contract_columns,
                preferred_element_type=jnp.float32,
            ).astype(jnp.bfloat16),
            "tensor",
        )
        for stream in range(2)
    ]
    grad_projection = scatter_weights(
        [
            lax.dot_general(
                joined[stream],
                column_rows[stream],
                contract_rows,
                preferred_element_type=jnp.float32,
            )
            for stream in range(2)
        ]
    )
    tensor_rank = lax.axis_index("tensor")
    width_local = heads_local * HEAD_DIM
    hidden_local = preact[0].shape[1]

    def placed(length, values, offset):
        return lax.dynamic_update_slice_in_dim(
            jnp.zeros((length,), jnp.float32), values, offset, 0
        )

    new_grads, slot_grads, bias_grads = ([], [], [])
    for stream in range(2):
        shift_back = jax.vjp(modulate, states[stream], shifts[stream][0], shifts[stream][1])[1]
        back_rows, back_shift, back_scale = shift_back(summed[stream])
        new_grads.append(grad_middle[stream] + back_rows)
        slot_grad = jnp.concatenate(
            [
                back_shift,
                back_scale,
                gate_attend[stream],
                shift_feed[stream],
                scale_feed[stream],
                gate_feed[stream],
            ]
        )
        slot_grads.append(slot_grad)
        bias_grads.append(
            jnp.concatenate(
                [
                    slot_grad,
                    placed(D, column_sums[stream][:, 0].reshape(-1), tensor_rank * width_local),
                    placed(D, column_sums[stream][:, 2].reshape(-1), tensor_rank * width_local),
                    jnp.sum(grad_attend[stream], 0),
                    placed(FF, hidden_sums[stream], tensor_rank * hidden_local),
                    jnp.sum(grad_branch[stream], 0),
                ]
            )
        )
    weight_grads = (grad_projection, grad_recombine, grad_expansion, grad_contraction)
    return (new_grads, weight_grads, jnp.stack(bias_grads), jnp.stack(slot_grads))


def slot_table(silu_rows, modulation, slots):
    size = lax.axis_size("tensor")
    rank = lax.axis_index("tensor")
    count = silu_rows.shape[0]
    partial = jnp.einsum(
        "nd,lsdm->nlsm", silu_rows, modulation.astype(jnp.float32), precision=highest
    ).reshape(count, -1)
    width = partial.shape[1] // size
    owned = 0.0
    for step in range(size):
        block = lax.dynamic_slice_in_dim(partial, (rank ^ step) * width, width, 1)
        owned = owned + (exchange(block, "tensor", step) if step else block)
    onehot = (slots[:, None] == jnp.arange(count, dtype=jnp.int32)[None, :]).astype(jnp.float32)
    per_slot = jnp.dot(onehot, owned, precision=highest)
    mine = per_slot[0]
    for step in range(1, per_slot.shape[0]):
        mine = mine + exchange(per_slot[step], "dp", step)
    table = jnp.zeros((partial.shape[1],), jnp.float32)
    for step, block in enumerate(gather_parts(mine, "tensor")):
        table = lax.dynamic_update_slice_in_dim(table, block, (rank ^ step) * width, 0)
    return table.reshape(LAYERS, 2, -1)


def on_device(
    image_tokens,
    text_tokens,
    conditioning,
    slot_sequence,
    rank_counts,
    projection,
    recombine,
    expansion,
    contraction,
    modulation,
    biases,
    cotangent_image,
    cotangent_text,
):
    tensor_rank = lax.axis_index("tensor")
    flat_rank = lax.axis_index(("dp", "tensor"))
    heads_local = HEADS // lax.axis_size("tensor")
    width_local = heads_local * HEAD_DIM
    hidden_local = FF // lax.axis_size("tensor")
    bias_all = lax.all_gather(biases, ("dp", "tensor"), axis=2, tiled=True).astype(jnp.float32)
    shard_rows = modulation.shape[2]
    owned_rows = lax.dynamic_slice_in_dim(
        jax.nn.silu(conditioning), flat_rank * shard_rows, shard_rows, 1
    )
    slots = jnp.concatenate(gather_parts(slot_sequence, "dp"))
    slot_shifts = slot_table(owned_rows, modulation, slots) + bias_all[:, :, : 6 * D]
    live = (rank_counts[0] > 0).astype(jnp.float32)
    states = [image_tokens.astype(jnp.float32), text_tokens.astype(jnp.float32)]
    stored = []
    for tier in range(LAYERS):
        weights = [
            [
                lax.all_gather(matrix[tier, stream], "dp", axis=0, tiled=True)
                for stream in range(2)
            ]
            for matrix in (projection, recombine, expansion, contraction)
        ]
        pieces = layer_biases(bias_all[tier], tensor_rank, width_local, hidden_local)
        shifts = [
            [slot_shifts[tier, stream, part * D : (part + 1) * D] for part in range(6)]
            for stream in range(2)
        ]
        record, states = forward_layer(states, weights, pieces, shifts, heads_local)
        stored.append((weights, shifts, record))
    gradients = [
        cotangent_image.astype(jnp.float32) * live,
        cotangent_text.astype(jnp.float32) * live,
    ]
    slot_rows = jnp.dot(
        (
            slots[:, None] == jnp.arange(conditioning.shape[0], dtype=jnp.int32)[None, :]
        ).astype(jnp.float32),
        owned_rows,
        precision=highest,
    )
    weight_store, bias_store, modulation_store = ([], [], [])
    for tier in reversed(range(LAYERS)):
        weights, shifts, record = stored[tier]
        gradients, layer_grads, bias_part, slot_grads = backward_layer(
            gradients, record, weights, shifts, heads_local
        )
        weight_store.insert(0, layer_grads)
        bias_store.insert(0, bias_part)
        slot_sums = jnp.stack(gather_parts(sum_over(slot_grads, "tensor"), "dp"))
        modulation_store.insert(
            0, jnp.einsum("pd,psm->sdm", slot_rows, slot_sums, precision=highest)
        )
    stacked = [
        jnp.stack([jnp.stack(entry[kind]) for entry in weight_store]) for kind in range(4)
    ]
    biases_grad = lax.psum_scatter(
        jnp.stack(bias_store), ("dp", "tensor"), scatter_dimension=2, tiled=True
    )
    return (
        (states[0] * live).astype(jnp.bfloat16),
        (states[1] * live).astype(jnp.bfloat16),
        gradients[0],
        gradients[1],
        stacked[0],
        stacked[1],
        stacked[2],
        stacked[3],
        jnp.stack(modulation_store),
        biases_grad,
    )


def solution(mesh):
    in_specs = (
        P(("dp", "tensor"), None),
        P(("dp", "tensor"), None),
        P(),
        P("dp"),
        P("dp"),
        P(None, None, "dp", "tensor"),
        P(None, None, "dp", "tensor"),
        P(None, None, "dp", "tensor"),
        P(None, None, "dp", "tensor"),
        P(None, None, ("dp", "tensor"), None),
        P(None, None, ("dp", "tensor")),
        P(("dp", "tensor"), None),
        P(("dp", "tensor"), None),
    )
    out_specs = (
        P(("dp", "tensor"), None),
        P(("dp", "tensor"), None),
        P(("dp", "tensor"), None),
        P(("dp", "tensor"), None),
        P(None, None, "dp", "tensor"),
        P(None, None, "dp", "tensor"),
        P(None, None, "dp", "tensor"),
        P(None, None, "dp", "tensor"),
        P(None, None, ("dp", "tensor"), None),
        P(None, None, ("dp", "tensor")),
    )
    return jax.shard_map(
        on_device, mesh=mesh, in_specs=in_specs, out_specs=out_specs, check_vma=False
    )
```

time: 2700 us -> 2260 us (0.84)
  waiting for transfers between devices: 1410 us -> 1110 us
  matrix products: 493 us -> 279 us
  starting transfers between devices: 5.14 us -> 172 us
  Pallas kernels: 0 us -> 123 us
  blocking collectives: 350 us -> 263 us
  local copies, waits for them, and re-layouts: 255 us -> 186 us
  other arithmetic: 152 us -> 97 us
    all_gather x16, waiting for transfers between devices: 601 us -> 0.06 us  [on_device(): lax.all_gather(matrix[tier, stream], 'dp', axis=0, tiled=True)]
    ppermute x0 -> x136, waiting for transfers between devices: none -> 452 us  [exchange(): lax.ppermute(values, axis, [(rank, rank ^ step) for rank in range(size)])]
    dot_general x155 -> x49, matrix products: 481 us -> 264 us  [the longest x4 38 us: backward_layer(): jnp.dot(branch_rows[stream], weights[3][stream], preferred_element_type=j...]
    ppermute x0 -> x136, starting transfers between devices: none -> 170 us  [exchange(): lax.ppermute(values, axis, [(rank, rank ^ step) for rank in range(size)])]
    psum x2 -> x0, waiting for transfers between devices: 142 us -> none  [the longest x1 142 us: on_device(): lax.psum((grad_table, jnp.stack(bias_store)), ('dp', 'tensor'))]
    pallas_call x0 -> x4, Pallas kernels: none -> 123 us  [the longest x2 67.6 us: attend_back(): pl.pallas_call(functools.partial(attend_back_kernel, heads, row_block(row...]
    all_gather x8 -> x0, blocking collectives: 89 us -> none  [the longest x2 24.3 us: forward_layer(): lax.all_gather(normed[1], 'tensor', axis=0, tiled=True)]
    unnamed x629 -> x685, local copies, waits for them, and re-layouts: 31.2 us -> 100 us
  transfers between devices with their start and end apart: 42 -> 169, of which waited for: 30 -> 66; matrix products, arithmetic and copies ran while one was open for 24% -> 23% of each run, Pallas kernels for 0% -> 5%
where the time goes in v1:
time: 2260 us; the launch traced here: 2250 us
  waiting for transfers between devices  1110 us (49%)
  matrix products  279 us (12%)
  blocking collectives  263 us (12%)
  local copies, waits for them, and re-layouts  186 us (8%)
  starting transfers between devices  172 us (8%)
  Pallas kernels  123 us (5%)
  other arithmetic  97 us (4%)
    reduce_scatter x16, waiting for transfers between devices, scatter_weights(): lax.psum_scatter(grad.astype(jnp.bfloat16), 'dp', scatter_dimension=0, ti...  651 us
    ppermute x136, waiting for transfers between devices, exchange(): lax.ppermute(values, axis, [(rank, rank ^ step) for rank in range(size)])  452 us
    all_gather x1, blocking collectives, on_device(): lax.all_gather(biases, ('dp', 'tensor'), axis=2, tiled=True)  263 us
    ppermute x136, starting transfers between devices, exchange(): lax.ppermute(values, axis, [(rank, rank ^ step) for rank in range(size)])  170 us
    unnamed x685, local copies, waits for them, and re-layouts  100 us
    pallas_call x2, Pallas kernels, attend_back(): pl.pallas_call(functools.partial(attend_back_kernel, heads, row_block(row...  67.6 us
    pallas_call x2, Pallas kernels, attend(): pl.pallas_call(functools.partial(attend_kernel, heads, row_block(rows)),...  55.2 us
  transfers between devices with their start and end apart: 169, of which 66 were waited for; matrix products, arithmetic and copies ran while one was open for 23% of the time, Pallas kernels for 5%

profile of v1, /device:TPU:0, one launch (start us, length us, event | category | flops | bytes accessed | tf_op | source)
XLA Modules:
  0.0 2250.0 jit_solution(12835185728367855801)
XLA Ops:
  36.9 263.1 %all_gather.51 = bf16[2,2,21504]{1,0,2:T(2,128)(2,1)} all-gather(bf16[2,2,672]{1,0,2:T(2,128)(2,1)S(1)} %copy.74), channel_id=1, replica_groups=mesh['dp'=8,'tensor'=4] {'dp','tensor'}, dimensions={2}, use_global_device_ids=true | all-gather | bytes 177408 | tf_op jit(solution)/shard_map/all_gather | solution.py:507
  299.9 21.5 copy.75
  384.2 31.2 %collective-permute-done.25 = bf16[32,1536]{1,0:T(8,128)(2,1)S(1)} collective-permute-done((bf16[32,1536]{1,0:T(8,128)(2,1)S(1)}, bf16[32,1536]{1,0:T(8,128)(2,1)S(1)}, u32[]{:S(2)}, u32[]{:S(2)}) %collective-permute-start.25) | collective-permute-done | bytes 98336 | tf_op jit(solution)/shard_map/ppermute | solution.py:41
  424.4 7.3 add_convert_fusion.1
  433.4 27.6 %attend.2 = (bf16[1152,384]{1,0:T(8,128)(2,1)}, f32[1152,128]{1,0:T(8,128)}) custom-call(bf16[1152,1152]{1,0:T(8,128)(2,1)} %pad_maximum_fusion.9.columns_ref), custom_call_target="tpu_custom_call" | custom-call | flops 2038431744 | bytes 3981312 | tf_op jit(solution)/shard_map/attend/pallas_call | solution.py:107
  477.5 14.0 collective-permute-done.28
  492.9 13.4 collective-permute-done.27
  530.6 14.1 collective-permute-done.30
  546.2 10.9 fusion.48
  557.0 9.4 fusion.53
  574.3 13.8 collective-permute-done.34
  588.1 15.3 collective-permute-done.33
  614.0 31.9 %collective-permute-done.48 = bf16[32,1536]{1,0:T(8,128)(2,1)S(1)} collective-permute-done((bf16[32,1536]{1,0:T(8,128)(2,1)S(1)}, bf16[32,1536]{1,0:T(8,128)(2,1)S(1)}, u32[]{:S(2)}, u32[]{:S(2)}) %collective-permute-start.48) | collective-permute-done | bytes 98336 | tf_op jit(solution)/shard_map/ppermute | solution.py:41
  652.2 7.3 add_convert_fusion
  661.3 27.6 %attend.3 = (bf16[1152,384]{1,0:T(8,128)(2,1)}, f32[1152,128]{1,0:T(8,128)}) custom-call(bf16[1152,1152]{1,0:T(8,128)(2,1)} %pad_maximum_fusion.10.columns_ref), custom_call_target="tpu_custom_call" | custom-call | flops 2038431744 | bytes 3981312 | tf_op jit(solution)/shard_map/attend/pallas_call | solution.py:107
  735.8 13.8 collective-permute-done.51
  761.2 15.6 collective-permute-done.55
  777.1 14.9 collective-permute-done.54
  795.2 11.0 fusion.30
  809.1 15.5 convert_reduce_fusion
  824.6 7.3 fusion.56
  835.7 8.0 fusion.59
  843.8 9.7 collective-permute-done.73
  855.0 15.3 collective-permute-done.72
  874.4 12.9 collective-permute-done.58
  888.5 12.2 collective-permute-done.57
  915.1 30.5 %collective-permute-done.85 = bf16[32,1536]{1,0:T(8,128)(2,1)S(1)} collective-permute-done((bf16[32,1536]{1,0:T(8,128)(2,1)S(1)}, bf16[32,1536]{1,0:T(8,128)(2,1)S(1)}, u32[]{:S(2)}, u32[]{:S(2)}) %collective-permute-start.85) | collective-permute-done | bytes 98336 | tf_op jit(solution)/shard_map/ppermute | solution.py:41
  960.1 33.6 %attend_back.2 = bf16[1152,1152]{1,0:T(8,128)(2,1)} custom-call(bf16[1152,1152]{1,0:T(8,128)(2,1)} %pad_maximum_fusion.10.columns_ref, bf16[1152,384]{1,0:T(8,128)(2,1)} %get-tuple-element.15.out_ref, f32[1152,128]{1,0:T(8,128)} %get-tuple-element.16.log_ref, bf16[1152,384]{1,0:T(8,128)(2,1)} %pad_maximum_fusion.11.grad_ref), custom_call_target="tpu_custom_call" | custom-call | flops 5096079360 | bytes 7962624 | tf_op jit(solution)/shard_map/attend_back/pallas_call | solution.py:176
  993.7 7.0 convolution_convert_fusion.15
  1033.4 7.7 collective-permute-done.99
  1083.0 11.6 collective-permute-done.86
  1114.8 9.1 collective-permute-done.91
  1123.8 11.0 collective-permute-done.90
  1134.8 13.7 convert_reduce_fusion.1
  1157.9 17.7 collective-permute-done.94
  1175.6 15.8 collective-permute-done.93
  1202.3 16.8 collective-permute-done.97
  1219.1 15.9 collective-permute-done.96
  1239.8 34.0 %attend_back.3 = bf16[1152,1152]{1,0:T(8,128)(2,1)} custom-call(bf16[1152,1152]{1,0:T(8,128)(2,1)} %pad_maximum_fusion.9.columns_ref, bf16[1152,384]{1,0:T(8,128)(2,1)} %get-tuple-element.14.out_ref, f32[1152,128]{1,0:T(8,128)} %get-tuple-element.17.log_ref, bf16[1152,384]{1,0:T(8,128)(2,1)} %pad_maximum_fusion.12.grad_ref), custom_call_target="tpu_custom_call" | custom-call | flops 5096079360 | bytes 7962624 | tf_op jit(solution)/shard_map/attend_back/pallas_call | solution.py:176
  1276.9 7.0 convolution_convert_fusion.14
  1297.4 13.3 collective-permute-done.115
  1312.0 16.7 collective-permute-done.114
  1353.2 19.3 copy.95
  1372.5 21.0 reshape.414
  1406.4 9.0 convolution_convert_fusion.4
  1421.9 8.9 convolution_convert_fusion.2
  1437.4 11.2 convolution_convert_fusion
  1453.5 8.2 convolution_convert_fusion.5
  1468.4 9.0 convolution_convert_fusion.3
  1486.7 10.6 convolution_convert_fusion.1
  1571.3 8.3 reduce-scatter.30.cloned.1.call-done
  1579.6 33.0 %reduce-scatter.28.cloned.1.call-done = bf16[192,384]{1,0:T(8,128)(2,1)} async-done(((bf16[1536,384]{1,0:T(8,128)(2,1)}), bf16[192,384]{1,0:T(8,128)(2,1)}) %reduce-scatter.28.cloned.1.call-update) | async-done | bytes 147472 | tf_op jit(solution)/shard_map/reduce_scatter | solution.py:293
  1615.7 41.8 %reduce-scatter.26.cloned.1.call-done = bf16[192,1152]{1,0:T(8,128)(2,1)} async-done(((bf16[1536,1152]{1,0:T(8,128)(2,1)}), bf16[192,1152]{1,0:T(8,128)(2,1)}) %reduce-scatter.26.cloned.1.call-update) | async-done | bytes 442384 | tf_op jit(solution)/shard_map/reduce_scatter | solution.py:293
  1657.5 44.8 %reduce-scatter.24.cloned.1.call-done = bf16[192,1152]{1,0:T(8,128)(2,1)} async-done(((bf16[1536,1152]{1,0:T(8,128)(2,1)}), bf16[192,1152]{1,0:T(8,128)(2,1)}) %reduce-scatter.24.cloned.1.call-update) | async-done | bytes 442384 | tf_op jit(solution)/shard_map/reduce_scatter | solution.py:293
  1703.6 55.0 %reduce-scatter.42.cloned.1.call-done = bf16[192,1536]{1,0:T(8,128)(2,1)} async-done(((bf16[1536,1536]{1,0:T(8,128)(2,1)}), bf16[192,1536]{1,0:T(8,128)(2,1)}) %reduce-scatter.42.cloned.1.call-update) | async-done | bytes 589840 | tf_op jit(solution)/shard_map/reduce_scatter | solution.py:293
  1758.6 56.2 %reduce-scatter.40.cloned.1.call-done = bf16[192,1536]{1,0:T(8,128)(2,1)} async-done(((bf16[1536,1536]{1,0:T(8,128)(2,1)}), bf16[192,1536]{1,0:T(8,128)(2,1)}) %reduce-scatter.40.cloned.1.call-update) | async-done | bytes 589840 | tf_op jit(solution)/shard_map/reduce_scatter | solution.py:293
  1816.1 54.2 %reduce-scatter.50.cloned.1.call-done = bf16[192,1536]{1,0:T(8,128)(2,1)} async-done(((bf16[1536,1536]{1,0:T(8,128)(2,1)}), bf16[192,1536]{1,0:T(8,128)(2,1)}) %reduce-scatter.50.cloned.1.call-update) | async-done | bytes 589840 | tf_op jit(solution)/shard_map/reduce_scatter | solution.py:293
  1870.3 55.5 %reduce-scatter.48.cloned.1.call-done = bf16[192,1536]{1,0:T(8,128)(2,1)} async-done(((bf16[1536,1536]{1,0:T(8,128)(2,1)}), bf16[192,1536]{1,0:T(8,128)(2,1)}) %reduce-scatter.48.cloned.1.call-update) | async-done | bytes 589840 | tf_op jit(solution)/shard_map/reduce_scatter | solution.py:293
  1928.2 42.2 %reduce-scatter.22.cloned.1.call-done = bf16[192,1152]{1,0:T(8,128)(2,1)} async-done(((bf16[1536,1152]{1,0:T(8,128)(2,1)}), bf16[192,1152]{1,0:T(8,128)(2,1)}) %reduce-scatter.22.cloned.1.call-update) | async-done | bytes 442384 | tf_op jit(solution)/shard_map/reduce_scatter | solution.py:293
  1970.4 44.8 %reduce-scatter.20.cloned.1.call-done = bf16[192,1152]{1,0:T(8,128)(2,1)} async-done(((bf16[1536,1152]{1,0:T(8,128)(2,1)}), bf16[192,1152]{1,0:T(8,128)(2,1)}) %reduce-scatter.20.cloned.1.call-update) | async-done | bytes 442384 | tf_op jit(solution)/shard_map/reduce_scatter | solution.py:293
  2018.4 52.4 %reduce-scatter.38.cloned.1.call-done = bf16[192,1536]{1,0:T(8,128)(2,1)} async-done(((bf16[1536,1536]{1,0:T(8,128)(2,1)}), bf16[192,1536]{1,0:T(8,128)(2,1)}) %reduce-scatter.38.cloned.1.call-update) | async-done | bytes 589840 | tf_op jit(solution)/shard_map/reduce_scatter | solution.py:293
  2070.8 55.6 %reduce-scatter.36.cloned.1.call-done = bf16[192,1536]{1,0:T(8,128)(2,1)} async-done(((bf16[1536,1536]{1,0:T(8,128)(2,1)}), bf16[192,1536]{1,0:T(8,128)(2,1)}) %reduce-scatter.36.cloned.1.call-update) | async-done | bytes 589840 | tf_op jit(solution)/shard_map/reduce_scatter | solution.py:293
  2130.3 51.8 %reduce-scatter.46.cloned.1.call-done = bf16[192,1536]{1,0:T(8,128)(2,1)} async-done(((bf16[1536,1536]{1,0:T(8,128)(2,1)}), bf16[192,1536]{1,0:T(8,128)(2,1)}) %reduce-scatter.46.cloned.1.call-update) | async-done | bytes 589840 | tf_op jit(solution)/shard_map/reduce_scatter | solution.py:293
  2182.1 55.5 %reduce-scatter.44.cloned.1.call-done = bf16[192,1536]{1,0:T(8,128)(2,1)} async-done(((bf16[1536,1536]{1,0:T(8,128)(2,1)}), bf16[192,1536]{1,0:T(8,128)(2,1)}) %reduce-scatter.44.cloned.1.call-update) | async-done | bytes 589840 | tf_op jit(solution)/shard_map/reduce_scatter | solution.py:293
  (1295 shorter events, 575.6 us)
Async XLA Ops:
  7.2 412.8 %all-gather.35.cloned.1.call-start = ((), (), s32[]{:S(2)}) async-start(), calls=%async_computation.34 | async-start | bytes 3981312 | tf_op jit(solution)/shard_map/all_gather | solution.py:520
  10.1 414.3 %all-gather.33.cloned.1.call-start = ((), (), s32[]{:S(2)}) async-start(), calls=%async_computation.33 | async-start | bytes 3981312 | tf_op jit(solution)/shard_map/all_gather | solution.py:520
  10.8 450.2 %all-gather.45.cloned.1.call-start = ((), (), s32[]{:S(2)}) async-start(), calls=%async_computation.39 | async-start | bytes 1327104 | tf_op jit(solution)/shard_map/all_gather | solution.py:520
  12.9 453.6 %all-gather.37.cloned.1.call-start = ((), (), s32[]{:S(2)}) async-start(), calls=%async_computation.35 | async-start | bytes 1327104 | tf_op jit(solution)/shard_map/all_gather | solution.py:520
  13.4 498.7 %all-gather.47.cloned.1.call-start = ((), (), s32[]{:S(2)}) async-start(), calls=%async_computation.40 | async-start | bytes 5308416 | tf_op jit(solution)/shard_map/all_gather | solution.py:520
  16.6 499.0 %all-gather.49.cloned.1.call-start = ((), (), s32[]{:S(2)}) async-start(), calls=%async_computation.41 | async-start | bytes 5308416 | tf_op jit(solution)/shard_map/all_gather | solution.py:520
  19.7 526.5 %all-gather.39.cloned.1.call-start = ((), (), s32[]{:S(2)}) async-start(), calls=%async_computation.36 | async-start | bytes 5308416 | tf_op jit(solution)/shard_map/all_gather | solution.py:520
  20.4 536.6 %all-gather.41.cloned.1.call-start = ((), (), s32[]{:S(2)}) async-start(), calls=%async_computation.37 | async-start | bytes 5308416 | tf_op jit(solution)/shard_map/all_gather | solution.py:520
  21.2 628.1 %all-gather.51.cloned.1.call-start = ((), (), s32[]{:S(2)}) async-start(), calls=%async_computation.42 | async-start | bytes 3981312 | tf_op jit(solution)/shard_map/all_gather | solution.py:520
  21.9 630.3 %all-gather.43.cloned.1.call-start = ((), (), s32[]{:S(2)}) async-start(), calls=%async_computation.38 | async-start | bytes 3981312 | tf_op jit(solution)/shard_map/all_gather | solution.py:520
  22.5 666.4 %all-gather.59.cloned.1.call-start = ((), (), s32[]{:S(2)}) async-start(), calls=%async_computation.46 | async-start | bytes 1327104 | tf_op jit(solution)/shard_map/all_gather | solution.py:520
  23.2 671.2 %all-gather.53.cloned.1.call-start = ((), (), s32[]{:S(2)}) async-start(), calls=%async_computation.43 | async-start | bytes 1327104 | tf_op jit(solution)/shard_map/all_gather | solution.py:520
  23.8 685.0 %all-gather.61.cloned.1.call-start = ((), (), s32[]{:S(2)}) async-start(), calls=%async_computation.47 | async-start | bytes 5308416 | tf_op jit(solution)/shard_map/all_gather | solution.py:520
  24.6 692.6 %all-gather.63.cloned.1.call-start = ((), (), s32[]{:S(2)}) async-start(), calls=%async_computation.48 | async-start | bytes 5308416 | tf_op jit(solution)/shard_map/all_gather | solution.py:520
  25.1 770.1 %all-gather.55.cloned.1.call-start = ((), (), s32[]{:S(2)}) async-start(), calls=%async_computation.44 | async-start | bytes 5308416 | tf_op jit(solution)/shard_map/all_gather | solution.py:520
  25.7 783.4 %all-gather.57.cloned.1.call-start = ((), (), s32[]{:S(2)}) async-start(), calls=%async_computation.45 | async-start | bytes 5308416 | tf_op jit(solution)/shard_map/all_gather | solution.py:520
  25.8 299.1 %collective-permute-start = (s32[1]{0:T(128)}, s32[1]{0:T(128)}, u32[]{:S(2)}, u32[]{:S(2)}) collective-permute-start(s32[1]{0:T(128)} %param.16), channel_id=1, source_target_pairs={{0,4},{4,0},{8,12},{12,8},{16,20},{20,16},{24,28},{28,24},{1,5},{5... | collective-permute-start | bytes 20 | tf_op jit(solution)/shard_map/ppermute | solution.py:41
  26.3 301.4 %collective-permute-start.1 = (s32[1]{0:T(128)}, s32[1]{0:T(128)}, u32[]{:S(2)}, u32[]{:S(2)}) collective-permute-start(s32[1]{0:T(128)} %param.16), channel_id=1, source_target_pairs={{0,8},{4,12},{8,0},{12,4},{16,24},{20,28},{24,16},{28,20},{1,9},{5... | collective-permute-start | bytes 20 | tf_op jit(solution)/shard_map/ppermute | solution.py:41
  32.3 310.9 %collective-permute-start.9 = (f32[6,9216]{1,0:T(8,128)S(1)}, f32[6,9216]{1,0:T(8,128)S(1)}, u32[]{:S(2)}, u32[]{:S(2)}) collective-permute-start(f32[6,9216]{1,0:T(8,128)S(1)} %get-tuple-element.189), channel_id=1, source_target_pairs={{0,3},{1,2},{2,1},{3,0},{4,7},{5,6},{6,5},{7,4},{8,11},{9,10},{10,... | collective-permute-start | bytes 663560 | tf_op jit(solution)/shard_map/ppermute | solution.py:41
  34.9 308.4 %collective-permute-start.8 = (f32[6,9216]{1,0:T(8,128)S(1)}, f32[6,9216]{1,0:T(8,128)S(1)}, u32[]{:S(2)}, u32[]{:S(2)}) collective-permute-start(f32[6,9216]{1,0:T(8,128)S(1)} %get-tuple-element.190), channel_id=1, source_target_pairs={{0,2},{1,3},{2,0},{3,1},{4,6},{5,7},{6,4},{7,5},{8,10},{9,11},{10,... | collective-permute-start | bytes 663560 | tf_op jit(solution)/shard_map/ppermute | solution.py:41
  35.4 307.9 %collective-permute-start.7 = (f32[6,9216]{1,0:T(8,128)S(1)}, f32[6,9216]{1,0:T(8,128)S(1)}, u32[]{:S(2)}, u32[]{:S(2)}) collective-permute-start(f32[6,9216]{1,0:T(8,128)S(1)} %get-tuple-element.188), channel_id=1, source_target_pairs={{0,1},{1,0},{2,3},{3,2},{4,5},{5,4},{6,7},{7,6},{8,9},{9,8},{10,11... | collective-permute-start | bytes 663560 | tf_op jit(solution)/shard_map/ppermute | solution.py:41
  35.9 1488.0 %reduce-scatter.34.cloned.1.call-start = ((), (), s32[]{:S(2)}) async-start(), calls=%async_computation.24 | async-start | bytes 1327104 | tf_op jit(solution)/shard_map/reduce_scatter | solution.py:293
  376.7 46.8 %collective-permute-start.22 = (bf16[256,1536]{1,0:T(8,128)(2,1)S(1)}, bf16[256,1536]{1,0:T(8,128)(2,1)S(1)}, u32[]{:S(2)}, u32[]{:S(2)}) collective-permute-start(bf16[256,1536]{1,0:T(8,128)(2,1)S(1)} %fusion.121), channel_id=1, source_target_pairs={{0,3},{1,2},{2,1},{3,0},{4,7},{5,6},{6,5},{7,4},{8,11},{9,10},{10,... | collective-permute-start | bytes 2359304 | tf_op jit(solution)/shard_map/ppermute | solution.py:41
  379.9 43.7 %collective-permute-start.21 = (bf16[256,1536]{1,0:T(8,128)(2,1)S(1)}, bf16[256,1536]{1,0:T(8,128)(2,1)}, u32[]{:S(2)}, u32[]{:S(2)}) collective-permute-start(bf16[256,1536]{1,0:T(8,128)(2,1)S(1)} %fusion.121), channel_id=1, source_target_pairs={{0,2},{1,3},{2,0},{3,1},{4,6},{5,7},{6,4},{7,5},{8,10},{9,11},{10,... | collective-permute-start | bytes 2359304 | tf_op jit(solution)/shard_map/ppermute | solution.py:41
  379.9 43.7 %collective-permute-start.20 = (bf16[256,1536]{1,0:T(8,128)(2,1)S(1)}, bf16[256,1536]{1,0:T(8,128)(2,1)}, u32[]{:S(2)}, u32[]{:S(2)}) collective-permute-start(bf16[256,1536]{1,0:T(8,128)(2,1)S(1)} %fusion.121), channel_id=1, source_target_pairs={{0,1},{1,0},{2,3},{3,2},{4,5},{5,4},{6,7},{7,6},{8,9},{9,8},{10,11... | collective-permute-start | bytes 2359304 | tf_op jit(solution)/shard_map/ppermute | solution.py:41
  520.7 48.0 %collective-permute-start.46 = (bf16[32,1536]{1,0:T(8,128)(2,1)}, bf16[32,1536]{1,0:T(8,128)(2,1)S(1)}, u32[]{:S(2)}, u32[]{:S(2)}) collective-permute-start(bf16[32,1536]{1,0:T(8,128)(2,1)} %get-tuple-element.215), channel_id=1, source_target_pairs={{0,3},{1,2},{2,1},{3,0},{4,7},{5,6},{6,5},{7,4},{8,11},{9,10},{10,... | collective-permute-start | bytes 294920 | tf_op jit(solution)/shard_map/ppermute | solution.py:41
  522.1 48.1 %collective-permute-start.45 = (bf16[32,1536]{1,0:T(8,128)(2,1)}, bf16[32,1536]{1,0:T(8,128)(2,1)S(1)}, u32[]{:S(2)}, u32[]{:S(2)}) collective-permute-start(bf16[32,1536]{1,0:T(8,128)(2,1)} %get-tuple-element.216), channel_id=1, source_target_pairs={{0,2},{1,3},{2,0},{3,1},{4,6},{5,7},{6,4},{7,5},{8,10},{9,11},{10,... | collective-permute-start | bytes 294920 | tf_op jit(solution)/shard_map/ppermute | solution.py:41
  529.5 40.8 %collective-permute-start.44 = (bf16[32,1536]{1,0:T(8,128)(2,1)}, bf16[32,1536]{1,0:T(8,128)(2,1)}, u32[]{:S(2)}, u32[]{:S(2)}) collective-permute-start(bf16[32,1536]{1,0:T(8,128)(2,1)} %get-tuple-element.214), channel_id=1, source_target_pairs={{0,1},{1,0},{2,3},{3,2},{4,5},{5,4},{6,7},{7,6},{8,9},{9,8},{10,11... | collective-permute-start | bytes 294920 | tf_op jit(solution)/shard_map/ppermute | solution.py:41
  573.0 39.7 %collective-permute-start.49 = (bf16[32,1536]{1,0:T(8,128)(2,1)S(1)}, bf16[32,1536]{1,0:T(8,128)(2,1)S(1)}, u32[]{:S(2)}, u32[]{:S(2)}) collective-permute-start(bf16[32,1536]{1,0:T(8,128)(2,1)S(1)} %add_convert_fusion.6), channel_id=1, source_target_pairs={{0,3},{1,2},{2,1},{3,0},{4,7},{5,6},{6,5},{7,4},{8,11},{9,10},{10,... | collective-permute-start | bytes 294920 | tf_op jit(solution)/shard_map/ppermute | solution.py:41
  606.5 45.7 %collective-permute-start.37 = (bf16[256,1536]{1,0:T(8,128)(2,1)}, bf16[256,1536]{1,0:T(8,128)(2,1)}, u32[]{:S(2)}, u32[]{:S(2)}) collective-permute-start(bf16[256,1536]{1,0:T(8,128)(2,1)} %add_convert_fusion.3), channel_id=1, source_target_pairs={{0,3},{1,2},{2,1},{3,0},{4,7},{5,6},{6,5},{7,4},{8,11},{9,10},{10,... | collective-permute-start | bytes 2359304 | tf_op jit(solution)/shard_map/ppermute | solution.py:41
  608.1 44.1 %collective-permute-start.36 = (bf16[256,1536]{1,0:T(8,128)(2,1)}, bf16[256,1536]{1,0:T(8,128)(2,1)}, u32[]{:S(2)}, u32[]{:S(2)}) collective-permute-start(bf16[256,1536]{1,0:T(8,128)(2,1)} %add_convert_fusion.3), channel_id=1, source_target_pairs={{0,2},{1,3},{2,0},{3,1},{4,6},{5,7},{6,4},{7,5},{8,10},{9,11},{10,... | collective-permute-start | bytes 2359304 | tf_op jit(solution)/shard_map/ppermute | solution.py:41
  609.6 42.6 %collective-permute-start.35 = (bf16[256,1536]{1,0:T(8,128)(2,1)}, bf16[256,1536]{1,0:T(8,128)(2,1)}, u32[]{:S(2)}, u32[]{:S(2)}) collective-permute-start(bf16[256,1536]{1,0:T(8,128)(2,1)} %add_convert_fusion.3), channel_id=1, source_target_pairs={{0,1},{1,0},{2,3},{3,2},{4,5},{5,4},{6,7},{7,6},{8,9},{9,8},{10,11... | collective-permute-start | bytes 2359304 | tf_op jit(solution)/shard_map/ppermute | solution.py:41
  645.9 160.2 %collective-permute-start.70 = (bf16[256,1536]{1,0:T(8,128)(2,1)}, bf16[256,1536]{1,0:T(8,128)(2,1)}, u32[]{:S(2)}, u32[]{:S(2)}) collective-permute-start(bf16[256,1536]{1,0:T(8,128)(2,1)} %fusion.127), channel_id=1, source_target_pairs={{0,3},{1,2},{2,1},{3,0},{4,7},{5,6},{6,5},{7,4},{8,11},{9,10},{10,... | collective-permute-start | bytes 2359304 | tf_op jit(solution)/shard_map/ppermute | solution.py:41
  647.8 158.4 %collective-permute-start.69 = (bf16[256,1536]{1,0:T(8,128)(2,1)}, bf16[256,1536]{1,0:T(8,128)(2,1)}, u32[]{:S(2)}, u32[]{:S(2)}) collective-permute-start(bf16[256,1536]{1,0:T(8,128)(2,1)} %fusion.127), channel_id=1, source_target_pairs={{0,2},{1,3},{2,0},{3,1},{4,6},{5,7},{6,4},{7,5},{8,10},{9,11},{10,... | collective-permute-start | bytes 2359304 | tf_op jit(solution)/shard_map/ppermute | solution.py:41
  757.2 36.0 %collective-permute-start.53 = (bf16[256,1536]{1,0:T(8,128)(2,1)S(1)}, bf16[256,1536]{1,0:T(8,128)(2,1)S(1)}, u32[]{:S(2)}, u32[]{:S(2)}) collective-permute-start(bf16[256,1536]{1,0:T(8,128)(2,1)S(1)} %add_convert_fusion.2), channel_id=1, source_target_pairs={{0,1},{1,0},{2,3},{3,2},{4,5},{5,4},{6,7},{7,6},{8,9},{9,8},{10,11... | collective-permute-start | bytes 2359304 | tf_op jit(solution)/shard_map/ppermute | solution.py:41
  792.0 117.0 %collective-permute-start.67 = (bf16[32,1536]{1,0:T(8,128)(2,1)}, bf16[32,1536]{1,0:T(8,128)(2,1)}, u32[]{:S(2)}, u32[]{:S(2)}) collective-permute-start(bf16[32,1536]{1,0:T(8,128)(2,1)} %get-tuple-element.209), channel_id=1, source_target_pairs={{0,3},{1,2},{2,1},{3,0},{4,7},{5,6},{6,5},{7,4},{8,11},{9,10},{10,... | collective-permute-start | bytes 294920 | tf_op jit(solution)/shard_map/ppermute | solution.py:41
  794.1 116.4 %collective-permute-start.66 = (bf16[32,1536]{1,0:T(8,128)(2,1)}, bf16[32,1536]{1,0:T(8,128)(2,1)}, u32[]{:S(2)}, u32[]{:S(2)}) collective-permute-start(bf16[32,1536]{1,0:T(8,128)(2,1)} %get-tuple-element.210), channel_id=1, source_target_pairs={{0,2},{1,3},{2,0},{3,1},{4,6},{5,7},{6,4},{7,5},{8,10},{9,11},{10,... | collective-permute-start | bytes 294920 | tf_op jit(solution)/shard_map/ppermute | solution.py:41
  833.6 36.7 %collective-permute-start.72 = (bf16[256,1536]{1,0:T(8,128)(2,1)S(1)}, bf16[256,1536]{1,0:T(8,128)(2,1)S(1)}, u32[]{:S(2)}, u32[]{:S(2)}) collective-permute-start(bf16[256,1536]{1,0:T(8,128)(2,1)S(1)} %get-tuple-element.162), channel_id=1, source_target_pairs={{0,2},{1,3},{2,0},{3,1},{4,6},{5,7},{6,4},{7,5},{8,10},{9,11},{10,... | collective-permute-start | bytes 2359304 | tf_op jit(solution)/shard_map/ppermute | solution.py:41
  834.8 36.8 %collective-permute-start.71 = (bf16[256,1536]{1,0:T(8,128)(2,1)S(1)}, bf16[256,1536]{1,0:T(8,128)(2,1)S(1)}, u32[]{:S(2)}, u32[]{:S(2)}) collective-permute-start(bf16[256,1536]{1,0:T(8,128)(2,1)S(1)} %get-tuple-element.160), channel_id=1, source_target_pairs={{0,1},{1,0},{2,3},{3,2},{4,5},{5,4},{6,7},{7,6},{8,9},{9,8},{10,11... | collective-permute-start | bytes 2359304 | tf_op jit(solution)/shard_map/ppermute | solution.py:41
  907.1 47.9 %collective-permute-start.76 = (bf16[256,1536]{1,0:T(8,128)(2,1)}, bf16[256,1536]{1,0:T(8,128)(2,1)}, u32[]{:S(2)}, u32[]{:S(2)}) collective-permute-start(bf16[256,1536]{1,0:T(8,128)(2,1)} %get-tuple-element.175), channel_id=1, source_target_pairs={{0,3},{1,2},{2,1},{3,0},{4,7},{5,6},{6,5},{7,4},{8,11},{9,10},{10,... | collective-permute-start | bytes 2359304 | tf_op jit(solution)/shard_map/ppermute | solution.py:41
  908.1 46.8 %collective-permute-start.75 = (bf16[256,1536]{1,0:T(8,128)(2,1)}, bf16[256,1536]{1,0:T(8,128)(2,1)}, u32[]{:S(2)}, u32[]{:S(2)}) collective-permute-start(bf16[256,1536]{1,0:T(8,128)(2,1)} %get-tuple-element.175), channel_id=1, source_target_pairs={{0,2},{1,3},{2,0},{3,1},{4,6},{5,7},{6,4},{7,5},{8,10},{9,11},{10,... | collective-permute-start | bytes 2359304 | tf_op jit(solution)/shard_map/ppermute | solution.py:41
  909.0 46.0 %collective-permute-start.74 = (bf16[256,1536]{1,0:T(8,128)(2,1)}, bf16[256,1536]{1,0:T(8,128)(2,1)}, u32[]{:S(2)}, u32[]{:S(2)}) collective-permute-start(bf16[256,1536]{1,0:T(8,128)(2,1)} %get-tuple-element.175), channel_id=1, source_target_pairs={{0,1},{1,0},{2,3},{3,2},{4,5},{5,4},{6,7},{7,6},{8,9},{9,8},{10,11... | collective-permute-start | bytes 2359304 | tf_op jit(solution)/shard_map/ppermute | solution.py:41
  952.8 571.1 %reduce-scatter.32.cloned.1.call-start = ((), (), s32[]{:S(2)}) async-start(), calls=%async_computation.23 | async-start | bytes 1327104 | tf_op jit(solution)/shard_map/reduce_scatter | solution.py:293
  1002.2 79.4 %collective-permute-start.88 = (bf16[256,1536]{1,0:T(8,128)(2,1)}, bf16[256,1536]{1,0:T(8,128)(2,1)}, u32[]{:S(2)}, u32[]{:S(2)}) collective-permute-start(bf16[256,1536]{1,0:T(8,128)(2,1)} %get-tuple-element.158), channel_id=1, source_target_pairs={{0,3},{1,2},{2,1},{3,0},{4,7},{5,6},{6,5},{7,4},{8,11},{9,10},{10,... | collective-permute-start | bytes 2359304 | tf_op jit(solution)/shard_map/ppermute | solution.py:41
  1003.4 79.6 %collective-permute-start.87 = (bf16[256,1536]{1,0:T(8,128)(2,1)}, bf16[256,1536]{1,0:T(8,128)(2,1)}, u32[]{:S(2)}, u32[]{:S(2)}) collective-permute-start(bf16[256,1536]{1,0:T(8,128)(2,1)} %get-tuple-element.159), channel_id=1, source_target_pairs={{0,2},{1,3},{2,0},{3,1},{4,6},{5,7},{6,4},{7,5},{8,10},{9,11},{10,... | collective-permute-start | bytes 2359304 | tf_op jit(solution)/shard_map/ppermute | solution.py:41
  1025.2 543.8 %reduce-scatter.52.cloned.1.call-start = ((), (), s32[]{:S(2)}) async-start(), calls=%async_computation.49 | async-start | bytes 11354112
  1199.0 36.0 %collective-permute-start.96 = (bf16[256,1536]{1,0:T(8,128)(2,1)S(1)}, bf16[256,1536]{1,0:T(8,128)(2,1)}, u32[]{:S(2)}, u32[]{:S(2)}) collective-permute-start(bf16[256,1536]{1,0:T(8,128)(2,1)S(1)} %multiply_convert_fusion.3), channel_id=1, source_target_pairs={{0,2},{1,3},{2,0},{3,1},{4,6},{5,7},{6,4},{7,5},{8,10},{9,11},{10,... | collective-permute-start | bytes 2359304 | tf_op jit(solution)/shard_map/ppermute | solution.py:41
  1287.0 60.2 %collective-permute-start.112 = (bf16[256,1536]{1,0:T(8,128)(2,1)}, bf16[256,1536]{1,0:T(8,128)(2,1)S(1)}, u32[]{:S(2)}, u32[]{:S(2)}) collective-permute-start(bf16[256,1536]{1,0:T(8,128)(2,1)} %get-tuple-element.152), channel_id=1, source_target_pairs={{0,3},{1,2},{2,1},{3,0},{4,7},{5,6},{6,5},{7,4},{8,11},{9,10},{10,... | collective-permute-start | bytes 2359304 | tf_op jit(solution)/shard_map/ppermute | solution.py:41
  1288.4 58.8 %collective-permute-start.111 = (bf16[256,1536]{1,0:T(8,128)(2,1)}, bf16[256,1536]{1,0:T(8,128)(2,1)S(1)}, u32[]{:S(2)}, u32[]{:S(2)}) collective-permute-start(bf16[256,1536]{1,0:T(8,128)(2,1)} %get-tuple-element.153), channel_id=1, source_target_pairs={{0,2},{1,3},{2,0},{3,1},{4,6},{5,7},{6,4},{7,5},{8,10},{9,11},{10,... | collective-permute-start | bytes 2359304 | tf_op jit(solution)/shard_map/ppermute | solution.py:41
  1310.7 38.2 %collective-permute-start.110 = (bf16[256,1536]{1,0:T(8,128)(2,1)}, bf16[256,1536]{1,0:T(8,128)(2,1)S(1)}, u32[]{:S(2)}, u32[]{:S(2)}) collective-permute-start(bf16[256,1536]{1,0:T(8,128)(2,1)} %get-tuple-element.151), channel_id=1, source_target_pairs={{0,1},{1,0},{2,3},{3,2},{4,5},{5,4},{6,7},{7,6},{8,9},{9,8},{10,11... | collective-permute-start | bytes 2359304 | tf_op jit(solution)/shard_map/ppermute | solution.py:41
  1393.6 186.0 %reduce-scatter.30.cloned.1.call-start = ((), (), s32[]{:S(2)}) async-start(), calls=%async_computation.22 | async-start | bytes 1327104 | tf_op jit(solution)/shard_map/reduce_scatter | solution.py:293
  1397.3 215.3 %reduce-scatter.28.cloned.1.call-start = ((), (), s32[]{:S(2)}) async-start(), calls=%async_computation.21 | async-start | bytes 1327104 | tf_op jit(solution)/shard_map/reduce_scatter | solution.py:293
  1402.1 255.4 %reduce-scatter.26.cloned.1.call-start = ((), (), s32[]{:S(2)}) async-start(), calls=%async_computation.20 | async-start | bytes 3981312 | tf_op jit(solution)/shard_map/reduce_scatter | solution.py:293
  1406.3 296.0 %reduce-scatter.24.cloned.1.call-start = ((), (), s32[]{:S(2)}) async-start(), calls=%async_computation.19 | async-start | bytes 3981312 | tf_op jit(solution)/shard_map/reduce_scatter | solution.py:293
  1415.4 343.2 %reduce-scatter.42.cloned.1.call-start = ((), (), s32[]{:S(2)}) async-start(), calls=%async_computation.28 | async-start | bytes 5308416 | tf_op jit(solution)/shard_map/reduce_scatter | solution.py:293
  1420.2 394.6 %reduce-scatter.40.cloned.1.call-start = ((), (), s32[]{:S(2)}) async-start(), calls=%async_computation.27 | async-start | bytes 5308416 | tf_op jit(solution)/shard_map/reduce_scatter | solution.py:293
  1430.9 439.4 %reduce-scatter.50.cloned.1.call-start = ((), (), s32[]{:S(2)}) async-start(), calls=%async_computation.32 | async-start | bytes 5308416 | tf_op jit(solution)/shard_map/reduce_scatter | solution.py:293
  1436.7 489.1 %reduce-scatter.48.cloned.1.call-start = ((), (), s32[]{:S(2)}) async-start(), calls=%async_computation.31 | async-start | bytes 5308416 | tf_op jit(solution)/shard_map/reduce_scatter | solution.py:293
  1448.6 521.8 %reduce-scatter.22.cloned.1.call-start = ((), (), s32[]{:S(2)}) async-start(), calls=%async_computation.18 | async-start | bytes 3981312 | tf_op jit(solution)/shard_map/reduce_scatter | solution.py:293
  1453.4 561.7 %reduce-scatter.20.cloned.1.call-start = ((), (), s32[]{:S(2)}) async-start(), calls=%async_computation.17 | async-start | bytes 3981312 | tf_op jit(solution)/shard_map/reduce_scatter | solution.py:293
  1461.7 609.1 %reduce-scatter.38.cloned.1.call-start = ((), (), s32[]{:S(2)}) async-start(), calls=%async_computation.26 | async-start | bytes 5308416 | tf_op jit(solution)/shard_map/reduce_scatter | solution.py:293
  1467.3 659.2 %reduce-scatter.36.cloned.1.call-start = ((), (), s32[]{:S(2)}) async-start(), calls=%async_computation.25 | async-start | bytes 5308416 | tf_op jit(solution)/shard_map/reduce_scatter | solution.py:293
  1477.5 704.6 %reduce-scatter.46.cloned.1.call-start = ((), (), s32[]{:S(2)}) async-start(), calls=%async_computation.30 | async-start | bytes 5308416 | tf_op jit(solution)/shard_map/reduce_scatter | solution.py:293
  1482.3 755.3 %reduce-scatter.44.cloned.1.call-start = ((), (), s32[]{:S(2)}) async-start(), calls=%async_computation.29 | async-start | bytes 5308416 | tf_op jit(solution)/shard_map/reduce_scatter | solution.py:293
  (425 other events, 6873.0 us)
Sparse Core Ops, SparseCore 0:
  10.2 45.5 all-gather.34
  58.1 47.3 all-gather.32
  107.1 24.6 all-gather.44
  133.2 27.3 all-gather.36
  162.7 56.3 all-gather.46
  221.2 60.9 all-gather.48
  284.4 55.0 all-gather.38
  341.6 54.7 all-gather.40
  398.1 41.3 all-gather.50
  440.9 40.4 all-gather.42
  483.0 21.5 all-gather.58
  506.1 22.5 all-gather.52
  530.3 51.2 all-gather.60
  583.1 50.5 all-gather.62
  635.2 50.5 all-gather.54
  687.2 50.5 all-gather.56
  952.9 30.1 reduce-scatter.33
  1025.3 30.5 reduce-scatter.31
  1393.7 151.6 reduce-scatter.51
  1547.5 32.0 reduce-scatter.29
  1581.9 30.6 reduce-scatter.27
  1615.5 41.9 reduce-scatter.25
  1660.0 42.3 reduce-scatter.23
  1705.1 53.4 reduce-scatter.41
  1761.5 53.2 reduce-scatter.39
  1816.9 53.3 reduce-scatter.49
  1872.4 53.3 reduce-scatter.47
  1928.1 42.1 reduce-scatter.21
  1972.8 42.3 reduce-scatter.19
  2017.3 53.4 reduce-scatter.37
  2073.1 53.2 reduce-scatter.35
  2128.8 53.3 reduce-scatter.45
  2184.3 53.3 reduce-scatter.43

commit v2 on v1

--- a/solution.py
+++ b/solution.py
@@ -65,6 +65,62 @@
     for step in range(1, lax.axis_size(axis)):
         total = total + exchange(values, axis, step)
     return total
+
+
+def after(values, *needed):
+    return lax.optimization_barrier((values, needed))[0]
+
+
+def spread_kernel(chunks_ref, out_ref):
+    count, _, width = chunks_ref.shape
+    for place in range(count):
+        out_ref[:, place * width : (place + 1) * width] = chunks_ref[place]
+
+
+def split_kernel(values_ref, out_ref):
+    count, _, width = out_ref.shape
+    for place in range(count):
+        out_ref[place] = values_ref[:, place * width : (place + 1) * width]
+
+
+def gather_biases(biases):
+    width = biases.shape[2]
+    held = biases.reshape(1, LAYERS * 2, width)
+    held = gather_rows(gather_rows(held, "tensor")[None], "dp")
+    outer, inner = held.shape[:2]
+    chunks = held.reshape(outer * inner, -1).astype(jnp.float32)
+    order = (
+        (jnp.arange(outer, dtype=jnp.int32) ^ lax.axis_index("dp"))[:, None] * inner
+        + (jnp.arange(inner, dtype=jnp.int32) ^ lax.axis_index("tensor"))[None, :]
+    ).reshape(-1)
+    select = (
+        order[:, None] == jnp.arange(outer * inner, dtype=jnp.int32)[None, :]
+    ).astype(jnp.float32)
+    ordered = jnp.dot(select, chunks, precision=highest)
+    spread = pl.pallas_call(
+        spread_kernel,
+        out_shape=jax.ShapeDtypeStruct((LAYERS * 2, outer * inner * width), jnp.float32),
+        name="spread",
+    )(ordered.reshape(outer * inner, LAYERS * 2, width))
+    return spread.reshape(LAYERS, 2, -1)
+
+
+def scatter_biases(values, width):
+    outer, inner = lax.axis_size("dp"), lax.axis_size("tensor")
+    chunks = pl.pallas_call(
+        split_kernel,
+        out_shape=jax.ShapeDtypeStruct((outer * inner, LAYERS * 2, width), jnp.float32),
+        name="split",
+    )(values.reshape(LAYERS * 2, -1))
+    chunks = chunks.reshape(outer, inner, LAYERS * 2, width)
+    for axis, size in (("dp", outer), ("tensor", inner)):
+        rank = lax.axis_index(axis)
+        total = lax.dynamic_index_in_dim(chunks, rank, 0, False)
+        for step in range(1, size):
+            block = lax.dynamic_index_in_dim(chunks, rank ^ step, 0, False)
+            total = total + exchange(block, axis, step)
+        chunks = total
+    return chunks.reshape(LAYERS, 2, width)
 
 
 def row_block(rows):
@@ -288,16 +344,62 @@
     return (record, result)
 
 
+def weight_grads_kernel(count, *refs):
+    out_ref = refs[-1]
+    offset = 0
+    for index in range(count):
+        left, right = refs[2 * index], refs[2 * index + 1]
+        width = right.shape[1]
+        tile = 384 if width % 384 == 0 else width
+        for place in range(0, width, tile):
+            out_ref[:, offset + place : offset + place + tile] = lax.dot_general(
+                left[...],
+                right[:, place : place + tile],
+                contract_rows,
+                preferred_element_type=jnp.float32,
+            ).astype(jnp.bfloat16)
+        offset += width
+
+
+def weight_grads(pairs):
+    tile = 256
+    specs, operands, total, flops, moved = ([], [], 0, 0, 0)
+    for left, right, place in pairs:
+        rows, width = left.shape[0], right.shape[1]
+        specs.append(pl.BlockSpec((rows, tile), lambda index: (0, index)))
+        specs.append(pl.BlockSpec((rows, width), lambda index, place=place: (place, 0)))
+        operands += [left, right]
+        total += width
+        flops += 2 * rows * width * left.shape[1]
+        moved += 2 * (left.size + rows * width)
+    depth = pairs[0][0].shape[1]
+    return pl.pallas_call(
+        functools.partial(weight_grads_kernel, len(pairs)),
+        grid=(depth // tile,),
+        in_specs=specs,
+        out_specs=pl.BlockSpec((tile, total), lambda index: (index, 0)),
+        out_shape=jax.ShapeDtypeStruct((depth, total), jnp.bfloat16),
+        cost_estimate=pl.CostEstimate(
+            flops=flops, bytes_accessed=moved + 2 * depth * total, transcendentals=0
+        ),
+        name="weight_grads",
+    )(*operands)
+
+
 def scatter_weights(grads):
-    return [
-        lax.psum_scatter(grad.astype(jnp.bfloat16), "dp", scatter_dimension=0, tiled=True).astype(
-            jnp.float32
-        )
-        for grad in grads
-    ]
-
-
-def backward_layer(gradients, record, weights, shifts, heads_local):
+    return lax.psum_scatter(grads, "dp", scatter_dimension=0, tiled=True)
+
+
+def unpack_weights(shares, offset, width):
+    return jnp.stack(
+        [
+            shares[:, offset + stream * width : offset + (stream + 1) * width].astype(jnp.float32)
+            for stream in range(2)
+        ]
+    )
+
+
+def backward_layer(gradients, record, weights, shifts, heads_local, pending):
     (
         states,
         joined,
@@ -318,21 +420,15 @@
     branch_rows = [
         gather_rows(grad_branch[stream].astype(jnp.bfloat16), "tensor") for stream in range(2)
     ]
-    grad_contraction = scatter_weights(
-        [
-            lax.dot_general(
-                branch_rows[stream],
-                activated[stream],
-                contract_rows,
-                preferred_element_type=jnp.float32,
-            )
-            for stream in range(2)
-        ]
-    )
+    grad_contraction = weight_grads(
+        [(branch_rows[stream], activated[stream], 0) for stream in range(2)]
+    )
+    branch_rows, feed_weights = after((branch_rows, weights[3]), grad_contraction, *pending[:1])
+    grad_contraction = scatter_weights(grad_contraction)
     grad_preact = []
     for stream in range(2):
         grad_activated = jnp.dot(
-            branch_rows[stream], weights[3][stream], preferred_element_type=jnp.float32
+            branch_rows[stream], feed_weights[stream], preferred_element_type=jnp.float32
         )
         gelu_back = jax.vjp(gelu_tanh, preact[stream])[1]
         grad_preact.append(gelu_back(grad_activated)[0].astype(jnp.bfloat16))
@@ -349,18 +445,13 @@
         )
         for stream in range(2)
     ]
-    grad_expansion = scatter_weights(
-        [
-            lax.dot_general(
-                joined_feed[stream],
-                grad_preact[stream],
-                contract_rows,
-                preferred_element_type=jnp.float32,
-            )
-            for stream in range(2)
-        ]
-    )
+    grad_expansion = weight_grads(
+        [(joined_feed[stream], grad_preact[stream], 0) for stream in range(2)]
+    )
+    summed = after(summed, grad_expansion)
+    grad_expansion = scatter_weights(grad_expansion)
     grad_middle, shift_feed, scale_feed = ([], [], [])
+    summed = after(summed, *pending[1:])
     for stream in range(2):
         shift_back = jax.vjp(modulate, middle[stream], shifts[stream][3], shifts[stream][4])[1]
         back_rows, back_shift, back_scale = shift_back(summed[stream])
@@ -380,17 +471,6 @@
             for stream in range(2)
         ]
     )
-    grad_recombine = scatter_weights(
-        [
-            lax.dot_general(
-                attend_rows[stream],
-                out_rows[stream],
-                contract_rows,
-                preferred_element_type=jnp.float32,
-            )
-            for stream in range(2)
-        ]
-    )
     grad_columns = attend_back(columns, attended, logsum, grad_heads, heads_local)
     column_rows = [grad_columns[:split], grad_columns[split:]]
     column_sums = [
@@ -409,17 +489,17 @@
         )
         for stream in range(2)
     ]
-    grad_projection = scatter_weights(
+    text_place = split // attend_rows[1].shape[0]
+    grad_attention = weight_grads(
         [
-            lax.dot_general(
-                joined[stream],
-                column_rows[stream],
-                contract_rows,
-                preferred_element_type=jnp.float32,
-            )
-            for stream in range(2)
+            (attend_rows[0], attended, 0),
+            (attend_rows[1], attended, text_place),
+            (joined[0], grad_columns, 0),
+            (joined[1], grad_columns, text_place),
         ]
     )
+    summed = after(summed, grad_attention)
+    grad_attention = scatter_weights(grad_attention)
     tensor_rank = lax.axis_index("tensor")
     width_local = heads_local * HEAD_DIM
     hidden_local = preact[0].shape[1]
@@ -457,8 +537,15 @@
                 ]
             )
         )
-    weight_grads = (grad_projection, grad_recombine, grad_expansion, grad_contraction)
-    return (new_grads, weight_grads, jnp.stack(bias_grads), jnp.stack(slot_grads))
+    out_width = attended.shape[1]
+    layer_grads = (
+        unpack_weights(grad_attention, 2 * out_width, 3 * out_width),
+        unpack_weights(grad_attention, 0, out_width),
+        unpack_weights(grad_expansion, 0, hidden_local),
+        unpack_weights(grad_contraction, 0, hidden_local),
+    )
+    pending = (grad_contraction, grad_expansion, grad_attention)
+    return (new_grads, layer_grads, pending, jnp.stack(bias_grads), jnp.stack(slot_grads))
 
 
 def slot_table(silu_rows, modulation, slots):
@@ -504,7 +591,7 @@
     heads_local = HEADS // lax.axis_size("tensor")
     width_local = heads_local * HEAD_DIM
     hidden_local = FF // lax.axis_size("tensor")
-    bias_all = lax.all_gather(biases, ("dp", "tensor"), axis=2, tiled=True).astype(jnp.float32)
+    bias_all = gather_biases(biases)
     shard_rows = modulation.shape[2]
     owned_rows = lax.dynamic_slice_in_dim(
         jax.nn.silu(conditioning), flat_rank * shard_rows, shard_rows, 1
@@ -516,10 +603,7 @@
     stored = []
     for tier in range(LAYERS):
         weights = [
-            [
-                lax.all_gather(matrix[tier, stream], "dp", axis=0, tiled=True)
-                for stream in range(2)
-            ]
+            lax.all_gather(matrix[tier], "dp", axis=1, tiled=True)
             for matrix in (projection, recombine, expansion, contraction)
         ]
         pieces = layer_biases(bias_all[tier], tensor_rank, width_local, hidden_local)
@@ -540,11 +624,11 @@
         owned_rows,
         precision=highest,
     )
-    weight_store, bias_store, modulation_store = ([], [], [])
+    weight_store, bias_store, modulation_store, pending = ([], [], [], ())
     for tier in reversed(range(LAYERS)):
         weights, shifts, record = stored[tier]
-        gradients, layer_grads, bias_part, slot_grads = backward_layer(
-            gradients, record, weights, shifts, heads_local
+        gradients, layer_grads, pending, bias_part, slot_grads = backward_layer(
+            gradients, record, weights, shifts, heads_local, pending
         )
         weight_store.insert(0, layer_grads)
         bias_store.insert(0, bias_part)
@@ -553,11 +637,9 @@
             0, jnp.einsum("pd,psm->sdm", slot_rows, slot_sums, precision=highest)
         )
     stacked = [
-        jnp.stack([jnp.stack(entry[kind]) for entry in weight_store]) for kind in range(4)
-    ]
-    biases_grad = lax.psum_scatter(
-        jnp.stack(bias_store), ("dp", "tensor"), scatter_dimension=2, tiled=True
-    )
+        jnp.stack([entry[kind] for entry in weight_store]) for kind in range(4)
+    ]
+    biases_grad = scatter_biases(jnp.stack(bias_store), biases.shape[2])
     return (
         (states[0] * live).astype(jnp.bfloat16),
         (states[1] * live).astype(jnp.bfloat16),

time: 2260 us -> 1360 us (0.60)
  waiting for transfers between devices: 1110 us -> 523 us
  blocking collectives: 263 us -> 0 us
  matrix products: 279 us -> 180 us
  local copies, waits for them, and re-layouts: 186 us -> 102 us
  Pallas kernels: 123 us -> 203 us
  other arithmetic: 97 us -> 124 us
    reduce_scatter x16 -> x6, waiting for transfers between devices: 651 us -> 0.03 us  [scatter_weights(): return lax.psum_scatter(grads, 'dp', scatter_dimension=0, tiled=True)]
    all_gather x1 -> x0, blocking collectives: 263 us -> none  [on_device(): lax.all_gather(biases, ('dp', 'tensor'), axis=2, tiled=True)]
    dot_general x20 -> x5, matrix products: 134 us -> 36.2 us  [the longest x4 36 us: backward_layer(): jnp.dot(branch_rows[stream], feed_weights[stream], preferred_element_type...]
    pallas_call x0 -> x8, Pallas kernels: none -> 81 us  [the longest x6 77.2 us: weight_grads(): pl.pallas_call(functools.partial(weight_grads_kernel, len(pairs)), grid=(...]
    all_gather x16 -> x8, waiting for transfers between devices: 0.06 us -> 71.5 us  [on_device(): lax.all_gather(matrix[tier], 'dp', axis=1, tiled=True)]
    unnamed x685 -> x636, local copies, waits for them, and re-layouts: 100 us -> 34.2 us
    concatenate x0 -> x16, other arithmetic: none -> 30.8 us  [gather_rows(): return jnp.concatenate(gather_parts(values, axis), axis=0)]
    ppermute x136 -> x156, starting transfers between devices: 170 us -> 191 us  [exchange(): lax.ppermute(values, axis, [(rank, rank ^ step) for rank in range(size)])]
  transfers between devices with their start and end apart: 169 -> 170, of which waited for: 66 -> 51; matrix products, arithmetic and copies ran while one was open for 23% -> 29% of each run, Pallas kernels for 5% -> 15%
where the time goes in v2:
time: 1360 us; the launch traced here: 1340 us
  waiting for transfers between devices  523 us (38%)
  Pallas kernels  203 us (15%)
  starting transfers between devices  193 us (14%)
  matrix products  180 us (13%)
  other arithmetic  124 us (9%)
  local copies, waits for them, and re-layouts  102 us (8%)
  between operations  20.1 us (1%)
    ppermute x156, waiting for transfers between devices, exchange(): lax.ppermute(values, axis, [(rank, rank ^ step) for rank in range(size)])  450 us
    ppermute x156, starting transfers between devices, exchange(): lax.ppermute(values, axis, [(rank, rank ^ step) for rank in range(size)])  191 us
    pallas_call x6, Pallas kernels, weight_grads(): pl.pallas_call(functools.partial(weight_grads_kernel, len(pairs)), grid=(...  77.2 us
    all_gather x8, waiting for transfers between devices, on_device(): lax.all_gather(matrix[tier], 'dp', axis=1, tiled=True)  71.5 us
    pallas_call x2, Pallas kernels, attend_back(): pl.pallas_call(functools.partial(attend_back_kernel, heads, row_block(row...  67.1 us
    pallas_call x2, Pallas kernels, attend(): pl.pallas_call(functools.partial(attend_kernel, heads, row_block(rows)),...  55 us
    dot_general x4, matrix products, backward_layer(): jnp.dot(branch_rows[stream], feed_weights[stream], preferred_element_type...  36 us
    unnamed x636, local copies, waits for them, and re-layouts  34.2 us
  transfers between devices with their start and end apart: 170, of which 51 were waited for; matrix products, arithmetic and copies ran while one was open for 29% of the time, Pallas kernels for 15%

profile of v2, /device:TPU:0, one launch (start us, length us, event | category | flops | bytes accessed | tf_op | source)
XLA Modules:
  0.0 1344.2 jit_solution(2766216070381025108)
XLA Ops:
  56.3 4.6 concatenate.97
  65.9 5.0 collective-permute-done.24
  73.0 6.0 collective-permute-done.26
  125.9 12.5 collective-permute-done.30
  139.8 15.7 %collective-permute-done.31 = bf16[256,1536]{1,0:T(8,128)(2,1)S(1)} collective-permute-done((bf16[256,1536]{1,0:T(8,128)(2,1)S(1)}, bf16[256,1536]{1,0:T(8,128)(2,1)S(1)}, u32[]{:S(2)}, u32[]{:S(2)}) %collective-permute-start.31) | collective-permute-done | bytes 786464 | tf_op jit(solution)/shard_map/ppermute | solution.py:41
  159.8 6.6 add_convert_fusion.1
  170.0 27.6 %attend.2 = (bf16[1152,384]{1,0:T(8,128)(2,1)}, f32[1152,128]{1,0:T(8,128)}) custom-call(bf16[1152,1152]{1,0:T(8,128)(2,1)} %pad_maximum_fusion.9.columns_ref), custom_call_target="tpu_custom_call" | custom-call | flops 2038431744 | bytes 3981312 | tf_op jit(solution)/shard_map/attend/pallas_call | solution.py:163
  210.8 16.4 %collective-permute-done.36 = bf16[256,1536]{1,0:T(8,128)(2,1)S(1)} collective-permute-done((bf16[256,1536]{1,0:T(8,128)(2,1)S(1)}, bf16[256,1536]{1,0:T(8,128)(2,1)S(1)}, u32[]{:S(2)}, u32[]{:S(2)}) %collective-permute-start.36) | collective-permute-done | bytes 786464 | tf_op jit(solution)/shard_map/ppermute | solution.py:41
  228.0 16.2 %collective-permute-done.37 = bf16[256,1536]{1,0:T(8,128)(2,1)S(1)} collective-permute-done((bf16[256,1536]{1,0:T(8,128)(2,1)S(1)}, bf16[256,1536]{1,0:T(8,128)(2,1)S(1)}, u32[]{:S(2)}, u32[]{:S(2)}) %collective-permute-start.37) | collective-permute-done | bytes 786464 | tf_op jit(solution)/shard_map/ppermute | solution.py:41
  252.3 4.6 multiply_convert_fusion.7
  256.9 52.3 %all-gather.23.cloned.1.call-done = bf16[1,2,1536,1536]{3,2,1,0:T(8,128)(2,1)} async-done(((bf16[1,2,192,1536]{3,2,1,0:T(8,128)(2,1)}), bf16[1,2,1536,1536]{3,2,1,0:T(8,128)(2,1)}) %all-gather.23.cloned.1.call-update) | async-done | bytes 9437200 | tf_op jit(solution)/shard_map/all_gather | solution.py:606
  309.2 4.2 fusion.58
  317.1 12.3 multiply_convert_fusion.1
  329.4 5.5 fusion.44
  339.8 16.0 %collective-permute-done.42 = bf16[256,1536]{1,0:T(8,128)(2,1)S(1)} collective-permute-done((bf16[256,1536]{1,0:T(8,128)(2,1)S(1)}, bf16[256,1536]{1,0:T(8,128)(2,1)S(1)}, u32[]{:S(2)}, u32[]{:S(2)}) %collective-permute-start.42) | collective-permute-done | bytes 786464 | tf_op jit(solution)/shard_map/ppermute | solution.py:41
  358.1 14.3 %collective-permute-done.43 = bf16[256,1536]{1,0:T(8,128)(2,1)S(1)} collective-permute-done((bf16[256,1536]{1,0:T(8,128)(2,1)S(1)}, bf16[256,1536]{1,0:T(8,128)(2,1)S(1)}, u32[]{:S(2)}, u32[]{:S(2)}) %collective-permute-start.43) | collective-permute-done | bytes 786464 | tf_op jit(solution)/shard_map/ppermute | solution.py:41
  385.6 25.3 %collective-permute-done.58 = bf16[32,1536]{1,0:T(8,128)(2,1)S(1)} collective-permute-done((bf16[32,1536]{1,0:T(8,128)(2,1)S(1)}, bf16[32,1536]{1,0:T(8,128)(2,1)S(1)}, u32[]{:S(2)}, u32[]{:S(2)}) %collective-permute-start.58) | collective-permute-done | bytes 98336 | tf_op jit(solution)/shard_map/ppermute | solution.py:41
  411.0 5.9 collective-permute-done.59
  419.8 7.6 add_convert_fusion
  429.0 27.5 %attend.3 = (bf16[1152,384]{1,0:T(8,128)(2,1)}, f32[1152,128]{1,0:T(8,128)}) custom-call(bf16[1152,1152]{1,0:T(8,128)(2,1)} %pad_maximum_fusion.10.columns_ref), custom_call_target="tpu_custom_call" | custom-call | flops 2038431744 | bytes 3981312 | tf_op jit(solution)/shard_map/attend/pallas_call | solution.py:163
  470.6 15.7 %collective-permute-done.60 = bf16[256,1536]{1,0:T(8,128)(2,1)S(1)} collective-permute-done((bf16[256,1536]{1,0:T(8,128)(2,1)S(1)}, bf16[256,1536]{1,0:T(8,128)(2,1)S(1)}, u32[]{:S(2)}, u32[]{:S(2)}) %collective-permute-start.60) | collective-permute-done | bytes 786464 | tf_op jit(solution)/shard_map/ppermute | solution.py:41
  489.2 19.5 %collective-permute-done.61 = bf16[256,1536]{1,0:T(8,128)(2,1)S(1)} collective-permute-done((bf16[256,1536]{1,0:T(8,128)(2,1)S(1)}, bf16[256,1536]{1,0:T(8,128)(2,1)S(1)}, u32[]{:S(2)}, u32[]{:S(2)}) %collective-permute-start.61) | collective-permute-done | bytes 786464 | tf_op jit(solution)/shard_map/ppermute | solution.py:41
  516.2 4.9 collective-permute-done.80
  528.2 4.7 multiply_convert_fusion.6
  532.9 8.3 collective-permute-done.63
  541.2 9.7 collective-permute-done.64
  550.9 10.7 multiply_convert_fusion
  561.6 13.0 weight_grads.6
  576.5 19.1 %all-gather.31.cloned.1.call-done = bf16[1,2,1536,1536]{3,2,1,0:T(8,128)(2,1)} async-done(((bf16[1,2,192,1536]{3,2,1,0:T(8,128)(2,1)}), bf16[1,2,1536,1536]{3,2,1,0:T(8,128)(2,1)}) %all-gather.31.cloned.1.call-update) | async-done | bytes 9437200 | tf_op jit(solution)/shard_map/all_gather | solution.py:606
  599.0 6.0 convert_reduce_fusion.5
  605.3 12.3 convert_reduce_fusion
  617.5 12.5 weight_grads.7
  643.9 8.3 fusion.42
  655.1 5.3 fusion.45
  664.5 8.5 collective-permute-done.84
  675.0 16.0 %collective-permute-done.85 = bf16[256,1536]{1,0:T(8,128)(2,1)S(1)} collective-permute-done((bf16[256,1536]{1,0:T(8,128)(2,1)S(1)}, bf16[256,1536]{1,0:T(8,128)(2,1)S(1)}, u32[]{:S(2)}, u32[]{:S(2)}) %collective-permute-start.85) | collective-permute-done | bytes 786464 | tf_op jit(solution)/shard_map/ppermute | solution.py:41
  702.9 8.6 collective-permute-done.66
  713.5 16.0 %collective-permute-done.67 = bf16[256,1536]{1,0:T(8,128)(2,1)S(1)} collective-permute-done((bf16[256,1536]{1,0:T(8,128)(2,1)S(1)}, bf16[256,1536]{1,0:T(8,128)(2,1)S(1)}, u32[]{:S(2)}, u32[]{:S(2)}) %collective-permute-start.67) | collective-permute-done | bytes 786464 | tf_op jit(solution)/shard_map/ppermute | solution.py:41
  729.6 4.4 multiply_reduce_fusion.15
  741.7 12.8 collective-permute-done.90
  754.5 12.6 collective-permute-done.91
  770.2 33.7 %attend_back.2.refs_5_.refs_7_ = bf16[1152,1152]{1,0:T(8,128)(2,1)} custom-call(bf16[1152,1152]{1,0:T(8,128)(2,1)} %pad_maximum_fusion.10.columns_ref, bf16[1152,384]{1,0:T(8,128)(2,1)} %get-tuple-element.33.out_ref.refs_1_.refs_3_, f32[1152,128]{1,0:T(8,128)} %get-tuple-element.40.log_ref, bf16[1152,384]{1,0:T(8,128)(2,1)} %pad_maximum_fusion.11.grad_ref), custom_call_target="tpu_custom_call" | custom-call | flops 5096079360 | bytes 7962624 | tf_op jit(solution)/shard_map/attend_back/pallas_call | solution.py:232
  803.8 13.3 weight_grads.8
  817.6 7.0 convolution_convert_fusion.3
  834.7 28.4 %collective-permute-done.100 = bf16[32,1536]{1,0:T(8,128)(2,1)S(1)} collective-permute-done((bf16[32,1536]{1,0:T(8,128)(2,1)S(1)}, bf16[32,1536]{1,0:T(8,128)(2,1)S(1)}, u32[]{:S(2)}, u32[]{:S(2)}) %collective-permute-start.100) | collective-permute-done | bytes 98336 | tf_op jit(solution)/shard_map/ppermute | solution.py:41
  863.4 5.0 collective-permute-done.99
  882.4 22.3 %collective-permute-done.105 = bf16[32,1536]{1,0:T(8,128)(2,1)S(1)} collective-permute-done((bf16[32,1536]{1,0:T(8,128)(2,1)S(1)}, bf16[32,1536]{1,0:T(8,128)(2,1)S(1)}, u32[]{:S(2)}, u32[]{:S(2)}) %collective-permute-start.105) | collective-permute-done | bytes 98336 | tf_op jit(solution)/shard_map/ppermute | solution.py:41
  905.4 4.8 collective-permute-done.107
  912.7 12.6 weight_grads.9
  933.3 5.5 pad_maximum_fusion.2.refs_0_
  966.6 4.7 convert_reduce_fusion.6
  971.3 13.1 convert_reduce_fusion.1
  984.4 12.5 weight_grads.10
  1011.9 7.1 collective-permute-done.143
  1020.6 4.7 convolution_bitcast_fusion
  1031.7 7.6 fusion.43
  1054.7 26.8 %collective-permute-done.113 = bf16[32,1536]{1,0:T(8,128)(2,1)S(1)} collective-permute-done((bf16[32,1536]{1,0:T(8,128)(2,1)}, bf16[32,1536]{1,0:T(8,128)(2,1)S(1)}, u32[]{:S(2)}, u32[]{:S(2)}) %collective-permute-start.113) | collective-permute-done | bytes 98336 | tf_op jit(solution)/shard_map/ppermute | solution.py:41
  1107.6 31.3 %collective-permute-done.119 = bf16[32,1536]{1,0:T(8,128)(2,1)S(1)} collective-permute-done((bf16[32,1536]{1,0:T(8,128)(2,1)S(1)}, bf16[32,1536]{1,0:T(8,128)(2,1)S(1)}, u32[]{:S(2)}, u32[]{:S(2)}) %collective-permute-start.119) | collective-permute-done | bytes 98336 | tf_op jit(solution)/shard_map/ppermute | solution.py:41
  1143.5 33.4 %attend_back.3.refs_5_.refs_7_ = bf16[1152,1152]{1,0:T(8,128)(2,1)} custom-call(bf16[1152,1152]{1,0:T(8,128)(2,1)} %pad_maximum_fusion.9.columns_ref, bf16[1152,384]{1,0:T(8,128)(2,1)} %get-tuple-element.32.out_ref.refs_1_.refs_3_, f32[1152,128]{1,0:T(8,128)} %get-tuple-element.50.log_ref, bf16[1152,384]{1,0:T(8,128)(2,1)} %pad_maximum_fusion.12.grad_ref), custom_call_target="tpu_custom_call" | custom-call | flops 5096079360 | bytes 7962624 | tf_op jit(solution)/shard_map/attend_back/pallas_call | solution.py:232
  1183.2 13.3 weight_grads.11
  1198.3 6.5 convolution_convert_fusion.2
  1215.0 30.3 %collective-permute-done.125 = bf16[32,1536]{1,0:T(8,128)(2,1)S(1)} collective-permute-done((bf16[32,1536]{1,0:T(8,128)(2,1)}, bf16[32,1536]{1,0:T(8,128)(2,1)S(1)}, u32[]{:S(2)}, u32[]{:S(2)}) %collective-permute-start.125) | collective-permute-done | bytes 98336 | tf_op jit(solution)/shard_map/ppermute | solution.py:41
  1257.8 8.0 collective-permute-start.147
  1287.9 4.5 collective-permute-start.130
  (1267 shorter events, 472.9 us)
Async XLA Ops:
  7.2 152.6 %all-gather.17.cloned.1.call-start = ((), (), s32[]{:S(2)}) async-start(), calls=%async_computation.12 | async-start | bytes 7962624 | tf_op jit(solution)/shard_map/all_gather | solution.py:606
  10.2 187.4 %all-gather.19.cloned.1.call-start = ((), (), s32[]{:S(2)}) async-start(), calls=%async_computation.13 | async-start | bytes 2654208 | tf_op jit(solution)/shard_map/all_gather | solution.py:606
  12.2 240.0 %all-gather.21.cloned.1.call-start = ((), (), s32[]{:S(2)}) async-start(), calls=%async_computation.14 | async-start | bytes 10616832 | tf_op jit(solution)/shard_map/all_gather | solution.py:606
  15.5 293.7 %all-gather.23.cloned.1.call-start = ((), (), s32[]{:S(2)}) async-start(), calls=%async_computation.15 | async-start | bytes 10616832 | tf_op jit(solution)/shard_map/all_gather | solution.py:606
  18.7 398.2 %all-gather.25.cloned.1.call-start = ((), (), s32[]{:S(2)}) async-start(), calls=%async_computation.16 | async-start | bytes 7962624 | tf_op jit(solution)/shard_map/all_gather | solution.py:606
  19.3 437.1 %all-gather.27.cloned.1.call-start = ((), (), s32[]{:S(2)}) async-start(), calls=%async_computation.17 | async-start | bytes 2654208 | tf_op jit(solution)/shard_map/all_gather | solution.py:606
  19.9 508.2 %all-gather.29.cloned.1.call-start = ((), (), s32[]{:S(2)}) async-start(), calls=%async_computation.18 | async-start | bytes 10616832 | tf_op jit(solution)/shard_map/all_gather | solution.py:606
  20.6 574.9 %all-gather.31.cloned.1.call-start = ((), (), s32[]{:S(2)}) async-start(), calls=%async_computation.19 | async-start | bytes 10616832 | tf_op jit(solution)/shard_map/all_gather | solution.py:606
  23.9 37.0 %collective-permute-start.20 = (bf16[1,4,672]{2,1,0:T(4,128)(2,1)S(1)}, bf16[1,4,672]{2,1,0:T(4,128)(2,1)}, u32[]{:S(2)}, u32[]{:S(2)}) collective-permute-start(bf16[1,4,672]{2,1,0:T(4,128)(2,1)S(1)} %reshape.415), channel_id=1, source_target_pairs={{0,1},{1,0},{2,3},{3,2},{4,5},{5,4},{6,7},{7,6},{8,9},{9,8},{10,11... | collective-permute-start | bytes 16136 | tf_op jit(solution)/shard_map/ppermute | solution.py:41
  25.4 36.9 %collective-permute-start.21 = (bf16[1,4,672]{2,1,0:T(4,128)(2,1)S(1)}, bf16[1,4,672]{2,1,0:T(4,128)(2,1)}, u32[]{:S(2)}, u32[]{:S(2)}) collective-permute-start(bf16[1,4,672]{2,1,0:T(4,128)(2,1)S(1)} %reshape.415), channel_id=1, source_target_pairs={{0,2},{1,3},{2,0},{3,1},{4,6},{5,7},{6,4},{7,5},{8,10},{9,11},{10,... | collective-permute-start | bytes 16136 | tf_op jit(solution)/shard_map/ppermute | solution.py:41
  27.0 35.4 %collective-permute-start.22 = (bf16[1,4,672]{2,1,0:T(4,128)(2,1)S(1)}, bf16[1,4,672]{2,1,0:T(4,128)(2,1)}, u32[]{:S(2)}, u32[]{:S(2)}) collective-permute-start(bf16[1,4,672]{2,1,0:T(4,128)(2,1)S(1)} %reshape.415), channel_id=1, source_target_pairs={{0,3},{1,2},{2,1},{3,0},{4,7},{5,6},{6,5},{7,4},{8,11},{9,10},{10,... | collective-permute-start | bytes 16136 | tf_op jit(solution)/shard_map/ppermute | solution.py:41
  27.5 939.1 %reduce-scatter.7.cloned.1.call-start = ((), (), s32[]{:S(2)}) async-start(), calls=%async_computation.6 | async-start | bytes 10616832 | tf_op jit(solution)/shard_map/reduce_scatter | solution.py:390
  54.1 34.9 %collective-permute-start.7 = (f32[6,9216]{1,0:T(8,128)S(1)}, f32[6,9216]{1,0:T(8,128)S(1)}, u32[]{:S(2)}, u32[]{:S(2)}) collective-permute-start(f32[6,9216]{1,0:T(8,128)S(1)} %get-tuple-element.224), channel_id=1, source_target_pairs={{0,1},{1,0},{2,3},{3,2},{4,5},{5,4},{6,7},{7,6},{8,9},{9,8},{10,11... | collective-permute-start | bytes 663560 | tf_op jit(solution)/shard_map/ppermute | solution.py:41
  118.8 36.7 %collective-permute-start.31 = (bf16[256,1536]{1,0:T(8,128)(2,1)S(1)}, bf16[256,1536]{1,0:T(8,128)(2,1)S(1)}, u32[]{:S(2)}, u32[]{:S(2)}) collective-permute-start(bf16[256,1536]{1,0:T(8,128)(2,1)S(1)} %fusion.71), channel_id=1, source_target_pairs={{0,2},{1,3},{2,0},{3,1},{4,6},{5,7},{6,4},{7,5},{8,10},{9,11},{10,... | collective-permute-start | bytes 2359304 | tf_op jit(solution)/shard_map/ppermute | solution.py:41
  120.1 37.1 %collective-permute-start.32 = (bf16[256,1536]{1,0:T(8,128)(2,1)S(1)}, bf16[256,1536]{1,0:T(8,128)(2,1)S(1)}, u32[]{:S(2)}, u32[]{:S(2)}) collective-permute-start(bf16[256,1536]{1,0:T(8,128)(2,1)S(1)} %fusion.71), channel_id=1, source_target_pairs={{0,3},{1,2},{2,1},{3,0},{4,7},{5,6},{6,5},{7,4},{8,11},{9,10},{10,... | collective-permute-start | bytes 2359304 | tf_op jit(solution)/shard_map/ppermute | solution.py:41
  122.3 44.2 %collective-permute-start.33 = (bf16[32,1536]{1,0:T(8,128)(2,1)}, bf16[32,1536]{1,0:T(8,128)(2,1)}, u32[]{:S(2)}, u32[]{:S(2)}) collective-permute-start(bf16[32,1536]{1,0:T(8,128)(2,1)} %fusion.112), channel_id=1, source_target_pairs={{0,1},{1,0},{2,3},{3,2},{4,5},{5,4},{6,7},{7,6},{8,9},{9,8},{10,11... | collective-permute-start | bytes 294920 | tf_op jit(solution)/shard_map/ppermute | solution.py:41
  123.0 43.5 %collective-permute-start.34 = (bf16[32,1536]{1,0:T(8,128)(2,1)}, bf16[32,1536]{1,0:T(8,128)(2,1)}, u32[]{:S(2)}, u32[]{:S(2)}) collective-permute-start(bf16[32,1536]{1,0:T(8,128)(2,1)} %fusion.112), channel_id=1, source_target_pairs={{0,2},{1,3},{2,0},{3,1},{4,6},{5,7},{6,4},{7,5},{8,10},{9,11},{10,... | collective-permute-start | bytes 294920 | tf_op jit(solution)/shard_map/ppermute | solution.py:41
  155.5 221.7 %collective-permute-start.81 = (bf16[32,1536]{1,0:T(8,128)(2,1)}, bf16[32,1536]{1,0:T(8,128)(2,1)}, u32[]{:S(2)}, u32[]{:S(2)}) collective-permute-start(bf16[32,1536]{1,0:T(8,128)(2,1)} %fusion.120), channel_id=1, source_target_pairs={{0,1},{1,0},{2,3},{3,2},{4,5},{5,4},{6,7},{7,6},{8,9},{9,8},{10,11... | collective-permute-start | bytes 294920 | tf_op jit(solution)/shard_map/ppermute | solution.py:41
  158.1 221.7 %collective-permute-start.82 = (bf16[32,1536]{1,0:T(8,128)(2,1)}, bf16[32,1536]{1,0:T(8,128)(2,1)}, u32[]{:S(2)}, u32[]{:S(2)}) collective-permute-start(bf16[32,1536]{1,0:T(8,128)(2,1)} %fusion.120), channel_id=1, source_target_pairs={{0,2},{1,3},{2,0},{3,1},{4,6},{5,7},{6,4},{7,5},{8,10},{9,11},{10,... | collective-permute-start | bytes 294920 | tf_op jit(solution)/shard_map/ppermute | solution.py:41
  207.6 36.6 %collective-permute-start.37 = (bf16[256,1536]{1,0:T(8,128)(2,1)S(1)}, bf16[256,1536]{1,0:T(8,128)(2,1)S(1)}, u32[]{:S(2)}, u32[]{:S(2)}) collective-permute-start(bf16[256,1536]{1,0:T(8,128)(2,1)S(1)} %get-tuple-element.200), channel_id=1, source_target_pairs={{0,2},{1,3},{2,0},{3,1},{4,6},{5,7},{6,4},{7,5},{8,10},{9,11},{10,... | collective-permute-start | bytes 2359304 | tf_op jit(solution)/shard_map/ppermute | solution.py:41
  207.6 36.6 %collective-permute-start.38 = (bf16[256,1536]{1,0:T(8,128)(2,1)S(1)}, bf16[256,1536]{1,0:T(8,128)(2,1)S(1)}, u32[]{:S(2)}, u32[]{:S(2)}) collective-permute-start(bf16[256,1536]{1,0:T(8,128)(2,1)S(1)} %get-tuple-element.199), channel_id=1, source_target_pairs={{0,3},{1,2},{2,1},{3,0},{4,7},{5,6},{6,5},{7,4},{8,11},{9,10},{10,... | collective-permute-start | bytes 2359304 | tf_op jit(solution)/shard_map/ppermute | solution.py:41
  246.7 66.8 %collective-permute-start.39 = (bf16[256,1536]{1,0:T(8,128)(2,1)S(1)}, bf16[256,1536]{1,0:T(8,128)(2,1)S(1)}, u32[]{:S(2)}, u32[]{:S(2)}) collective-permute-start(bf16[256,1536]{1,0:T(8,128)(2,1)S(1)} %add_convert_fusion.4), channel_id=1, source_target_pairs={{0,1},{1,0},{2,3},{3,2},{4,5},{5,4},{6,7},{7,6},{8,9},{9,8},{10,11... | collective-permute-start | bytes 2359304 | tf_op jit(solution)/shard_map/ppermute | solution.py:41
  250.9 64.1 %collective-permute-start.40 = (bf16[256,1536]{1,0:T(8,128)(2,1)S(1)}, bf16[256,1536]{1,0:T(8,128)(2,1)}, u32[]{:S(2)}, u32[]{:S(2)}) collective-permute-start(bf16[256,1536]{1,0:T(8,128)(2,1)S(1)} %add_convert_fusion.4), channel_id=1, source_target_pairs={{0,2},{1,3},{2,0},{3,1},{4,6},{5,7},{6,4},{7,5},{8,10},{9,11},{10,... | collective-permute-start | bytes 2359304 | tf_op jit(solution)/shard_map/ppermute | solution.py:41
  252.2 64.4 %collective-permute-start.41 = (bf16[256,1536]{1,0:T(8,128)(2,1)S(1)}, bf16[256,1536]{1,0:T(8,128)(2,1)}, u32[]{:S(2)}, u32[]{:S(2)}) collective-permute-start(bf16[256,1536]{1,0:T(8,128)(2,1)S(1)} %add_convert_fusion.4), channel_id=1, source_target_pairs={{0,3},{1,2},{2,1},{3,0},{4,7},{5,6},{6,5},{7,4},{8,11},{9,10},{10,... | collective-permute-start | bytes 2359304 | tf_op jit(solution)/shard_map/ppermute | solution.py:41
  336.7 35.7 %collective-permute-start.43 = (bf16[256,1536]{1,0:T(8,128)(2,1)S(1)}, bf16[256,1536]{1,0:T(8,128)(2,1)S(1)}, u32[]{:S(2)}, u32[]{:S(2)}) collective-permute-start(bf16[256,1536]{1,0:T(8,128)(2,1)S(1)} %get-tuple-element.197), channel_id=1, source_target_pairs={{0,2},{1,3},{2,0},{3,1},{4,6},{5,7},{6,4},{7,5},{8,10},{9,11},{10,... | collective-permute-start | bytes 2359304 | tf_op jit(solution)/shard_map/ppermute | solution.py:41
  338.2 35.3 %collective-permute-start.44 = (bf16[256,1536]{1,0:T(8,128)(2,1)S(1)}, bf16[256,1536]{1,0:T(8,128)(2,1)S(1)}, u32[]{:S(2)}, u32[]{:S(2)}) collective-permute-start(bf16[256,1536]{1,0:T(8,128)(2,1)S(1)} %get-tuple-element.196), channel_id=1, source_target_pairs={{0,3},{1,2},{2,1},{3,0},{4,7},{5,6},{6,5},{7,4},{8,11},{9,10},{10,... | collective-permute-start | bytes 2359304 | tf_op jit(solution)/shard_map/ppermute | solution.py:41
  375.7 44.0 %collective-permute-start.45 = (bf16[256,1536]{1,0:T(8,128)(2,1)S(1)}, bf16[256,1536]{1,0:T(8,128)(2,1)}, u32[]{:S(2)}, u32[]{:S(2)}) collective-permute-start(bf16[256,1536]{1,0:T(8,128)(2,1)S(1)} %add_convert_fusion.3), channel_id=1, source_target_pairs={{0,1},{1,0},{2,3},{3,2},{4,5},{5,4},{6,7},{7,6},{8,9},{9,8},{10,11... | collective-permute-start | bytes 2359304 | tf_op jit(solution)/shard_map/ppermute | solution.py:41
  377.2 42.5 %collective-permute-start.46 = (bf16[256,1536]{1,0:T(8,128)(2,1)S(1)}, bf16[256,1536]{1,0:T(8,128)(2,1)}, u32[]{:S(2)}, u32[]{:S(2)}) collective-permute-start(bf16[256,1536]{1,0:T(8,128)(2,1)S(1)} %add_convert_fusion.3), channel_id=1, source_target_pairs={{0,2},{1,3},{2,0},{3,1},{4,6},{5,7},{6,4},{7,5},{8,10},{9,11},{10,... | collective-permute-start | bytes 2359304 | tf_op jit(solution)/shard_map/ppermute | solution.py:41
  379.8 39.9 %collective-permute-start.47 = (bf16[256,1536]{1,0:T(8,128)(2,1)S(1)}, bf16[256,1536]{1,0:T(8,128)(2,1)}, u32[]{:S(2)}, u32[]{:S(2)}) collective-permute-start(bf16[256,1536]{1,0:T(8,128)(2,1)S(1)} %add_convert_fusion.3), channel_id=1, source_target_pairs={{0,3},{1,2},{2,1},{3,0},{4,7},{5,6},{6,5},{7,4},{8,11},{9,10},{10,... | collective-permute-start | bytes 2359304 | tf_op jit(solution)/shard_map/ppermute | solution.py:41
  382.6 34.4 %collective-permute-start.59 = (bf16[32,1536]{1,0:T(8,128)(2,1)S(1)}, bf16[32,1536]{1,0:T(8,128)(2,1)S(1)}, u32[]{:S(2)}, u32[]{:S(2)}) collective-permute-start(bf16[32,1536]{1,0:T(8,128)(2,1)S(1)} %add_convert_fusion.6), channel_id=1, source_target_pairs={{0,3},{1,2},{2,1},{3,0},{4,7},{5,6},{6,5},{7,4},{8,11},{9,10},{10,... | collective-permute-start | bytes 294920 | tf_op jit(solution)/shard_map/ppermute | solution.py:41
  411.0 103.3 %collective-permute-start.78 = (bf16[256,1536]{1,0:T(8,128)(2,1)}, bf16[256,1536]{1,0:T(8,128)(2,1)}, u32[]{:S(2)}, u32[]{:S(2)}) collective-permute-start(bf16[256,1536]{1,0:T(8,128)(2,1)} %fusion.77), channel_id=1, source_target_pairs={{0,1},{1,0},{2,3},{3,2},{4,5},{5,4},{6,7},{7,6},{8,9},{9,8},{10,11... | collective-permute-start | bytes 2359304 | tf_op jit(solution)/shard_map/ppermute | solution.py:41
  416.9 98.8 %collective-permute-start.79 = (bf16[256,1536]{1,0:T(8,128)(2,1)}, bf16[256,1536]{1,0:T(8,128)(2,1)}, u32[]{:S(2)}, u32[]{:S(2)}) collective-permute-start(bf16[256,1536]{1,0:T(8,128)(2,1)} %fusion.77), channel_id=1, source_target_pairs={{0,2},{1,3},{2,0},{3,1},{4,6},{5,7},{6,4},{7,5},{8,10},{9,11},{10,... | collective-permute-start | bytes 2359304 | tf_op jit(solution)/shard_map/ppermute | solution.py:41
  467.4 41.4 %collective-permute-start.61 = (bf16[256,1536]{1,0:T(8,128)(2,1)S(1)}, bf16[256,1536]{1,0:T(8,128)(2,1)S(1)}, u32[]{:S(2)}, u32[]{:S(2)}) collective-permute-start(bf16[256,1536]{1,0:T(8,128)(2,1)S(1)} %get-tuple-element.194), channel_id=1, source_target_pairs={{0,2},{1,3},{2,0},{3,1},{4,6},{5,7},{6,4},{7,5},{8,10},{9,11},{10,... | collective-permute-start | bytes 2359304 | tf_op jit(solution)/shard_map/ppermute | solution.py:41
  469.3 40.2 %collective-permute-start.62 = (bf16[256,1536]{1,0:T(8,128)(2,1)S(1)}, bf16[256,1536]{1,0:T(8,128)(2,1)S(1)}, u32[]{:S(2)}, u32[]{:S(2)}) collective-permute-start(bf16[256,1536]{1,0:T(8,128)(2,1)S(1)} %get-tuple-element.193), channel_id=1, source_target_pairs={{0,3},{1,2},{2,1},{3,0},{4,7},{5,6},{6,5},{7,4},{8,11},{9,10},{10,... | collective-permute-start | bytes 2359304 | tf_op jit(solution)/shard_map/ppermute | solution.py:41
  486.3 34.8 %collective-permute-start.80 = (bf16[256,1536]{1,0:T(8,128)(2,1)}, bf16[256,1536]{1,0:T(8,128)(2,1)S(1)}, u32[]{:S(2)}, u32[]{:S(2)}) collective-permute-start(bf16[256,1536]{1,0:T(8,128)(2,1)} %fusion.77), channel_id=1, source_target_pairs={{0,3},{1,2},{2,1},{3,0},{4,7},{5,6},{6,5},{7,4},{8,11},{9,10},{10,... | collective-permute-start | bytes 2359304 | tf_op jit(solution)/shard_map/ppermute | solution.py:41
  574.6 470.8 %reduce-scatter.9.cloned.1.call-start = ((), (), s32[]{:S(2)}) async-start(), calls=%async_computation.7 | async-start | bytes 10616832 | tf_op jit(solution)/shard_map/reduce_scatter | solution.py:390
  630.1 455.5 %reduce-scatter.11.cloned.1.call-start = ((), (), s32[]{:S(2)}) async-start(), calls=%async_computation.8 | async-start | bytes 10616832 | tf_op jit(solution)/shard_map/reduce_scatter | solution.py:390
  653.6 37.4 %collective-permute-start.85 = (bf16[256,1536]{1,0:T(8,128)(2,1)S(1)}, bf16[256,1536]{1,0:T(8,128)(2,1)S(1)}, u32[]{:S(2)}, u32[]{:S(2)}) collective-permute-start(bf16[256,1536]{1,0:T(8,128)(2,1)S(1)} %get-tuple-element.188), channel_id=1, source_target_pairs={{0,2},{1,3},{2,0},{3,1},{4,6},{5,7},{6,4},{7,5},{8,10},{9,11},{10,... | collective-permute-start | bytes 2359304 | tf_op jit(solution)/shard_map/ppermute | solution.py:41
  691.0 38.5 %collective-permute-start.67 = (bf16[256,1536]{1,0:T(8,128)(2,1)S(1)}, bf16[256,1536]{1,0:T(8,128)(2,1)S(1)}, u32[]{:S(2)}, u32[]{:S(2)}) collective-permute-start(bf16[256,1536]{1,0:T(8,128)(2,1)S(1)} %get-tuple-element.191), channel_id=1, source_target_pairs={{0,2},{1,3},{2,0},{3,1},{4,6},{5,7},{6,4},{7,5},{8,10},{9,11},{10,... | collective-permute-start | bytes 2359304 | tf_op jit(solution)/shard_map/ppermute | solution.py:41
  695.0 34.4 %collective-permute-start.68 = (bf16[256,1536]{1,0:T(8,128)(2,1)S(1)}, bf16[256,1536]{1,0:T(8,128)(2,1)S(1)}, u32[]{:S(2)}, u32[]{:S(2)}) collective-permute-start(bf16[256,1536]{1,0:T(8,128)(2,1)S(1)} %get-tuple-element.190), channel_id=1, source_target_pairs={{0,3},{1,2},{2,1},{3,0},{4,7},{5,6},{6,5},{7,4},{8,11},{9,10},{10,... | collective-permute-start | bytes 2359304 | tf_op jit(solution)/shard_map/ppermute | solution.py:41
  699.0 36.3 %collective-permute-start.93 = (bf16[32,1536]{1,0:T(8,128)(2,1)S(1)}, bf16[32,1536]{1,0:T(8,128)(2,1)S(1)}, u32[]{:S(2)}, u32[]{:S(2)}) collective-permute-start(bf16[32,1536]{1,0:T(8,128)(2,1)S(1)} %get-tuple-element.263), channel_id=1, source_target_pairs={{0,1},{1,0},{2,3},{3,2},{4,5},{5,4},{6,7},{7,6},{8,9},{9,8},{10,11... | collective-permute-start | bytes 294920 | tf_op jit(solution)/shard_map/ppermute | solution.py:41
  699.5 40.9 %collective-permute-start.94 = (bf16[32,1536]{1,0:T(8,128)(2,1)S(1)}, bf16[32,1536]{1,0:T(8,128)(2,1)S(1)}, u32[]{:S(2)}, u32[]{:S(2)}) collective-permute-start(bf16[32,1536]{1,0:T(8,128)(2,1)S(1)} %get-tuple-element.263), channel_id=1, source_target_pairs={{0,2},{1,3},{2,0},{3,1},{4,6},{5,7},{6,4},{7,5},{8,10},{9,11},{10,... | collective-permute-start | bytes 294920 | tf_op jit(solution)/shard_map/ppermute | solution.py:41
  817.1 451.7 %reduce-scatter.17.cloned.1.call-start = ((), (), s32[]{:S(2)}) async-start(), calls=%async_computation.11 | async-start | bytes 10616832 | tf_op jit(solution)/shard_map/reduce_scatter | solution.py:390
  824.8 43.7 %collective-permute-start.96 = (bf16[256,1536]{1,0:T(8,128)(2,1)S(1)}, bf16[256,1536]{1,0:T(8,128)(2,1)S(1)}, u32[]{:S(2)}, u32[]{:S(2)}) collective-permute-start(bf16[256,1536]{1,0:T(8,128)(2,1)S(1)} %get-tuple-element.183), channel_id=1, source_target_pairs={{0,1},{1,0},{2,3},{3,2},{4,5},{5,4},{6,7},{7,6},{8,9},{9,8},{10,11... | collective-permute-start | bytes 2359304 | tf_op jit(solution)/shard_map/ppermute | solution.py:41
  826.2 42.2 %collective-permute-start.97 = (bf16[256,1536]{1,0:T(8,128)(2,1)S(1)}, bf16[256,1536]{1,0:T(8,128)(2,1)S(1)}, u32[]{:S(2)}, u32[]{:S(2)}) collective-permute-start(bf16[256,1536]{1,0:T(8,128)(2,1)S(1)} %get-tuple-element.185), channel_id=1, source_target_pairs={{0,2},{1,3},{2,0},{3,1},{4,6},{5,7},{6,4},{7,5},{8,10},{9,11},{10,... | collective-permute-start | bytes 2359304 | tf_op jit(solution)/shard_map/ppermute | solution.py:41
  826.8 41.6 %collective-permute-start.98 = (bf16[256,1536]{1,0:T(8,128)(2,1)S(1)}, bf16[256,1536]{1,0:T(8,128)(2,1)S(1)}, u32[]{:S(2)}, u32[]{:S(2)}) collective-permute-start(bf16[256,1536]{1,0:T(8,128)(2,1)S(1)} %get-tuple-element.184), channel_id=1, source_target_pairs={{0,3},{1,2},{2,1},{3,0},{4,7},{5,6},{6,5},{7,4},{8,11},{9,10},{10,... | collective-permute-start | bytes 2359304 | tf_op jit(solution)/shard_map/ppermute | solution.py:41
  875.3 35.6 %collective-permute-start.102 = (bf16[256,1536]{1,0:T(8,128)(2,1)S(1)}, bf16[256,1536]{1,0:T(8,128)(2,1)S(1)}, u32[]{:S(2)}, u32[]{:S(2)}) collective-permute-start(bf16[256,1536]{1,0:T(8,128)(2,1)S(1)} %multiply_convert_fusion.4), channel_id=1, source_target_pairs={{0,1},{1,0},{2,3},{3,2},{4,5},{5,4},{6,7},{7,6},{8,9},{9,8},{10,11... | collective-permute-start | bytes 2359304 | tf_op jit(solution)/shard_map/ppermute | solution.py:41
  875.4 35.5 %collective-permute-start.103 = (bf16[256,1536]{1,0:T(8,128)(2,1)S(1)}, bf16[256,1536]{1,0:T(8,128)(2,1)S(1)}, u32[]{:S(2)}, u32[]{:S(2)}) collective-permute-start(bf16[256,1536]{1,0:T(8,128)(2,1)S(1)} %multiply_convert_fusion.4), channel_id=1, source_target_pairs={{0,2},{1,3},{2,0},{3,1},{4,6},{5,7},{6,4},{7,5},{8,10},{9,11},{10,... | collective-permute-start | bytes 2359304 | tf_op jit(solution)/shard_map/ppermute | solution.py:41
  876.1 34.8 %collective-permute-start.104 = (bf16[256,1536]{1,0:T(8,128)(2,1)S(1)}, bf16[256,1536]{1,0:T(8,128)(2,1)S(1)}, u32[]{:S(2)}, u32[]{:S(2)}) collective-permute-start(bf16[256,1536]{1,0:T(8,128)(2,1)S(1)} %multiply_convert_fusion.4), channel_id=1, source_target_pairs={{0,3},{1,2},{2,1},{3,0},{4,7},{5,6},{6,5},{7,4},{8,11},{9,10},{10,... | collective-permute-start | bytes 2359304 | tf_op jit(solution)/shard_map/ppermute | solution.py:41
  925.4 402.1 %reduce-scatter.15.cloned.1.call-start = ((), (), s32[]{:S(2)}) async-start(), calls=%async_computation.10 | async-start | bytes 10616832 | tf_op jit(solution)/shard_map/reduce_scatter | solution.py:390
  960.4 37.5 %collective-permute-start.136 = (f32[2,9216]{1,0:T(2,128)}, f32[2,9216]{1,0:T(2,128)}, u32[]{:S(2)}, u32[]{:S(2)}) collective-permute-start(f32[2,9216]{1,0:T(2,128)} %pad_maximum_fusion.23), channel_id=1, source_target_pairs={{0,1},{1,0},{2,3},{3,2},{4,5},{5,4},{6,7},{7,6},{8,9},{9,8},{10,11... | collective-permute-start | bytes 221192 | tf_op jit(solution)/shard_map/ppermute | solution.py:41
  961.4 36.6 %collective-permute-start.137 = (f32[2,9216]{1,0:T(2,128)}, f32[2,9216]{1,0:T(2,128)}, u32[]{:S(2)}, u32[]{:S(2)}) collective-permute-start(f32[2,9216]{1,0:T(2,128)} %pad_maximum_fusion.23), channel_id=1, source_target_pairs={{0,2},{1,3},{2,0},{3,1},{4,6},{5,7},{6,4},{7,5},{8,10},{9,11},{10,... | collective-permute-start | bytes 221192 | tf_op jit(solution)/shard_map/ppermute | solution.py:41
  961.4 36.6 %collective-permute-start.138 = (f32[2,9216]{1,0:T(2,128)}, f32[2,9216]{1,0:T(2,128)}, u32[]{:S(2)}, u32[]{:S(2)}) collective-permute-start(f32[2,9216]{1,0:T(2,128)} %pad_maximum_fusion.23), channel_id=1, source_target_pairs={{0,3},{1,2},{2,1},{3,0},{4,7},{5,6},{6,5},{7,4},{8,11},{9,10},{10,... | collective-permute-start | bytes 221192 | tf_op jit(solution)/shard_map/ppermute | solution.py:41
  997.0 334.6 %reduce-scatter.13.cloned.1.call-start = ((), (), s32[]{:S(2)}) async-start(), calls=%async_computation.9 | async-start | bytes 10616832 | tf_op jit(solution)/shard_map/reduce_scatter | solution.py:390
  1040.8 42.4 %collective-permute-start.108 = (bf16[256,1536]{1,0:T(8,128)(2,1)}, bf16[256,1536]{1,0:T(8,128)(2,1)}, u32[]{:S(2)}, u32[]{:S(2)}) collective-permute-start(bf16[256,1536]{1,0:T(8,128)(2,1)} %get-tuple-element.180), channel_id=1, source_target_pairs={{0,1},{1,0},{2,3},{3,2},{4,5},{5,4},{6,7},{7,6},{8,9},{9,8},{10,11... | collective-permute-start | bytes 2359304 | tf_op jit(solution)/shard_map/ppermute | solution.py:41
  1041.6 41.6 %collective-permute-start.109 = (bf16[256,1536]{1,0:T(8,128)(2,1)}, bf16[256,1536]{1,0:T(8,128)(2,1)}, u32[]{:S(2)}, u32[]{:S(2)}) collective-permute-start(bf16[256,1536]{1,0:T(8,128)(2,1)} %get-tuple-element.182), channel_id=1, source_target_pairs={{0,2},{1,3},{2,0},{3,1},{4,6},{5,7},{6,4},{7,5},{8,10},{9,11},{10,... | collective-permute-start | bytes 2359304 | tf_op jit(solution)/shard_map/ppermute | solution.py:41
  1043.4 39.8 %collective-permute-start.110 = (bf16[256,1536]{1,0:T(8,128)(2,1)}, bf16[256,1536]{1,0:T(8,128)(2,1)}, u32[]{:S(2)}, u32[]{:S(2)}) collective-permute-start(bf16[256,1536]{1,0:T(8,128)(2,1)} %get-tuple-element.181), channel_id=1, source_target_pairs={{0,3},{1,2},{2,1},{3,0},{4,7},{5,6},{6,5},{7,4},{8,11},{9,10},{10,... | collective-permute-start | bytes 2359304 | tf_op jit(solution)/shard_map/ppermute | solution.py:41
  1099.8 40.4 %collective-permute-start.114 = (bf16[256,1536]{1,0:T(8,128)(2,1)S(1)}, bf16[256,1536]{1,0:T(8,128)(2,1)S(1)}, u32[]{:S(2)}, u32[]{:S(2)}) collective-permute-start(bf16[256,1536]{1,0:T(8,128)(2,1)S(1)} %multiply_convert_fusion.3), channel_id=1, source_target_pairs={{0,1},{1,0},{2,3},{3,2},{4,5},{5,4},{6,7},{7,6},{8,9},{9,8},{10,11... | collective-permute-start | bytes 2359304 | tf_op jit(solution)/shard_map/ppermute | solution.py:41
  1101.1 39.0 %collective-permute-start.115 = (bf16[256,1536]{1,0:T(8,128)(2,1)S(1)}, bf16[256,1536]{1,0:T(8,128)(2,1)S(1)}, u32[]{:S(2)}, u32[]{:S(2)}) collective-permute-start(bf16[256,1536]{1,0:T(8,128)(2,1)S(1)} %multiply_convert_fusion.3), channel_id=1, source_target_pairs={{0,2},{1,3},{2,0},{3,1},{4,6},{5,7},{6,4},{7,5},{8,10},{9,11},{10,... | collective-permute-start | bytes 2359304 | tf_op jit(solution)/shard_map/ppermute | solution.py:41
  1102.6 37.5 %collective-permute-start.116 = (bf16[256,1536]{1,0:T(8,128)(2,1)S(1)}, bf16[256,1536]{1,0:T(8,128)(2,1)S(1)}, u32[]{:S(2)}, u32[]{:S(2)}) collective-permute-start(bf16[256,1536]{1,0:T(8,128)(2,1)S(1)} %multiply_convert_fusion.3), channel_id=1, source_target_pairs={{0,3},{1,2},{2,1},{3,0},{4,7},{5,6},{6,5},{7,4},{8,11},{9,10},{10,... | collective-permute-start | bytes 2359304 | tf_op jit(solution)/shard_map/ppermute | solution.py:41
  1104.5 34.4 %collective-permute-start.119 = (bf16[32,1536]{1,0:T(8,128)(2,1)S(1)}, bf16[32,1536]{1,0:T(8,128)(2,1)S(1)}, u32[]{:S(2)}, u32[]{:S(2)}) collective-permute-start(bf16[32,1536]{1,0:T(8,128)(2,1)S(1)} %multiply_convert_fusion.9), channel_id=1, source_target_pairs={{0,3},{1,2},{2,1},{3,0},{4,7},{5,6},{6,5},{7,4},{8,11},{9,10},{10,... | collective-permute-start | bytes 294920 | tf_op jit(solution)/shard_map/ppermute | solution.py:41
  1207.9 38.6 %collective-permute-start.120 = (bf16[256,1536]{1,0:T(8,128)(2,1)}, bf16[256,1536]{1,0:T(8,128)(2,1)}, u32[]{:S(2)}, u32[]{:S(2)}) collective-permute-start(bf16[256,1536]{1,0:T(8,128)(2,1)} %get-tuple-element.177), channel_id=1, source_target_pairs={{0,1},{1,0},{2,3},{3,2},{4,5},{5,4},{6,7},{7,6},{8,9},{9,8},{10,11... | collective-permute-start | bytes 2359304 | tf_op jit(solution)/shard_map/ppermute | solution.py:41
  1208.8 37.6 %collective-permute-start.121 = (bf16[256,1536]{1,0:T(8,128)(2,1)}, bf16[256,1536]{1,0:T(8,128)(2,1)}, u32[]{:S(2)}, u32[]{:S(2)}) collective-permute-start(bf16[256,1536]{1,0:T(8,128)(2,1)} %get-tuple-element.179), channel_id=1, source_target_pairs={{0,2},{1,3},{2,0},{3,1},{4,6},{5,7},{6,4},{7,5},{8,10},{9,11},{10,... | collective-permute-start | bytes 2359304 | tf_op jit(solution)/shard_map/ppermute | solution.py:41
  1210.3 36.2 %collective-permute-start.122 = (bf16[256,1536]{1,0:T(8,128)(2,1)}, bf16[256,1536]{1,0:T(8,128)(2,1)}, u32[]{:S(2)}, u32[]{:S(2)}) collective-permute-start(bf16[256,1536]{1,0:T(8,128)(2,1)} %get-tuple-element.178), channel_id=1, source_target_pairs={{0,3},{1,2},{2,1},{3,0},{4,7},{5,6},{6,5},{7,4},{8,11},{9,10},{10,... | collective-permute-start | bytes 2359304 | tf_op jit(solution)/shard_map/ppermute | solution.py:41
  (401 other events, 6465.5 us)
Sparse Core Ops, SparseCore 0:
  10.3 78.1 all-gather.16
  90.1 35.5 all-gather.18
  127.8 90.1 all-gather.20
  220.0 89.1 all-gather.22
  311.2 69.6 all-gather.24
  382.4 30.2 all-gather.26
  414.9 89.8 all-gather.28
  506.4 89.1 all-gather.30
  597.9 97.9 reduce-scatter.6
  698.1 97.8 reduce-scatter.8
  817.3 96.9 reduce-scatter.10
  925.5 105.7 reduce-scatter.16
  1033.6 100.0 reduce-scatter.14
  1196.7 121.4 reduce-scatter.12

commit v3 on v2

--- a/solution.py
+++ b/solution.py
@@ -49,15 +49,58 @@
     return jnp.concatenate(gather_parts(values, axis), axis=0)
 
 
-def scatter_rows(values, axis):
-    size = lax.axis_size(axis)
-    rows = values.shape[0] // size
-    total = values[:rows].astype(jnp.float32)
-    for step in range(1, size):
-        total = total + exchange(values[step * rows : (step + 1) * rows], axis, step).astype(
-            jnp.float32
-        )
-    return total
+def gather_streams(streams):
+    counts = [values.shape[0] for values in streams]
+    rows = jnp.concatenate(streams)
+    if lax.axis_size("tensor") == 4:
+        half = rows.shape[0] // 2
+        first, second = (exchange(rows, "tensor", step) for step in (1, 2))
+        far = jnp.concatenate(
+            [exchange(first[:half], "tensor", 2), exchange(second[half:], "tensor", 1)]
+        )
+        parts = [rows, first, second, far]
+    else:
+        parts = gather_parts(rows, "tensor")
+    return [
+        jnp.concatenate([part[: counts[0]] for part in parts]),
+        jnp.concatenate([part[counts[0] :] for part in parts]),
+    ]
+
+
+def scatter_streams(left, right):
+    size = lax.axis_size("tensor")
+    counts = [values.shape[0] // size for values in left]
+
+    def piece(step):
+        return jnp.concatenate(
+            [
+                lax.dot_general(
+                    left[stream][step * counts[stream] : (step + 1) * counts[stream]],
+                    right[stream],
+                    contract_columns,
+                    preferred_element_type=jnp.float32,
+                ).astype(jnp.bfloat16)
+                for stream in range(2)
+            ]
+        )
+
+    if size == 4:
+        half = sum(counts) // 2
+        far = lax.optimization_barrier(piece(3))
+        first_in = exchange(far[:half], "tensor", 1)
+        second_in = exchange(far[half:], "tensor", 2)
+        first, second = lax.optimization_barrier((piece(1), piece(2)))
+        first = jnp.concatenate([first[:half], first[half:] + second_in])
+        second = jnp.concatenate([second[:half] + first_in, second[half:]])
+        pieces = [exchange(first, "tensor", 1), exchange(second, "tensor", 2)]
+    else:
+        far = piece(size - 1)
+        pieces = [exchange(far, "tensor", size - 1)]
+        pieces += [exchange(piece(step), "tensor", step) for step in range(1, size - 1)]
+    total = piece(0).astype(jnp.float32)
+    for values in pieces:
+        total = total + values.astype(jnp.float32)
+    return [total[: counts[0]], total[counts[0] :]], far
 
 
 def sum_over(values, axis):
@@ -268,13 +311,12 @@
 
 def forward_layer(states, weights, pieces, shifts, heads_local):
     query_bias, value_bias, out_bias, hidden_bias, last_bias = pieces
-    joined = [
-        gather_rows(
-            modulate(states[stream], shifts[stream][0], shifts[stream][1]).astype(jnp.bfloat16),
-            "tensor",
-        )
-        for stream in range(2)
-    ]
+    joined = gather_streams(
+        [
+            modulate(states[stream], shifts[stream][0], shifts[stream][1]).astype(jnp.bfloat16)
+            for stream in range(2)
+        ]
+    )
     columns = jnp.concatenate(
         [
             (
@@ -287,46 +329,23 @@
     attended, logsum = attend(columns, heads_local)
     split = joined[0].shape[0]
     out_rows = [attended[:split], attended[split:]]
-    branch_attend = [
-        scatter_rows(
-            lax.dot_general(
-                out_rows[stream],
-                weights[1][stream],
-                contract_columns,
-                preferred_element_type=jnp.float32,
-            ).astype(jnp.bfloat16),
-            "tensor",
-        )
-        + out_bias[stream]
-        for stream in range(2)
-    ]
+    summed = scatter_streams(out_rows, weights[1])[0]
+    branch_attend = [summed[stream] + out_bias[stream] for stream in range(2)]
     middle = [states[stream] + shifts[stream][2] * branch_attend[stream] for stream in range(2)]
-    joined_feed = [
-        gather_rows(
-            modulate(middle[stream], shifts[stream][3], shifts[stream][4]).astype(jnp.bfloat16),
-            "tensor",
-        )
-        for stream in range(2)
-    ]
+    joined_feed = gather_streams(
+        [
+            modulate(middle[stream], shifts[stream][3], shifts[stream][4]).astype(jnp.bfloat16)
+            for stream in range(2)
+        ]
+    )
     preact = [
         jnp.dot(joined_feed[stream], weights[2][stream], preferred_element_type=jnp.float32)
         + hidden_bias[stream]
         for stream in range(2)
     ]
     activated = [gelu_tanh(preact[stream]).astype(jnp.bfloat16) for stream in range(2)]
-    branch_feed = [
-        scatter_rows(
-            lax.dot_general(
-                activated[stream],
-                weights[3][stream],
-                contract_columns,
-                preferred_element_type=jnp.float32,
-            ).astype(jnp.bfloat16),
-            "tensor",
-        )
-        + last_bias[stream]
-        for stream in range(2)
-    ]
+    summed = scatter_streams(activated, weights[3])[0]
+    branch_feed = [summed[stream] + last_bias[stream] for stream in range(2)]
     result = [middle[stream] + shifts[stream][5] * branch_feed[stream] for stream in range(2)]
     record = (
         states,
@@ -417,9 +436,7 @@
     out_rows = [attended[:split], attended[split:]]
     grad_branch = [shifts[stream][5] * gradients[stream] for stream in range(2)]
     gate_feed = [jnp.sum(gradients[stream] * branch_feed[stream], 0) for stream in range(2)]
-    branch_rows = [
-        gather_rows(grad_branch[stream].astype(jnp.bfloat16), "tensor") for stream in range(2)
-    ]
+    branch_rows = gather_streams([values.astype(jnp.bfloat16) for values in grad_branch])
     grad_contraction = weight_grads(
         [(branch_rows[stream], activated[stream], 0) for stream in range(2)]
     )
@@ -433,20 +450,10 @@
         gelu_back = jax.vjp(gelu_tanh, preact[stream])[1]
         grad_preact.append(gelu_back(grad_activated)[0].astype(jnp.bfloat16))
     hidden_sums = [jnp.sum(grad_preact[stream], 0, dtype=jnp.float32) for stream in range(2)]
-    summed = [
-        scatter_rows(
-            lax.dot_general(
-                grad_preact[stream],
-                weights[2][stream],
-                contract_columns,
-                preferred_element_type=jnp.float32,
-            ).astype(jnp.bfloat16),
-            "tensor",
-        )
-        for stream in range(2)
-    ]
+    summed, started = scatter_streams(grad_preact, weights[2])
+    behind = after(grad_preact, started)
     grad_expansion = weight_grads(
-        [(joined_feed[stream], grad_preact[stream], 0) for stream in range(2)]
+        [(joined_feed[stream], behind[stream], 0) for stream in range(2)]
     )
     summed = after(summed, grad_expansion)
     grad_expansion = scatter_weights(grad_expansion)
@@ -460,9 +467,7 @@
         scale_feed.append(back_scale)
     grad_attend = [shifts[stream][2] * grad_middle[stream] for stream in range(2)]
     gate_attend = [jnp.sum(grad_middle[stream] * branch_attend[stream], 0) for stream in range(2)]
-    attend_rows = [
-        gather_rows(grad_attend[stream].astype(jnp.bfloat16), "tensor") for stream in range(2)
-    ]
+    attend_rows = gather_streams([values.astype(jnp.bfloat16) for values in grad_attend])
     grad_heads = jnp.concatenate(
         [
             jnp.dot(
@@ -477,28 +482,27 @@
         jnp.sum(column_rows[stream], 0, dtype=jnp.float32).reshape(heads_local, 3, HEAD_DIM)
         for stream in range(2)
     ]
-    summed = [
-        scatter_rows(
-            lax.dot_general(
-                column_rows[stream],
-                weights[0][stream],
-                contract_columns,
-                preferred_element_type=jnp.float32,
-            ).astype(jnp.bfloat16),
-            "tensor",
-        )
-        for stream in range(2)
-    ]
     text_place = split // attend_rows[1].shape[0]
-    grad_attention = weight_grads(
-        [
-            (attend_rows[0], attended, 0),
-            (attend_rows[1], attended, text_place),
-            (joined[0], grad_columns, 0),
-            (joined[1], grad_columns, text_place),
-        ]
-    )
-    summed = after(summed, grad_attention)
+
+    def attention_grads(behind):
+        return weight_grads(
+            [
+                (attend_rows[0], attended, 0),
+                (attend_rows[1], attended, text_place),
+                (joined[0], behind, 0),
+                (joined[1], behind, text_place),
+            ]
+        )
+
+    if pending:
+        grad_attention = attention_grads(grad_columns)
+        column_rows = after(column_rows, grad_attention)
+        summed, _ = scatter_streams(column_rows, weights[0])
+    else:
+        summed, started = scatter_streams(column_rows, weights[0])
+        grad_attention = attention_grads(after(grad_columns, started))
+        summed = after(summed, grad_attention)
+    computed = grad_attention
     grad_attention = scatter_weights(grad_attention)
     tensor_rank = lax.axis_index("tensor")
     width_local = heads_local * HEAD_DIM
@@ -545,7 +549,14 @@
         unpack_weights(grad_contraction, 0, hidden_local),
     )
     pending = (grad_contraction, grad_expansion, grad_attention)
-    return (new_grads, layer_grads, pending, jnp.stack(bias_grads), jnp.stack(slot_grads))
+    return (
+        new_grads,
+        layer_grads,
+        pending,
+        computed,
+        jnp.stack(bias_grads),
+        jnp.stack(slot_grads),
+    )
 
 
 def slot_table(silu_rows, modulation, slots):
@@ -624,17 +635,20 @@
         owned_rows,
         precision=highest,
     )
-    weight_store, bias_store, modulation_store, pending = ([], [], [], ())
+    weight_store, bias_store, slot_store, modulation_store, pending = ([], [], [], [], ())
     for tier in reversed(range(LAYERS)):
         weights, shifts, record = stored[tier]
-        gradients, layer_grads, pending, bias_part, slot_grads = backward_layer(
+        gradients, layer_grads, pending, computed, bias_part, slot_grads = backward_layer(
             gradients, record, weights, shifts, heads_local, pending
         )
         weight_store.insert(0, layer_grads)
         bias_store.insert(0, bias_part)
+        slot_store.insert(0, slot_grads)
+    slot_store[1:], bias_store[1:] = after((slot_store[1:], bias_store[1:]), computed)
+    for slot_grads in slot_store:
         slot_sums = jnp.stack(gather_parts(sum_over(slot_grads, "tensor"), "dp"))
-        modulation_store.insert(
-            0, jnp.einsum("pd,psm->sdm", slot_rows, slot_sums, precision=highest)
+        modulation_store.append(
+            jnp.einsum("pd,psm->sdm", slot_rows, slot_sums, precision=highest)
         )
     stacked = [
         jnp.stack([entry[kind] for entry in weight_store]) for kind in range(4)

time: 1360 us -> 1260 us (0.926)
  waiting for transfers between devices: 523 us -> 428 us
  starting transfers between devices: 193 us -> 128 us
  matrix products: 180 us -> 228 us
  local copies, waits for them, and re-layouts: 102 us -> 117 us
    ppermute x156 -> x124, waiting for transfers between devices: 450 us -> 369 us  [exchange(): lax.ppermute(values, axis, [(rank, rank ^ step) for rank in range(size)])]
    ppermute x156 -> x124, starting transfers between devices: 191 us -> 127 us  [exchange(): lax.ppermute(values, axis, [(rank, rank ^ step) for rank in range(size)])]
    dot_general x16 -> x64, matrix products: 74.1 us -> 134 us  [piece(): lax.dot_general(left[stream][step * counts[stream]:(step + 1) * counts[st...]
    slice x17 -> x80, local copies, waits for them, and re-layouts: 6.28 us -> 36.5 us  [the longest x24 12.9 us: gather_streams(): part[counts[0]:]]
    all_gather x8, waiting for transfers between devices: 71.5 us -> 57.3 us  [on_device(): lax.all_gather(matrix[tier], 'dp', axis=1, tiled=True)]
    unnamed x636 -> x696, local copies, waits for them, and re-layouts: 34.2 us -> 20.6 us
    concatenate x16 -> x64, other arithmetic: 30.8 us -> 42.4 us  [the longest x8 25.7 us: gather_streams(): jnp.concatenate([part[:counts[0]] for part in parts])]
  transfers between devices with their start and end apart: 170 -> 138, of which waited for: 51 -> 65; matrix products, arithmetic and copies ran while one was open for 29% -> 35% of each run, Pallas kernels for 15% -> 16%
where the time goes in v3:
time: 1260 us; the launch traced here: 1250 us
  waiting for transfers between devices  428 us (34%)
  matrix products  228 us (18%)
  Pallas kernels  203 us (16%)
  starting transfers between devices  128 us (10%)
  other arithmetic  122 us (10%)
  local copies, waits for them, and re-layouts  117 us (9%)
  between operations  21.3 us (2%)
    ppermute x124, waiting for transfers between devices, exchange(): lax.ppermute(values, axis, [(rank, rank ^ step) for rank in range(size)])  369 us
    dot_general x64, matrix products, piece(): lax.dot_general(left[stream][step * counts[stream]:(step + 1) * counts[st...  134 us
    ppermute x124, starting transfers between devices, exchange(): lax.ppermute(values, axis, [(rank, rank ^ step) for rank in range(size)])  127 us
    pallas_call x6, Pallas kernels, weight_grads(): pl.pallas_call(functools.partial(weight_grads_kernel, len(pairs)), grid=(...  77.1 us
    pallas_call x2, Pallas kernels, attend_back(): pl.pallas_call(functools.partial(attend_back_kernel, heads, row_block(row...  67.2 us
    all_gather x8, waiting for transfers between devices, on_device(): lax.all_gather(matrix[tier], 'dp', axis=1, tiled=True)  57.3 us
    pallas_call x2, Pallas kernels, attend(): pl.pallas_call(functools.partial(attend_kernel, heads, row_block(rows)),...  55.3 us
    dot_general x4, matrix products, forward_layer(): jnp.dot(joined_feed[stream], weights[2][stream], preferred_element_type=j...  30.6 us
  transfers between devices with their start and end apart: 138, of which 65 were waited for; matrix products, arithmetic and copies ran while one was open for 35% of the time, Pallas kernels for 16%

profile of v3, /device:TPU:0, one launch (start us, length us, event | category | flops | bytes accessed | tf_op | source)
XLA Modules:
  0.0 1247.6 jit_solution(3742905142352866993)
XLA Ops:
  19.4 5.1 collective-permute-start.5
  58.2 4.5 concatenate.289
  65.7 5.1 collective-permute-done.24
  70.9 5.1 collective-permute-done.25
  76.0 7.8 collective-permute-done.26
  83.7 4.5 collective-permute-done.27
  122.9 17.4 %collective-permute-done.31 = bf16[288,1536]{1,0:T(8,128)(2,1)} collective-permute-done((bf16[288,1536]{1,0:T(8,128)(2,1)}, bf16[288,1536]{1,0:T(8,128)(2,1)}, u32[]{:S(2)}, u32[]{:S(2)}) %collective-permute-start.31) | collective-permute-done | bytes 884768 | tf_op jit(solution)/shard_map/ppermute | solution.py:41
  152.9 6.8 fusion.37.refs_4_
  159.7 7.3 add_convert_fusion.1
  169.5 27.7 %attend.2 = (bf16[1152,384]{1,0:T(8,128)(2,1)}, f32[1152,128]{1,0:T(8,128)}) custom-call(bf16[1152,1152]{1,0:T(8,128)(2,1)} %pad_maximum_fusion.9.columns_ref), custom_call_target="tpu_custom_call" | custom-call | flops 2038431744 | bytes 3981312 | tf_op jit(solution)/shard_map/attend/pallas_call | solution.py:206
  206.6 4.6 collective-permute-done.36
  220.6 8.7 collective-permute-done.37
  236.8 14.4 %collective-permute-done.39 = bf16[288,1536]{1,0:T(8,128)(2,1)S(1)} collective-permute-done((bf16[288,1536]{1,0:T(8,128)(2,1)S(1)}, bf16[288,1536]{1,0:T(8,128)(2,1)S(1)}, u32[]{:S(2)}, u32[]{:S(2)}) %collective-permute-start.39) | collective-permute-done | bytes 884768 | tf_op jit(solution)/shard_map/ppermute | solution.py:41
  264.5 6.6 fusion.36.refs_0_
  271.1 4.4 multiply_convert_fusion.7
  275.5 29.7 %all-gather.23.cloned.1.call-done = bf16[1,2,1536,1536]{3,2,1,0:T(8,128)(2,1)} async-done(((bf16[1,2,192,1536]{3,2,1,0:T(8,128)(2,1)}), bf16[1,2,1536,1536]{3,2,1,0:T(8,128)(2,1)}) %all-gather.23.cloned.1.call-update) | async-done | bytes 9437200 | tf_op jit(solution)/shard_map/all_gather | solution.py:617
  309.3 10.7 multiply_convert_fusion.1
  330.4 4.6 collective-permute-done.44
  340.5 15.6 %collective-permute-done.45 = bf16[288,1536]{1,0:T(8,128)(2,1)S(1)} collective-permute-done((bf16[288,1536]{1,0:T(8,128)(2,1)S(1)}, bf16[288,1536]{1,0:T(8,128)(2,1)S(1)}, u32[]{:S(2)}, u32[]{:S(2)}) %collective-permute-start.45) | collective-permute-done | bytes 884768 | tf_op jit(solution)/shard_map/ppermute | solution.py:41
  365.5 14.9 %collective-permute-done.47 = bf16[288,1536]{1,0:T(8,128)(2,1)} collective-permute-done((bf16[288,1536]{1,0:T(8,128)(2,1)}, bf16[288,1536]{1,0:T(8,128)(2,1)}, u32[]{:S(2)}, u32[]{:S(2)}) %collective-permute-start.47) | collective-permute-done | bytes 884768 | tf_op jit(solution)/shard_map/ppermute | solution.py:41
  399.0 6.3 fusion.35.refs_4_
  407.2 4.5 add_convert_fusion
  413.4 27.6 %attend.3 = (bf16[1152,384]{1,0:T(8,128)(2,1)}, f32[1152,128]{1,0:T(8,128)}) custom-call(bf16[1152,1152]{1,0:T(8,128)(2,1)} %pad_maximum_fusion.10.columns_ref), custom_call_target="tpu_custom_call" | custom-call | flops 2038431744 | bytes 3981312 | tf_op jit(solution)/shard_map/attend/pallas_call | solution.py:206
  448.6 6.1 collective-permute-done.52
  460.4 17.0 %collective-permute-done.53 = bf16[288,1536]{1,0:T(8,128)(2,1)S(1)} collective-permute-done((bf16[288,1536]{1,0:T(8,128)(2,1)S(1)}, bf16[288,1536]{1,0:T(8,128)(2,1)S(1)}, u32[]{:S(2)}, u32[]{:S(2)}) %collective-permute-start.53) | collective-permute-done | bytes 884768 | tf_op jit(solution)/shard_map/ppermute | solution.py:41
  483.0 13.5 %collective-permute-done.63 = bf16[288,1536]{1,0:T(8,128)(2,1)S(1)} collective-permute-done((bf16[288,1536]{1,0:T(8,128)(2,1)S(1)}, bf16[288,1536]{1,0:T(8,128)(2,1)S(1)}, u32[]{:S(2)}, u32[]{:S(2)}) %collective-permute-start.63) | collective-permute-done | bytes 884768 | tf_op jit(solution)/shard_map/ppermute | solution.py:41
  500.9 22.1 %collective-permute-done.65 = bf16[144,1536]{1,0:T(8,128)(2,1)S(1)} collective-permute-done((bf16[144,1536]{1,0:T(8,128)(2,1)S(1)}, bf16[144,1536]{1,0:T(8,128)(2,1)S(1)}, u32[]{:S(2)}, u32[]{:S(2)}) %collective-permute-start.65) | collective-permute-done | bytes 442400 | tf_op jit(solution)/shard_map/ppermute | solution.py:41
  527.5 4.6 collective-permute-done.57
  534.6 4.6 multiply_convert_fusion.6
  539.2 10.9 multiply_convert_fusion
  550.1 12.5 %weight_grads.6 = bf16[1536,3072]{1,0:T(8,128)(2,1)} custom-call(bf16[1024,1536]{1,0:T(8,128)(2,1)} %fusion.33.refs_0_, bf16[1024,1536]{1,0:T(8,128)(2,1)} %get-tuple-element.377.refs_1_, bf16[128,1536]{1,0:T(8,128)(2,1)} %pad_maximum_fusion.65.refs_2_, bf16[128,1536]{1,0:T(8,128)(2,1)} %get-tuple-element.379.refs_3_), custom_call_target="tpu_custom_call" | custom-call | flops 5435817984 | bytes 16515072 | tf_op jit(solution)/shard_map/weight_grads/pallas_call | solution.py:395
  562.9 27.6 %all-gather.31.cloned.1.call-done = bf16[1,2,1536,1536]{3,2,1,0:T(8,128)(2,1)} async-done(((bf16[1,2,192,1536]{3,2,1,0:T(8,128)(2,1)}), bf16[1,2,1536,1536]{3,2,1,0:T(8,128)(2,1)}) %all-gather.31.cloned.1.call-update) | async-done | bytes 9437200 | tf_op jit(solution)/shard_map/all_gather | solution.py:617
  590.5 4.0 fusion.89
  594.5 4.7 fusion.57
  603.2 11.3 convert_reduce_fusion.1
  617.9 12.5 %weight_grads.7 = bf16[1536,3072]{1,0:T(8,128)(2,1)} custom-call(bf16[1024,1536]{1,0:T(8,128)(2,1)} %fusion.34.refs_0_, bf16[1024,1536]{1,0:T(8,128)(2,1)} %copy-done.300, bf16[128,1536]{1,0:T(8,128)(2,1)} %pad_maximum_fusion.64.refs_2_, bf16[128,1536]{1,0:T(8,128)(2,1)} %copy-done.294), custom_call_target="tpu_custom_call" | custom-call | flops 5435817984 | bytes 16515072 | tf_op jit(solution)/shard_map/weight_grads/pallas_call | solution.py:395
  664.7 4.9 collective-permute-done.68
  674.4 17.9 %collective-permute-done.69 = bf16[288,1536]{1,0:T(8,128)(2,1)S(1)} collective-permute-done((bf16[288,1536]{1,0:T(8,128)(2,1)S(1)}, bf16[288,1536]{1,0:T(8,128)(2,1)S(1)}, u32[]{:S(2)}, u32[]{:S(2)}) %collective-permute-start.69) | collective-permute-done | bytes 884768 | tf_op jit(solution)/shard_map/ppermute | solution.py:41
  697.5 11.3 collective-permute-done.61
  716.1 17.9 %collective-permute-done.71 = bf16[288,1536]{1,0:T(8,128)(2,1)S(1)} collective-permute-done((bf16[288,1536]{1,0:T(8,128)(2,1)S(1)}, bf16[288,1536]{1,0:T(8,128)(2,1)S(1)}, u32[]{:S(2)}, u32[]{:S(2)}) %collective-permute-start.71) | collective-permute-done | bytes 884768 | tf_op jit(solution)/shard_map/ppermute | solution.py:41
  738.1 5.3 collective-permute-done.73
  747.9 33.6 %attend_back.2.refs_5_.refs_7_ = bf16[1152,1152]{1,0:T(8,128)(2,1)} custom-call(bf16[1152,1152]{1,0:T(8,128)(2,1)} %pad_maximum_fusion.10.columns_ref, bf16[1152,384]{1,0:T(8,128)(2,1)} %get-tuple-element.60.out_ref.refs_1_.refs_3_, f32[1152,128]{1,0:T(8,128)} %get-tuple-element.75.log_ref, bf16[1152,384]{1,0:T(8,128)(2,1)} %pad_maximum_fusion.42.grad_ref), custom_call_target="tpu_custom_call" | custom-call | flops 5096079360 | bytes 7962624 | tf_op jit(solution)/shard_map/attend_back/pallas_call | solution.py:275
  789.0 13.4 %weight_grads.8 = bf16[1536,3072]{1,0:T(8,128)(2,1)} custom-call(bf16[1024,1536]{1,0:T(8,128)(2,1)} %copy-done.25, bf16[1152,384]{1,0:T(8,128)(2,1)} %get-tuple-element.60.out_ref.refs_1_.refs_3_, bf16[128,1536]{1,0:T(8,128)(2,1)} %pad_maximum_fusion.66.refs_2_, bf16[1152,384]{1,0:T(8,128)(2,1)} %get-tuple-element.60.out_ref.refs_1_.refs_3_, ...), custom_call_target="tpu_custom_call" | custom-call | flops 5435817984 | bytes 20054016 | tf_op jit(solution)/shard_map/weight_grads/pallas_call | solution.py:395
  818.0 10.9 collective-permute-done.74
  832.2 12.2 collective-permute-done.77
  853.9 16.8 %collective-permute-done.79 = bf16[288,1536]{1,0:T(8,128)(2,1)S(1)} collective-permute-done((bf16[288,1536]{1,0:T(8,128)(2,1)S(1)}, bf16[288,1536]{1,0:T(8,128)(2,1)S(1)}, u32[]{:S(2)}, u32[]{:S(2)}) %collective-permute-start.79) | collective-permute-done | bytes 884768 | tf_op jit(solution)/shard_map/ppermute | solution.py:41
  874.6 6.9 collective-permute-done.81
  884.7 12.5 %weight_grads.9 = bf16[1536,3072]{1,0:T(8,128)(2,1)} custom-call(bf16[1024,1536]{1,0:T(8,128)(2,1)} %fusion.31.refs_0_, bf16[1024,1536]{1,0:T(8,128)(2,1)} %copy-done.296, bf16[128,1536]{1,0:T(8,128)(2,1)} %pad_maximum_fusion.67.refs_2_, bf16[128,1536]{1,0:T(8,128)(2,1)} %copy-done.289), custom_call_target="tpu_custom_call" | custom-call | flops 5435817984 | bytes 16515072 | tf_op jit(solution)/shard_map/weight_grads/pallas_call | solution.py:395
  910.8 4.5 convert_reduce_fusion.5
  915.4 4.0 fusion.85
  919.4 11.9 convert_reduce_fusion
  933.1 12.6 %weight_grads.10 = bf16[1536,3072]{1,0:T(8,128)(2,1)} custom-call(bf16[1024,1536]{1,0:T(8,128)(2,1)} %fusion.36.refs_0_, bf16[1024,1536]{1,0:T(8,128)(2,1)} %copy-done.298, bf16[128,1536]{1,0:T(8,128)(2,1)} %pad_maximum_fusion.62.refs_2_, bf16[128,1536]{1,0:T(8,128)(2,1)} %copy-done.291), custom_call_target="tpu_custom_call" | custom-call | flops 5435817984 | bytes 16515072 | tf_op jit(solution)/shard_map/weight_grads/pallas_call | solution.py:395
  948.0 4.6 fusion.84
  964.3 7.6 collective-permute-done.84
  982.3 8.5 collective-permute-done.85
  1009.6 11.0 collective-permute-done.87
  1021.9 5.6 collective-permute-done.86
  1040.0 33.6 %attend_back.3.refs_5_.refs_7_ = bf16[1152,1152]{1,0:T(8,128)(2,1)} custom-call(bf16[1152,1152]{1,0:T(8,128)(2,1)} %pad_maximum_fusion.9.columns_ref, bf16[1152,384]{1,0:T(8,128)(2,1)} %get-tuple-element.55.out_ref.refs_1_.refs_3_, f32[1152,128]{1,0:T(8,128)} %get-tuple-element.92.log_ref, bf16[1152,384]{1,0:T(8,128)(2,1)} %pad_maximum_fusion.55.grad_ref), custom_call_target="tpu_custom_call" | custom-call | flops 5096079360 | bytes 7962624 | tf_op jit(solution)/shard_map/attend_back/pallas_call | solution.py:275
  1078.8 13.6 %weight_grads.11 = bf16[1536,3072]{1,0:T(8,128)(2,1)} custom-call(bf16[1024,1536]{1,0:T(8,128)(2,1)} %copy-done.26, bf16[1152,384]{1,0:T(8,128)(2,1)} %get-tuple-element.55.out_ref.refs_1_.refs_3_, bf16[128,1536]{1,0:T(8,128)(2,1)} %pad_maximum_fusion.68.refs_2_, bf16[1152,384]{1,0:T(8,128)(2,1)} %get-tuple-element.55.out_ref.refs_1_.refs_3_, ...), custom_call_target="tpu_custom_call" | custom-call | flops 5435817984 | bytes 20054016 | tf_op jit(solution)/shard_map/weight_grads/pallas_call | solution.py:395
  1131.6 7.9 collective-permute-done.111
  1151.9 4.7 convolution_bitcast_fusion
  1206.3 6.3 collective-permute-done.101
  1215.2 5.5 collective-permute-done.100
  1223.3 4.2 convolution_bitcast_fusion.1
  (1444 shorter events, 521.5 us)
Async XLA Ops:
  7.2 152.5 %all-gather.17.cloned.1.call-start = ((), (), s32[]{:S(2)}) async-start(), calls=%async_computation.12 | async-start | bytes 7962624 | tf_op jit(solution)/shard_map/all_gather | solution.py:617
  10.2 187.0 %all-gather.19.cloned.1.call-start = ((), (), s32[]{:S(2)}) async-start(), calls=%async_computation.13 | async-start | bytes 2654208 | tf_op jit(solution)/shard_map/all_gather | solution.py:617
  12.2 258.9 %all-gather.21.cloned.1.call-start = ((), (), s32[]{:S(2)}) async-start(), calls=%async_computation.14 | async-start | bytes 10616832 | tf_op jit(solution)/shard_map/all_gather | solution.py:617
  15.5 289.8 %all-gather.23.cloned.1.call-start = ((), (), s32[]{:S(2)}) async-start(), calls=%async_computation.15 | async-start | bytes 10616832 | tf_op jit(solution)/shard_map/all_gather | solution.py:617
  18.7 377.2 %all-gather.25.cloned.1.call-start = ((), (), s32[]{:S(2)}) async-start(), calls=%async_computation.16 | async-start | bytes 7962624 | tf_op jit(solution)/shard_map/all_gather | solution.py:617
  19.3 421.7 %all-gather.27.cloned.1.call-start = ((), (), s32[]{:S(2)}) async-start(), calls=%async_computation.17 | async-start | bytes 2654208 | tf_op jit(solution)/shard_map/all_gather | solution.py:617
  19.4 21.4 %collective-permute-start.5 = (s32[1]{0:T(128)}, s32[1]{0:T(128)}, u32[]{:S(2)}, u32[]{:S(2)}) collective-permute-start(s32[1]{0:T(128)} %param.16), channel_id=1, source_target_pairs={{0,24},{4,28},{8,16},{12,20},{16,8},{20,12},{24,0},{28,4},{1,25},{... | collective-permute-start | bytes 20 | tf_op jit(solution)/shard_map/ppermute | solution.py:41
  24.5 18.3 %collective-permute-start.4 = (s32[1]{0:T(128)}, s32[1]{0:T(128)}, u32[]{:S(2)}, u32[]{:S(2)}) collective-permute-start(s32[1]{0:T(128)} %param.16), channel_id=1, source_target_pairs={{0,20},{4,16},{8,28},{12,24},{16,4},{20,0},{24,12},{28,8},{1,21},{... | collective-permute-start | bytes 20 | tf_op jit(solution)/shard_map/ppermute | solution.py:41
  24.5 38.2 %collective-permute-start.22 = (bf16[1,4,672]{2,1,0:T(4,128)(2,1)S(1)}, bf16[1,4,672]{2,1,0:T(4,128)(2,1)}, u32[]{:S(2)}, u32[]{:S(2)}) collective-permute-start(bf16[1,4,672]{2,1,0:T(4,128)(2,1)S(1)} %reshape.415), channel_id=1, source_target_pairs={{0,3},{1,2},{2,1},{3,0},{4,7},{5,6},{6,5},{7,4},{8,11},{9,10},{10,... | collective-permute-start | bytes 16136 | tf_op jit(solution)/shard_map/ppermute | solution.py:41
  27.0 35.8 %collective-permute-start.21 = (bf16[1,4,672]{2,1,0:T(4,128)(2,1)S(1)}, bf16[1,4,672]{2,1,0:T(4,128)(2,1)}, u32[]{:S(2)}, u32[]{:S(2)}) collective-permute-start(bf16[1,4,672]{2,1,0:T(4,128)(2,1)S(1)} %reshape.415), channel_id=1, source_target_pairs={{0,2},{1,3},{2,0},{3,1},{4,6},{5,7},{6,4},{7,5},{8,10},{9,11},{10,... | collective-permute-start | bytes 16136 | tf_op jit(solution)/shard_map/ppermute | solution.py:41
  27.5 35.3 %collective-permute-start.20 = (bf16[1,4,672]{2,1,0:T(4,128)(2,1)S(1)}, bf16[1,4,672]{2,1,0:T(4,128)(2,1)}, u32[]{:S(2)}, u32[]{:S(2)}) collective-permute-start(bf16[1,4,672]{2,1,0:T(4,128)(2,1)S(1)} %reshape.415), channel_id=1, source_target_pairs={{0,1},{1,0},{2,3},{3,2},{4,5},{5,4},{6,7},{7,6},{8,9},{9,8},{10,11... | collective-permute-start | bytes 16136 | tf_op jit(solution)/shard_map/ppermute | solution.py:41
  50.3 39.6 %collective-permute-start.7 = (f32[6,9216]{1,0:T(8,128)S(1)}, f32[6,9216]{1,0:T(8,128)S(1)}, u32[]{:S(2)}, u32[]{:S(2)}) collective-permute-start(f32[6,9216]{1,0:T(8,128)S(1)} %get-tuple-element.247), channel_id=1, source_target_pairs={{0,1},{1,0},{2,3},{3,2},{4,5},{5,4},{6,7},{7,6},{8,9},{9,8},{10,11... | collective-permute-start | bytes 663560 | tf_op jit(solution)/shard_map/ppermute | solution.py:41
  54.5 35.4 %collective-permute-start.9 = (f32[6,9216]{1,0:T(8,128)S(1)}, f32[6,9216]{1,0:T(8,128)S(1)}, u32[]{:S(2)}, u32[]{:S(2)}) collective-permute-start(f32[6,9216]{1,0:T(8,128)S(1)} %get-tuple-element.248), channel_id=1, source_target_pairs={{0,3},{1,2},{2,1},{3,0},{4,7},{5,6},{6,5},{7,4},{8,11},{9,10},{10,... | collective-permute-start | bytes 663560 | tf_op jit(solution)/shard_map/ppermute | solution.py:41
  62.7 27.2 %collective-permute-start.8 = (f32[6,9216]{1,0:T(8,128)S(1)}, f32[6,9216]{1,0:T(8,128)S(1)}, u32[]{:S(2)}, u32[]{:S(2)}) collective-permute-start(f32[6,9216]{1,0:T(8,128)S(1)} %get-tuple-element.249), channel_id=1, source_target_pairs={{0,2},{1,3},{2,0},{3,1},{4,6},{5,7},{6,4},{7,5},{8,10},{9,11},{10,... | collective-permute-start | bytes 663560 | tf_op jit(solution)/shard_map/ppermute | solution.py:41
  63.6 32.2 %collective-permute-start.29 = (bf16[1,4,4,672]{3,2,1,0:T(4,128)(2,1)S(1)}, bf16[1,4,4,672]{3,2,1,0:T(4,128)(2,1)S(1)}, u32[]{:S(2)}, u32[]{:S(2)}) collective-permute-start(bf16[1,4,4,672]{3,2,1,0:T(4,128)(2,1)S(1)} %maximum_bitcast_fusion.9), channel_id=1, source_target_pairs={{0,28},{4,24},{8,20},{12,16},{16,12},{20,8},{24,4},{28,0},{1,29},{... | collective-permute-start | bytes 64520 | tf_op jit(solution)/shard_map/ppermute | solution.py:41
  120.1 20.1 %collective-permute-start.31 = (bf16[288,1536]{1,0:T(8,128)(2,1)}, bf16[288,1536]{1,0:T(8,128)(2,1)}, u32[]{:S(2)}, u32[]{:S(2)}) collective-permute-start(bf16[288,1536]{1,0:T(8,128)(2,1)} %pad_maximum_fusion.11), channel_id=1, source_target_pairs={{0,2},{1,3},{2,0},{3,1},{4,6},{5,7},{6,4},{7,5},{8,10},{9,11},{10,... | collective-permute-start | bytes 2654216 | tf_op jit(solution)/shard_map/ppermute | solution.py:41
  122.1 20.5 %collective-permute-start.30 = (bf16[288,1536]{1,0:T(8,128)(2,1)}, bf16[288,1536]{1,0:T(8,128)(2,1)S(1)}, u32[]{:S(2)}, u32[]{:S(2)}) collective-permute-start(bf16[288,1536]{1,0:T(8,128)(2,1)} %pad_maximum_fusion.11), channel_id=1, source_target_pairs={{0,1},{1,0},{2,3},{3,2},{4,5},{5,4},{6,7},{7,6},{8,9},{9,8},{10,11... | collective-permute-start | bytes 2654216 | tf_op jit(solution)/shard_map/ppermute | solution.py:41
  122.2 412.3 %all-gather.29.cloned.1.call-start = ((), (), s32[]{:S(2)}) async-start(), calls=%async_computation.18 | async-start | bytes 10616832 | tf_op jit(solution)/shard_map/all_gather | solution.py:617
  212.3 17.0 %collective-permute-start.37 = (bf16[288,1536]{1,0:T(8,128)(2,1)}, bf16[288,1536]{1,0:T(8,128)(2,1)}, u32[]{:S(2)}, u32[]{:S(2)}) collective-permute-start(bf16[288,1536]{1,0:T(8,128)(2,1)} %pad_maximum_fusion.16), channel_id=1, source_target_pairs={{0,2},{1,3},{2,0},{3,1},{4,6},{5,7},{6,4},{7,5},{8,10},{9,11},{10,... | collective-permute-start | bytes 2654216 | tf_op jit(solution)/shard_map/ppermute | solution.py:41
  213.8 16.9 %collective-permute-start.35 = (bf16[288,1536]{1,0:T(8,128)(2,1)}, bf16[288,1536]{1,0:T(8,128)(2,1)}, u32[]{:S(2)}, u32[]{:S(2)}) collective-permute-start(bf16[288,1536]{1,0:T(8,128)(2,1)} %pad_maximum_fusion.15), channel_id=1, source_target_pairs={{0,1},{1,0},{2,3},{3,2},{4,5},{5,4},{6,7},{7,6},{8,9},{9,8},{10,11... | collective-permute-start | bytes 2654216 | tf_op jit(solution)/shard_map/ppermute | solution.py:41
  215.3 375.1 %all-gather.31.cloned.1.call-start = ((), (), s32[]{:S(2)}) async-start(), calls=%async_computation.19 | async-start | bytes 10616832 | tf_op jit(solution)/shard_map/all_gather | solution.py:617
  234.3 16.9 %collective-permute-start.39 = (bf16[288,1536]{1,0:T(8,128)(2,1)S(1)}, bf16[288,1536]{1,0:T(8,128)(2,1)S(1)}, u32[]{:S(2)}, u32[]{:S(2)}) collective-permute-start(bf16[288,1536]{1,0:T(8,128)(2,1)S(1)} %pad_maximum_fusion.17), channel_id=1, source_target_pairs={{0,2},{1,3},{2,0},{3,1},{4,6},{5,7},{6,4},{7,5},{8,10},{9,11},{10,... | collective-permute-start | bytes 2654216 | tf_op jit(solution)/shard_map/ppermute | solution.py:41
  235.8 19.2 %collective-permute-start.38 = (bf16[288,1536]{1,0:T(8,128)(2,1)S(1)}, bf16[288,1536]{1,0:T(8,128)(2,1)S(1)}, u32[]{:S(2)}, u32[]{:S(2)}) collective-permute-start(bf16[288,1536]{1,0:T(8,128)(2,1)S(1)} %pad_maximum_fusion.17), channel_id=1, source_target_pairs={{0,1},{1,0},{2,3},{3,2},{4,5},{5,4},{6,7},{7,6},{8,9},{9,8},{10,11... | collective-permute-start | bytes 2654216 | tf_op jit(solution)/shard_map/ppermute | solution.py:41
  335.2 20.8 %collective-permute-start.45 = (bf16[288,1536]{1,0:T(8,128)(2,1)S(1)}, bf16[288,1536]{1,0:T(8,128)(2,1)S(1)}, u32[]{:S(2)}, u32[]{:S(2)}) collective-permute-start(bf16[288,1536]{1,0:T(8,128)(2,1)S(1)} %pad_maximum_fusion.22), channel_id=1, source_target_pairs={{0,2},{1,3},{2,0},{3,1},{4,6},{5,7},{6,4},{7,5},{8,10},{9,11},{10,... | collective-permute-start | bytes 2654216 | tf_op jit(solution)/shard_map/ppermute | solution.py:41
  336.0 20.5 %collective-permute-start.43 = (bf16[288,1536]{1,0:T(8,128)(2,1)S(1)}, bf16[288,1536]{1,0:T(8,128)(2,1)S(1)}, u32[]{:S(2)}, u32[]{:S(2)}) collective-permute-start(bf16[288,1536]{1,0:T(8,128)(2,1)S(1)} %pad_maximum_fusion.21), channel_id=1, source_target_pairs={{0,1},{1,0},{2,3},{3,2},{4,5},{5,4},{6,7},{7,6},{8,9},{9,8},{10,11... | collective-permute-start | bytes 2654216 | tf_op jit(solution)/shard_map/ppermute | solution.py:41
  360.5 20.0 %collective-permute-start.47 = (bf16[288,1536]{1,0:T(8,128)(2,1)}, bf16[288,1536]{1,0:T(8,128)(2,1)}, u32[]{:S(2)}, u32[]{:S(2)}) collective-permute-start(bf16[288,1536]{1,0:T(8,128)(2,1)} %pad_maximum_fusion.23), channel_id=1, source_target_pairs={{0,2},{1,3},{2,0},{3,1},{4,6},{5,7},{6,4},{7,5},{8,10},{9,11},{10,... | collective-permute-start | bytes 2654216 | tf_op jit(solution)/shard_map/ppermute | solution.py:41
  362.0 21.1 %collective-permute-start.46 = (bf16[288,1536]{1,0:T(8,128)(2,1)}, bf16[288,1536]{1,0:T(8,128)(2,1)}, u32[]{:S(2)}, u32[]{:S(2)}) collective-permute-start(bf16[288,1536]{1,0:T(8,128)(2,1)} %pad_maximum_fusion.23), channel_id=1, source_target_pairs={{0,1},{1,0},{2,3},{3,2},{4,5},{5,4},{6,7},{7,6},{8,9},{9,8},{10,11... | collective-permute-start | bytes 2654216 | tf_op jit(solution)/shard_map/ppermute | solution.py:41
  363.5 547.3 %reduce-scatter.7.cloned.1.call-start = ((), (), s32[]{:S(2)}) async-start(), calls=%async_computation.6 | async-start | bytes 10616832 | tf_op jit(solution)/shard_map/reduce_scatter | solution.py:409
  454.8 22.7 %collective-permute-start.53 = (bf16[288,1536]{1,0:T(8,128)(2,1)S(1)}, bf16[288,1536]{1,0:T(8,128)(2,1)S(1)}, u32[]{:S(2)}, u32[]{:S(2)}) collective-permute-start(bf16[288,1536]{1,0:T(8,128)(2,1)S(1)} %pad_maximum_fusion.28), channel_id=1, source_target_pairs={{0,2},{1,3},{2,0},{3,1},{4,6},{5,7},{6,4},{7,5},{8,10},{9,11},{10,... | collective-permute-start | bytes 2654216 | tf_op jit(solution)/shard_map/ppermute | solution.py:41
  456.7 22.7 %collective-permute-start.51 = (bf16[288,1536]{1,0:T(8,128)(2,1)S(1)}, bf16[288,1536]{1,0:T(8,128)(2,1)S(1)}, u32[]{:S(2)}, u32[]{:S(2)}) collective-permute-start(bf16[288,1536]{1,0:T(8,128)(2,1)S(1)} %pad_maximum_fusion.27), channel_id=1, source_target_pairs={{0,1},{1,0},{2,3},{3,2},{4,5},{5,4},{6,7},{7,6},{8,9},{9,8},{10,11... | collective-permute-start | bytes 2654216 | tf_op jit(solution)/shard_map/ppermute | solution.py:41
  457.9 38.6 %collective-permute-start.63 = (bf16[288,1536]{1,0:T(8,128)(2,1)S(1)}, bf16[288,1536]{1,0:T(8,128)(2,1)S(1)}, u32[]{:S(2)}, u32[]{:S(2)}) collective-permute-start(bf16[288,1536]{1,0:T(8,128)(2,1)S(1)} %pad_maximum_fusion.35), channel_id=1, source_target_pairs={{0,2},{1,3},{2,0},{3,1},{4,6},{5,7},{6,4},{7,5},{8,10},{9,11},{10,... | collective-permute-start | bytes 2654216 | tf_op jit(solution)/shard_map/ppermute | solution.py:41
  458.0 40.3 %collective-permute-start.62 = (bf16[288,1536]{1,0:T(8,128)(2,1)S(1)}, bf16[288,1536]{1,0:T(8,128)(2,1)S(1)}, u32[]{:S(2)}, u32[]{:S(2)}) collective-permute-start(bf16[288,1536]{1,0:T(8,128)(2,1)S(1)} %pad_maximum_fusion.35), channel_id=1, source_target_pairs={{0,1},{1,0},{2,3},{3,2},{4,5},{5,4},{6,7},{7,6},{8,9},{9,8},{10,11... | collective-permute-start | bytes 2654216 | tf_op jit(solution)/shard_map/ppermute | solution.py:41
  481.8 41.9 %collective-permute-start.55 = (bf16[288,1536]{1,0:T(8,128)(2,1)S(1)}, bf16[288,1536]{1,0:T(8,128)(2,1)S(1)}, u32[]{:S(2)}, u32[]{:S(2)}) collective-permute-start(bf16[288,1536]{1,0:T(8,128)(2,1)S(1)} %pad_maximum_fusion.29), channel_id=1, source_target_pairs={{0,2},{1,3},{2,0},{3,1},{4,6},{5,7},{6,4},{7,5},{8,10},{9,11},{10,... | collective-permute-start | bytes 2654216 | tf_op jit(solution)/shard_map/ppermute | solution.py:41
  482.3 42.1 %collective-permute-start.54 = (bf16[288,1536]{1,0:T(8,128)(2,1)S(1)}, bf16[288,1536]{1,0:T(8,128)(2,1)S(1)}, u32[]{:S(2)}, u32[]{:S(2)}) collective-permute-start(bf16[288,1536]{1,0:T(8,128)(2,1)S(1)} %pad_maximum_fusion.29), channel_id=1, source_target_pairs={{0,1},{1,0},{2,3},{3,2},{4,5},{5,4},{6,7},{7,6},{8,9},{9,8},{10,11... | collective-permute-start | bytes 2654216 | tf_op jit(solution)/shard_map/ppermute | solution.py:41
  496.5 26.5 %collective-permute-start.65 = (bf16[144,1536]{1,0:T(8,128)(2,1)S(1)}, bf16[144,1536]{1,0:T(8,128)(2,1)S(1)}, u32[]{:S(2)}, u32[]{:S(2)}) collective-permute-start(bf16[144,1536]{1,0:T(8,128)(2,1)S(1)} %slice.1458), channel_id=1, source_target_pairs={{0,1},{1,0},{2,3},{3,2},{4,5},{5,4},{6,7},{7,6},{8,9},{9,8},{10,11... | collective-permute-start | bytes 1327112 | tf_op jit(solution)/shard_map/ppermute | solution.py:41
  498.3 26.7 %collective-permute-start.64 = (bf16[144,1536]{1,0:T(8,128)(2,1)S(1)}, bf16[144,1536]{1,0:T(8,128)(2,1)S(1)}, u32[]{:S(2)}, u32[]{:S(2)}) collective-permute-start(bf16[144,1536]{1,0:T(8,128)(2,1)S(1)} %slice.1457), channel_id=1, source_target_pairs={{0,2},{1,3},{2,0},{3,1},{4,6},{5,7},{6,4},{7,5},{8,10},{9,11},{10,... | collective-permute-start | bytes 1327112 | tf_op jit(solution)/shard_map/ppermute | solution.py:41
  562.6 417.1 %reduce-scatter.9.cloned.1.call-start = ((), (), s32[]{:S(2)}) async-start(), calls=%async_computation.7 | async-start | bytes 10616832 | tf_op jit(solution)/shard_map/reduce_scatter | solution.py:409
  630.5 361.9 %reduce-scatter.11.cloned.1.call-start = ((), (), s32[]{:S(2)}) async-start(), calls=%async_computation.8 | async-start | bytes 10616832 | tf_op jit(solution)/shard_map/reduce_scatter | solution.py:409
  630.8 42.2 %collective-permute-start.58 = (bf16[144,1536]{1,0:T(8,128)(2,1)S(1)}, bf16[144,1536]{1,0:T(8,128)(2,1)S(1)}, u32[]{:S(2)}, u32[]{:S(2)}) collective-permute-start(bf16[144,1536]{1,0:T(8,128)(2,1)S(1)} %get-tuple-element.276), channel_id=1, source_target_pairs={{0,2},{1,3},{2,0},{3,1},{4,6},{5,7},{6,4},{7,5},{8,10},{9,11},{10,... | collective-permute-start | bytes 1327112 | tf_op jit(solution)/shard_map/ppermute | solution.py:41
  632.3 39.8 %collective-permute-start.60 = (bf16[144,1536]{1,0:T(8,128)(2,1)S(1)}, bf16[144,1536]{1,0:T(8,128)(2,1)S(1)}, u32[]{:S(2)}, u32[]{:S(2)}) collective-permute-start(bf16[144,1536]{1,0:T(8,128)(2,1)S(1)} %get-tuple-element.277), channel_id=1, source_target_pairs={{0,1},{1,0},{2,3},{3,2},{4,5},{5,4},{6,7},{7,6},{8,9},{9,8},{10,11... | collective-permute-start | bytes 1327112 | tf_op jit(solution)/shard_map/ppermute | solution.py:41
  669.7 22.7 %collective-permute-start.69 = (bf16[288,1536]{1,0:T(8,128)(2,1)S(1)}, bf16[288,1536]{1,0:T(8,128)(2,1)S(1)}, u32[]{:S(2)}, u32[]{:S(2)}) collective-permute-start(bf16[288,1536]{1,0:T(8,128)(2,1)S(1)} %pad_maximum_fusion.40), channel_id=1, source_target_pairs={{0,2},{1,3},{2,0},{3,1},{4,6},{5,7},{6,4},{7,5},{8,10},{9,11},{10,... | collective-permute-start | bytes 2654216 | tf_op jit(solution)/shard_map/ppermute | solution.py:41
  671.2 22.7 %collective-permute-start.67 = (bf16[288,1536]{1,0:T(8,128)(2,1)S(1)}, bf16[288,1536]{1,0:T(8,128)(2,1)S(1)}, u32[]{:S(2)}, u32[]{:S(2)}) collective-permute-start(bf16[288,1536]{1,0:T(8,128)(2,1)S(1)} %pad_maximum_fusion.39), channel_id=1, source_target_pairs={{0,1},{1,0},{2,3},{3,2},{4,5},{5,4},{6,7},{7,6},{8,9},{9,8},{10,11... | collective-permute-start | bytes 2654216 | tf_op jit(solution)/shard_map/ppermute | solution.py:41
  672.3 36.5 %collective-permute-start.61 = (bf16[288,1536]{1,0:T(8,128)(2,1)S(1)}, bf16[288,1536]{1,0:T(8,128)(2,1)S(1)}, u32[]{:S(2)}, u32[]{:S(2)}) collective-permute-start(bf16[288,1536]{1,0:T(8,128)(2,1)S(1)} %pad_maximum_fusion.34), channel_id=1, source_target_pairs={{0,2},{1,3},{2,0},{3,1},{4,6},{5,7},{6,4},{7,5},{8,10},{9,11},{10,... | collective-permute-start | bytes 2654216 | tf_op jit(solution)/shard_map/ppermute | solution.py:41
  673.2 36.9 %collective-permute-start.59 = (bf16[288,1536]{1,0:T(8,128)(2,1)S(1)}, bf16[288,1536]{1,0:T(8,128)(2,1)S(1)}, u32[]{:S(2)}, u32[]{:S(2)}) collective-permute-start(bf16[288,1536]{1,0:T(8,128)(2,1)S(1)} %pad_maximum_fusion.33), channel_id=1, source_target_pairs={{0,1},{1,0},{2,3},{3,2},{4,5},{5,4},{6,7},{7,6},{8,9},{9,8},{10,11... | collective-permute-start | bytes 2654216 | tf_op jit(solution)/shard_map/ppermute | solution.py:41
  714.5 19.5 %collective-permute-start.71 = (bf16[288,1536]{1,0:T(8,128)(2,1)S(1)}, bf16[288,1536]{1,0:T(8,128)(2,1)S(1)}, u32[]{:S(2)}, u32[]{:S(2)}) collective-permute-start(bf16[288,1536]{1,0:T(8,128)(2,1)S(1)} %pad_maximum_fusion.41), channel_id=1, source_target_pairs={{0,2},{1,3},{2,0},{3,1},{4,6},{5,7},{6,4},{7,5},{8,10},{9,11},{10,... | collective-permute-start | bytes 2654216 | tf_op jit(solution)/shard_map/ppermute | solution.py:41
  715.2 19.6 %collective-permute-start.70 = (bf16[288,1536]{1,0:T(8,128)(2,1)S(1)}, bf16[288,1536]{1,0:T(8,128)(2,1)S(1)}, u32[]{:S(2)}, u32[]{:S(2)}) collective-permute-start(bf16[288,1536]{1,0:T(8,128)(2,1)S(1)} %pad_maximum_fusion.41), channel_id=1, source_target_pairs={{0,1},{1,0},{2,3},{3,2},{4,5},{5,4},{6,7},{7,6},{8,9},{9,8},{10,11... | collective-permute-start | bytes 2654216 | tf_op jit(solution)/shard_map/ppermute | solution.py:41
  802.5 378.0 %reduce-scatter.17.cloned.1.call-start = ((), (), s32[]{:S(2)}) async-start(), calls=%async_computation.11 | async-start | bytes 10616832 | tf_op jit(solution)/shard_map/reduce_scatter | solution.py:409
  817.1 27.3 %collective-permute-start.77 = (bf16[288,1536]{1,0:T(8,128)(2,1)S(1)}, bf16[288,1536]{1,0:T(8,128)(2,1)S(1)}, u32[]{:S(2)}, u32[]{:S(2)}) collective-permute-start(bf16[288,1536]{1,0:T(8,128)(2,1)S(1)} %pad_maximum_fusion.47), channel_id=1, source_target_pairs={{0,2},{1,3},{2,0},{3,1},{4,6},{5,7},{6,4},{7,5},{8,10},{9,11},{10,... | collective-permute-start | bytes 2654216 | tf_op jit(solution)/shard_map/ppermute | solution.py:41
  851.7 18.9 %collective-permute-start.79 = (bf16[288,1536]{1,0:T(8,128)(2,1)S(1)}, bf16[288,1536]{1,0:T(8,128)(2,1)S(1)}, u32[]{:S(2)}, u32[]{:S(2)}) collective-permute-start(bf16[288,1536]{1,0:T(8,128)(2,1)S(1)} %pad_maximum_fusion.48), channel_id=1, source_target_pairs={{0,2},{1,3},{2,0},{3,1},{4,6},{5,7},{6,4},{7,5},{8,10},{9,11},{10,... | collective-permute-start | bytes 2654216 | tf_op jit(solution)/shard_map/ppermute | solution.py:41
  853.7 20.7 %collective-permute-start.78 = (bf16[288,1536]{1,0:T(8,128)(2,1)S(1)}, bf16[288,1536]{1,0:T(8,128)(2,1)S(1)}, u32[]{:S(2)}, u32[]{:S(2)}) collective-permute-start(bf16[288,1536]{1,0:T(8,128)(2,1)S(1)} %pad_maximum_fusion.48), channel_id=1, source_target_pairs={{0,1},{1,0},{2,3},{3,2},{4,5},{5,4},{6,7},{7,6},{8,9},{9,8},{10,11... | collective-permute-start | bytes 2654216 | tf_op jit(solution)/shard_map/ppermute | solution.py:41
  897.3 333.8 %reduce-scatter.15.cloned.1.call-start = ((), (), s32[]{:S(2)}) async-start(), calls=%async_computation.10 | async-start | bytes 10616832 | tf_op jit(solution)/shard_map/reduce_scatter | solution.py:409
  945.8 289.5 %reduce-scatter.13.cloned.1.call-start = ((), (), s32[]{:S(2)}) async-start(), calls=%async_computation.9 | async-start | bytes 10616832 | tf_op jit(solution)/shard_map/reduce_scatter | solution.py:409
  972.1 18.7 %collective-permute-start.85 = (bf16[288,1536]{1,0:T(8,128)(2,1)S(1)}, bf16[288,1536]{1,0:T(8,128)(2,1)S(1)}, u32[]{:S(2)}, u32[]{:S(2)}) collective-permute-start(bf16[288,1536]{1,0:T(8,128)(2,1)S(1)} %pad_maximum_fusion.53), channel_id=1, source_target_pairs={{0,2},{1,3},{2,0},{3,1},{4,6},{5,7},{6,4},{7,5},{8,10},{9,11},{10,... | collective-permute-start | bytes 2654216 | tf_op jit(solution)/shard_map/ppermute | solution.py:41
  974.1 17.8 %collective-permute-start.83 = (bf16[288,1536]{1,0:T(8,128)(2,1)S(1)}, bf16[288,1536]{1,0:T(8,128)(2,1)S(1)}, u32[]{:S(2)}, u32[]{:S(2)}) collective-permute-start(bf16[288,1536]{1,0:T(8,128)(2,1)S(1)} %pad_maximum_fusion.52), channel_id=1, source_target_pairs={{0,1},{1,0},{2,3},{3,2},{4,5},{5,4},{6,7},{7,6},{8,9},{9,8},{10,11... | collective-permute-start | bytes 2654216 | tf_op jit(solution)/shard_map/ppermute | solution.py:41
  1003.5 17.1 %collective-permute-start.87 = (bf16[288,1536]{1,0:T(8,128)(2,1)}, bf16[288,1536]{1,0:T(8,128)(2,1)S(1)}, u32[]{:S(2)}, u32[]{:S(2)}) collective-permute-start(bf16[288,1536]{1,0:T(8,128)(2,1)} %pad_maximum_fusion.54), channel_id=1, source_target_pairs={{0,2},{1,3},{2,0},{3,1},{4,6},{5,7},{6,4},{7,5},{8,10},{9,11},{10,... | collective-permute-start | bytes 2654216 | tf_op jit(solution)/shard_map/ppermute | solution.py:41
  1005.6 22.0 %collective-permute-start.86 = (bf16[288,1536]{1,0:T(8,128)(2,1)}, bf16[288,1536]{1,0:T(8,128)(2,1)}, u32[]{:S(2)}, u32[]{:S(2)}) collective-permute-start(bf16[288,1536]{1,0:T(8,128)(2,1)} %pad_maximum_fusion.54), channel_id=1, source_target_pairs={{0,1},{1,0},{2,3},{3,2},{4,5},{5,4},{6,7},{7,6},{8,9},{9,8},{10,11... | collective-permute-start | bytes 2654216 | tf_op jit(solution)/shard_map/ppermute | solution.py:41
  1092.3 29.2 %collective-permute-start.106 = (f32[2,9216]{1,0:T(2,128)}, f32[2,9216]{1,0:T(2,128)}, u32[]{:S(2)}, u32[]{:S(2)}) collective-permute-start(f32[2,9216]{1,0:T(2,128)} %pad_maximum_fusion.72), channel_id=1, source_target_pairs={{0,3},{1,2},{2,1},{3,0},{4,7},{5,6},{6,5},{7,4},{8,11},{9,10},{10,... | collective-permute-start | bytes 221192 | tf_op jit(solution)/shard_map/ppermute | solution.py:41
  1092.9 28.7 %collective-permute-start.105 = (f32[2,9216]{1,0:T(2,128)}, f32[2,9216]{1,0:T(2,128)}, u32[]{:S(2)}, u32[]{:S(2)}) collective-permute-start(f32[2,9216]{1,0:T(2,128)} %pad_maximum_fusion.72), channel_id=1, source_target_pairs={{0,2},{1,3},{2,0},{3,1},{4,6},{5,7},{6,4},{7,5},{8,10},{9,11},{10,... | collective-permute-start | bytes 221192 | tf_op jit(solution)/shard_map/ppermute | solution.py:41
  1094.2 27.3 %collective-permute-start.104 = (f32[2,9216]{1,0:T(2,128)}, f32[2,9216]{1,0:T(2,128)}, u32[]{:S(2)}, u32[]{:S(2)}) collective-permute-start(f32[2,9216]{1,0:T(2,128)} %pad_maximum_fusion.72), channel_id=1, source_target_pairs={{0,1},{1,0},{2,3},{3,2},{4,5},{5,4},{6,7},{7,6},{8,9},{9,8},{10,11... | collective-permute-start | bytes 221192 | tf_op jit(solution)/shard_map/ppermute | solution.py:41
  1103.1 16.8 %collective-permute-start.90 = (bf16[144,1536]{1,0:T(8,128)(2,1)S(1)}, bf16[144,1536]{1,0:T(8,128)(2,1)S(1)}, u32[]{:S(2)}, u32[]{:S(2)}) collective-permute-start(bf16[144,1536]{1,0:T(8,128)(2,1)S(1)} %get-tuple-element.252), channel_id=1, source_target_pairs={{0,2},{1,3},{2,0},{3,1},{4,6},{5,7},{6,4},{7,5},{8,10},{9,11},{10,... | collective-permute-start | bytes 1327112 | tf_op jit(solution)/shard_map/ppermute | solution.py:41
  1118.4 38.4 %collective-permute-start.93 = (bf16[288,1536]{1,0:T(8,128)(2,1)}, bf16[288,1536]{1,0:T(8,128)(2,1)}, u32[]{:S(2)}, u32[]{:S(2)}) collective-permute-start(bf16[288,1536]{1,0:T(8,128)(2,1)} %pad_maximum_fusion.60), channel_id=1, source_target_pairs={{0,2},{1,3},{2,0},{3,1},{4,6},{5,7},{6,4},{7,5},{8,10},{9,11},{10,... | collective-permute-start | bytes 2654216 | tf_op jit(solution)/shard_map/ppermute | solution.py:41
  1120.1 36.7 %collective-permute-start.91 = (bf16[288,1536]{1,0:T(8,128)(2,1)S(1)}, bf16[288,1536]{1,0:T(8,128)(2,1)}, u32[]{:S(2)}, u32[]{:S(2)}) collective-permute-start(bf16[288,1536]{1,0:T(8,128)(2,1)S(1)} %pad_maximum_fusion.59), channel_id=1, source_target_pairs={{0,1},{1,0},{2,3},{3,2},{4,5},{5,4},{6,7},{7,6},{8,9},{9,8},{10,11... | collective-permute-start | bytes 2654216 | tf_op jit(solution)/shard_map/ppermute | solution.py:41
  1201.2 19.8 %collective-permute-start.103 = (f32[2,9216]{1,0:T(2,128)S(1)}, f32[2,9216]{1,0:T(2,128)S(1)}, u32[]{:S(2)}, u32[]{:S(2)}) collective-permute-start(f32[2,9216]{1,0:T(2,128)S(1)} %add_add_fusion.17), channel_id=1, source_target_pairs={{0,28},{4,24},{8,20},{12,16},{16,12},{20,8},{24,4},{28,0},{1,29},{... | collective-permute-start | bytes 221192 | tf_op jit(solution)/shard_map/ppermute | solution.py:41
  1202.0 18.6 %collective-permute-start.100 = (f32[2,9216]{1,0:T(2,128)S(1)}, f32[2,9216]{1,0:T(2,128)S(1)}, u32[]{:S(2)}, u32[]{:S(2)}) collective-permute-start(f32[2,9216]{1,0:T(2,128)S(1)} %add_add_fusion.17), channel_id=1, source_target_pairs={{0,16},{4,20},{8,24},{12,28},{16,0},{20,4},{24,8},{28,12},{1,17},{... | collective-permute-start | bytes 221192 | tf_op jit(solution)/shard_map/ppermute | solution.py:41
  (406 other events, 4015.0 us)
Sparse Core Ops, SparseCore 0:
  10.3 76.0 all-gather.16
  88.0 34.3 all-gather.18
  124.5 89.3 all-gather.20
  216.0 89.1 all-gather.22
  306.7 69.6 all-gather.24
  377.9 30.2 all-gather.26
  409.8 89.8 all-gather.28
  501.2 89.1 all-gather.30
  592.8 97.9 reduce-scatter.6
  692.9 97.8 reduce-scatter.8
  802.6 97.0 reduce-scatter.10
  901.8 97.8 reduce-scatter.16
  1002.1 97.7 reduce-scatter.14
  1102.0 123.1 reduce-scatter.12

commit v4 on v3

--- a/solution.py
+++ b/solution.py
@@ -49,58 +49,93 @@
     return jnp.concatenate(gather_parts(values, axis), axis=0)
 
 
+def assemble_kernel(count, *refs):
+    parts, (image_ref, text_ref) = refs[:-2], refs[-2:]
+    place = 0
+    size = count + text_ref.shape[0] * count // image_ref.shape[0]
+    for part in parts:
+        rows, taken = part.shape[0], 0
+        while taken < rows:
+            owner, offset = divmod(place, size)
+            if offset < count:
+                length = min(rows - taken, count - offset)
+                target, start = image_ref, owner * count + offset
+            else:
+                length = min(rows - taken, size - offset)
+                target, start = text_ref, owner * (size - count) + offset - count
+            target[start : start + length] = part[taken : taken + length]
+            place, taken = place + length, taken + length
+
+
+def assemble(parts, counts):
+    size = lax.axis_size("tensor")
+    return pl.pallas_call(
+        functools.partial(assemble_kernel, counts[0]),
+        out_shape=[
+            jax.ShapeDtypeStruct((size * count, parts[0].shape[1]), parts[0].dtype)
+            for count in counts
+        ],
+        cost_estimate=pl.CostEstimate(
+            flops=0, bytes_accessed=4 * size * sum(counts) * parts[0].shape[1], transcendentals=0
+        ),
+        name="assemble",
+    )(*parts)
+
+
 def gather_streams(streams):
     counts = [values.shape[0] for values in streams]
     rows = jnp.concatenate(streams)
     if lax.axis_size("tensor") == 4:
         half = rows.shape[0] // 2
         first, second = (exchange(rows, "tensor", step) for step in (1, 2))
-        far = jnp.concatenate(
-            [exchange(first[:half], "tensor", 2), exchange(second[half:], "tensor", 1)]
-        )
-        parts = [rows, first, second, far]
+        parts = [
+            rows,
+            first,
+            second,
+            exchange(first[:half], "tensor", 2),
+            exchange(second[half:], "tensor", 1),
+        ]
     else:
         parts = gather_parts(rows, "tensor")
-    return [
-        jnp.concatenate([part[: counts[0]] for part in parts]),
-        jnp.concatenate([part[counts[0] :] for part in parts]),
-    ]
+    return assemble(parts, counts)
 
 
 def scatter_streams(left, right):
     size = lax.axis_size("tensor")
     counts = [values.shape[0] // size for values in left]
 
-    def piece(step):
-        return jnp.concatenate(
-            [
-                lax.dot_general(
-                    left[stream][step * counts[stream] : (step + 1) * counts[stream]],
-                    right[stream],
-                    contract_columns,
-                    preferred_element_type=jnp.float32,
-                ).astype(jnp.bfloat16)
-                for stream in range(2)
-            ]
-        )
+    def product(stream, start, stop):
+        return lax.dot_general(
+            left[stream][start * counts[stream] : stop * counts[stream]],
+            right[stream],
+            contract_columns,
+            preferred_element_type=jnp.float32,
+        ).astype(jnp.bfloat16)
+
+    text = product(1, 0, size)
+
+    def joined(image, step):
+        return jnp.concatenate([image, text[step * counts[1] : (step + 1) * counts[1]]])
 
     if size == 4:
         half = sum(counts) // 2
-        far = lax.optimization_barrier(piece(3))
+        far = joined(product(0, 3, 4), 3)
         first_in = exchange(far[:half], "tensor", 1)
         second_in = exchange(far[half:], "tensor", 2)
-        first, second = lax.optimization_barrier((piece(1), piece(2)))
+        near = after(product(0, 1, 3), far)
+        first = joined(near[: counts[0]], 1)
+        second = joined(near[counts[0] :], 2)
+        started = (far, near)
         first = jnp.concatenate([first[:half], first[half:] + second_in])
         second = jnp.concatenate([second[:half] + first_in, second[half:]])
         pieces = [exchange(first, "tensor", 1), exchange(second, "tensor", 2)]
     else:
-        far = piece(size - 1)
-        pieces = [exchange(far, "tensor", size - 1)]
-        pieces += [exchange(piece(step), "tensor", step) for step in range(1, size - 1)]
-    total = piece(0).astype(jnp.float32)
+        started = [joined(product(0, step, step + 1), step) for step in range(1, size)]
+        pieces = [exchange(started[step - 1], "tensor", step) for step in range(1, size)]
+    total = joined(product(0, 0, 1), 0).astype(jnp.float32)
     for values in pieces:
         total = total + values.astype(jnp.float32)
-    return [total[: counts[0]], total[counts[0] :]], far
+    return [total[: counts[0]], total[counts[0] :]], started
 
 
 def sum_over(values, axis):
@@ -580,6 +615,21 @@
     for step, block in enumerate(gather_parts(mine, "tensor")):
         table = lax.dynamic_update_slice_in_dim(table, block, (rank ^ step) * width, 0)
     return table.reshape(LAYERS, 2, -1)
+
+
+def gather_slots(slot_grads):
+    size = lax.axis_size("tensor")
+    rank = lax.axis_index("tensor")
+    values = slot_grads.reshape(size, 1, -1)
+    owned = lax.dynamic_index_in_dim(values, rank, 0, False)
+    for step in range(1, size):
+        block = lax.dynamic_index_in_dim(values, rank ^ step, 0, False)
+        owned = owned + exchange(block, "tensor", step)
+    owned = gather_rows(owned, "dp")
+    result = jnp.zeros((owned.shape[0], size * owned.shape[1]), jnp.float32)
+    for step, block in enumerate(gather_parts(owned, "tensor")):
+        result = lax.dynamic_update_slice_in_dim(result, block, (rank ^ step) * owned.shape[1], 1)
+    return result
 
 
 def on_device(
@@ -613,10 +663,16 @@
     states = [image_tokens.astype(jnp.float32), text_tokens.astype(jnp.float32)]
     stored = []
     for tier in range(LAYERS):
-        weights = [
-            lax.all_gather(matrix[tier], "dp", axis=1, tiled=True)
-            for matrix in (projection, recombine, expansion, contraction)
+        attention, up, down = [
+            lax.all_gather(matrix, "dp", axis=1, tiled=True)
+            for matrix in (
+                jnp.concatenate([projection[tier], recombine[tier]], axis=2),
+                expansion[tier],
+                contraction[tier],
+            )
         ]
+        width = projection.shape[3]
+        weights = [attention[:, :, :width], attention[:, :, width:], up, down]
         pieces = layer_biases(bias_all[tier], tensor_rank, width_local, hidden_local)
         shifts = [
             [slot_shifts[tier, stream, part * D : (part + 1) * D] for part in range(6)]
@@ -646,9 +702,10 @@
         slot_store.insert(0, slot_grads)
     slot_store[1:], bias_store[1:] = after((slot_store[1:], bias_store[1:]), computed)
     for slot_grads in slot_store:
-        slot_sums = jnp.stack(gather_parts(sum_over(slot_grads, "tensor"), "dp"))
         modulation_store.append(
-            jnp.einsum("pd,psm->sdm", slot_rows, slot_sums, precision=highest)
+            jnp.dot(slot_rows.T, gather_slots(slot_grads), precision=highest)
+            .reshape(shard_rows, 2, -1)
+            .transpose(1, 0, 2)
         )
     stacked = [
         jnp.stack([entry[kind] for entry in weight_store]) for kind in range(4)

time: 1260 us -> 1230 us (0.976)
  other arithmetic: 122 us -> 88.1 us
  Pallas kernels: 203 us -> 235 us
  starting transfers between devices: 128 us -> 154 us
  matrix products: 228 us -> 203 us
  local copies, waits for them, and re-layouts: 117 us -> 95.8 us
    dot_general x66 -> x34, matrix products: 143 us -> 103 us  [the longest x32 96.9 us: product(): lax.dot_general(left[stream][start * counts[stream]:stop * counts[stream]...]
    pallas_call x0 -> x8, Pallas kernels: none -> 32.1 us  [assemble(): pl.pallas_call(functools.partial(assemble_kernel, counts[0]), out_shape=[...]
    concatenate x40 -> x10, other arithmetic: 35.5 us -> 7.28 us  [the longest x8 3.8 us: joined(): jnp.concatenate([image, text[step * counts[1]:(step + 1) * counts[1]]])]
    ppermute x124 -> x130, starting transfers between devices: 127 us -> 153 us  [exchange(): lax.ppermute(values, axis, [(rank, rank ^ step) for rank in range(size)])]
    slice x65 -> x24, local copies, waits for them, and re-layouts: 34.1 us -> 11.4 us  [the longest x1 3.21 us: on_device(): contraction[tier]]
    all_gather x8 -> x6, waiting for transfers between devices: 57.3 us -> 41 us  [on_device(): lax.all_gather(matrix, 'dp', axis=1, tiled=True)]
    ppermute x124 -> x130, waiting for transfers between devices: 369 us -> 377 us  [exchange(): lax.ppermute(values, axis, [(rank, rank ^ step) for rank in range(size)])]
  transfers between devices with their start and end apart: 138 -> 142, of which waited for: 65 -> 66; matrix products, arithmetic and copies ran while one was open for 35% -> 29% of each run, Pallas kernels for 16% -> 19%
where the time goes in v4:
time: 1230 us; the launch traced here: 1220 us
  waiting for transfers between devices  419 us (34%)
  Pallas kernels  235 us (19%)
  matrix products  203 us (17%)
  starting transfers between devices  154 us (13%)
  local copies, waits for them, and re-layouts  95.8 us (8%)
  other arithmetic  88.1 us (7%)
  between operations  20.7 us (2%)
    ppermute x130, waiting for transfers between devices, exchange(): lax.ppermute(values, axis, [(rank, rank ^ step) for rank in range(size)])  377 us
    ppermute x130, starting transfers between devices, exchange(): lax.ppermute(values, axis, [(rank, rank ^ step) for rank in range(size)])  153 us
    dot_general x32, matrix products, product(): lax.dot_general(left[stream][start * counts[stream]:stop * counts[stream]...  96.9 us
    pallas_call x6, Pallas kernels, weight_grads(): pl.pallas_call(functools.partial(weight_grads_kernel, len(pairs)), grid=(...  77.2 us
    pallas_call x2, Pallas kernels, attend_back(): pl.pallas_call(functools.partial(attend_back_kernel, heads, row_block(row...  67.4 us
    pallas_call x2, Pallas kernels, attend(): pl.pallas_call(functools.partial(attend_kernel, heads, row_block(rows)),...  54.7 us
    all_gather x6, waiting for transfers between devices, on_device(): lax.all_gather(matrix, 'dp', axis=1, tiled=True)  41 us
    dot_general x4, matrix products, backward_layer(): jnp.dot(branch_rows[stream], feed_weights[stream], preferred_element_type...  32.3 us
  transfers between devices with their start and end apart: 142, of which 66 were waited for; matrix products, arithmetic and copies ran while one was open for 29% of the time, Pallas kernels for 19%

profile of v4, /device:TPU:0, one launch (start us, length us, event | category | flops | bytes accessed | tf_op | source)
XLA Modules:
  0.0 1215.8 jit_solution(6804644682073962179)
XLA Ops:
  47.7 4.5 collective-permute-start.6
  54.2 4.4 concatenate.229
  63.8 4.8 collective-permute-done.24
  74.4 4.9 collective-permute-start.28
  112.4 17.5 %collective-permute-done.30.refs_1_ = bf16[288,1536]{1,0:T(8,128)(2,1)S(1)} collective-permute-done((bf16[288,1536]{1,0:T(8,128)(2,1)S(1)}, bf16[288,1536]{1,0:T(8,128)(2,1)S(1)}, u32[]{:S(2)}, u32[]{:S(2)}) %collective-permute-start.30) | collective-permute-done | bytes 884768 | tf_op jit(solution)/shard_map/ppermute | solution.py:41
  150.8 6.5 add_convert_fusion.1
  159.1 27.4 %attend.2 = (bf16[1152,384]{1,0:T(8,128)(2,1)}, f32[1152,128]{1,0:T(8,128)}) custom-call(bf16[1152,1152]{1,0:T(8,128)(2,1)} %pad_maximum_fusion.1.columns_ref), custom_call_target="tpu_custom_call" | custom-call | flops 2038431744 | bytes 3981312 | tf_op jit(solution)/shard_map/attend/pallas_call | solution.py:241
  195.0 6.9 collective-permute-done.36
  210.1 11.8 collective-permute-done.37
  227.0 16.3 %collective-permute-done.38.refs_1_ = bf16[288,1536]{1,0:T(8,128)(2,1)S(1)} collective-permute-done((bf16[288,1536]{1,0:T(8,128)(2,1)S(1)}, bf16[288,1536]{1,0:T(8,128)(2,1)S(1)}, u32[]{:S(2)}, u32[]{:S(2)}) %collective-permute-start.38) | collective-permute-done | bytes 884768 | tf_op jit(solution)/shard_map/ppermute | solution.py:41
  249.0 4.7 collective-permute-done.40.refs_3_
  259.3 11.6 multiply_convert_fusion.1
  270.9 28.1 %all-gather.17.cloned.1.call-done = bf16[1,2,1536,1536]{3,2,1,0:T(8,128)(2,1)} async-done(((bf16[1,2,192,1536]{3,2,1,0:T(8,128)(2,1)}), bf16[1,2,1536,1536]{3,2,1,0:T(8,128)(2,1)}) %all-gather.17.cloned.1.call-update) | async-done | bytes 9437200 | tf_op jit(solution)/shard_map/all_gather | solution.py:667
  299.0 5.6 fusion.57
  316.6 9.3 collective-permute-done.44
  330.2 4.1 fusion.64
  334.3 13.0 %collective-permute-done.45 = bf16[288,1536]{1,0:T(8,128)(2,1)} collective-permute-done((bf16[288,1536]{1,0:T(8,128)(2,1)S(1)}, bf16[288,1536]{1,0:T(8,128)(2,1)}, u32[]{:S(2)}, u32[]{:S(2)}) %collective-permute-start.45) | collective-permute-done | bytes 884768 | tf_op jit(solution)/shard_map/ppermute | solution.py:41
  358.3 16.5 %collective-permute-done.46.refs_1_ = bf16[288,1536]{1,0:T(8,128)(2,1)} collective-permute-done((bf16[288,1536]{1,0:T(8,128)(2,1)S(1)}, bf16[288,1536]{1,0:T(8,128)(2,1)}, u32[]{:S(2)}, u32[]{:S(2)}) %collective-permute-start.46) | collective-permute-done | bytes 884768 | tf_op jit(solution)/shard_map/ppermute | solution.py:41
  380.0 5.4 collective-permute-done.48.refs_3_
  394.2 7.1 add_convert_fusion
  403.0 27.3 %attend.3 = (bf16[1152,384]{1,0:T(8,128)(2,1)}, f32[1152,128]{1,0:T(8,128)}) custom-call(bf16[1152,1152]{1,0:T(8,128)(2,1)} %pad_maximum_fusion.2.columns_ref), custom_call_target="tpu_custom_call" | custom-call | flops 2038431744 | bytes 3981312 | tf_op jit(solution)/shard_map/attend/pallas_call | solution.py:241
  439.3 8.1 collective-permute-done.52
  454.5 15.7 %collective-permute-done.53 = bf16[288,1536]{1,0:T(8,128)(2,1)S(1)} collective-permute-done((bf16[288,1536]{1,0:T(8,128)(2,1)S(1)}, bf16[288,1536]{1,0:T(8,128)(2,1)S(1)}, u32[]{:S(2)}, u32[]{:S(2)}) %collective-permute-start.53) | collective-permute-done | bytes 884768 | tf_op jit(solution)/shard_map/ppermute | solution.py:41
  476.8 14.0 %collective-permute-done.62.refs_1_ = bf16[288,1536]{1,0:T(8,128)(2,1)S(1)} collective-permute-done((bf16[288,1536]{1,0:T(8,128)(2,1)S(1)}, bf16[288,1536]{1,0:T(8,128)(2,1)S(1)}, u32[]{:S(2)}, u32[]{:S(2)}) %collective-permute-start.62) | collective-permute-done | bytes 884768 | tf_op jit(solution)/shard_map/ppermute | solution.py:41
  493.1 16.7 %collective-permute-done.54.refs_1_ = bf16[288,1536]{1,0:T(8,128)(2,1)S(1)} collective-permute-done((bf16[288,1536]{1,0:T(8,128)(2,1)S(1)}, bf16[288,1536]{1,0:T(8,128)(2,1)S(1)}, u32[]{:S(2)}, u32[]{:S(2)}) %collective-permute-start.54) | collective-permute-done | bytes 884768 | tf_op jit(solution)/shard_map/ppermute | solution.py:41
  529.8 4.6 multiply_convert_fusion.6
  534.4 10.9 multiply_convert_fusion
  545.2 12.6 %weight_grads.6 = bf16[1536,3072]{1,0:T(8,128)(2,1)} custom-call(bf16[1024,1536]{1,0:T(8,128)(2,1)} %get-tuple-element.79.refs_0_, bf16[1024,1536]{1,0:T(8,128)(2,1)} %get-tuple-element.431.refs_1_, bf16[128,1536]{1,0:T(8,128)(2,1)} %get-tuple-element.81.refs_2_, bf16[128,1536]{1,0:T(8,128)(2,1)} %get-tuple-element.433.refs_3_), custom_call_target="tpu_custom_call" | custom-call | flops 5435817984 | bytes 16515072 | tf_op jit(solution)/shard_map/weight_grads/pallas_call | solution.py:430
  558.2 12.9 %all-gather.21.cloned.1.call-done = bf16[1,2,1536,1536]{3,2,1,0:T(8,128)(2,1)} async-done(((bf16[1,2,192,1536]{3,2,1,0:T(8,128)(2,1)}), bf16[1,2,1536,1536]{3,2,1,0:T(8,128)(2,1)}) %all-gather.21.cloned.1.call-update) | async-done | bytes 9437200 | tf_op jit(solution)/shard_map/all_gather | solution.py:667
  571.1 4.6 convert_reduce_fusion.6
  575.7 4.7 fusion.72
  581.1 11.5 convert_reduce_fusion.1
  598.6 12.5 %weight_grads.7 = bf16[1536,3072]{1,0:T(8,128)(2,1)} custom-call(bf16[1024,1536]{1,0:T(8,128)(2,1)} %get-tuple-element.74.refs_0_, bf16[1024,1536]{1,0:T(8,128)(2,1)} %copy-done.283, bf16[128,1536]{1,0:T(8,128)(2,1)} %get-tuple-element.75.refs_2_, bf16[128,1536]{1,0:T(8,128)(2,1)} %copy-done.287), custom_call_target="tpu_custom_call" | custom-call | flops 5435817984 | bytes 16515072 | tf_op jit(solution)/shard_map/weight_grads/pallas_call | solution.py:430
  615.7 5.8 fusion.56
  640.1 17.5 %collective-permute-done.69 = bf16[288,1536]{1,0:T(8,128)(2,1)S(1)} collective-permute-done((bf16[288,1536]{1,0:T(8,128)(2,1)S(1)}, bf16[288,1536]{1,0:T(8,128)(2,1)S(1)}, u32[]{:S(2)}, u32[]{:S(2)}) %collective-permute-start.69) | collective-permute-done | bytes 884768 | tf_op jit(solution)/shard_map/ppermute | solution.py:41
  661.2 13.6 %collective-permute-done.61 = bf16[288,1536]{1,0:T(8,128)(2,1)S(1)} collective-permute-done((bf16[288,1536]{1,0:T(8,128)(2,1)S(1)}, bf16[288,1536]{1,0:T(8,128)(2,1)S(1)}, u32[]{:S(2)}, u32[]{:S(2)}) %collective-permute-start.61) | collective-permute-done | bytes 884768 | tf_op jit(solution)/shard_map/ppermute | solution.py:41
  682.2 18.5 %collective-permute-done.70.refs_1_ = bf16[288,1536]{1,0:T(8,128)(2,1)S(1)} collective-permute-done((bf16[288,1536]{1,0:T(8,128)(2,1)S(1)}, bf16[288,1536]{1,0:T(8,128)(2,1)S(1)}, u32[]{:S(2)}, u32[]{:S(2)}) %collective-permute-start.70) | collective-permute-done | bytes 884768 | tf_op jit(solution)/shard_map/ppermute | solution.py:41
  703.5 8.0 collective-permute-done.72.refs_3_
  712.6 4.1 assemble.13
  718.5 4.2 convolution_convert_fusion.15
  723.7 33.8 %attend_back.2.refs_5_.refs_7_ = bf16[1152,1152]{1,0:T(8,128)(2,1)} custom-call(bf16[1152,1152]{1,0:T(8,128)(2,1)} %pad_maximum_fusion.2.columns_ref, bf16[1152,384]{1,0:T(8,128)(2,1)} %get-tuple-element.72.out_ref.refs_1_.refs_3_, f32[1152,128]{1,0:T(8,128)} %get-tuple-element.88.log_ref, bf16[1152,384]{1,0:T(8,128)(2,1)} %pad_maximum_fusion.24.grad_ref), custom_call_target="tpu_custom_call" | custom-call | flops 5096079360 | bytes 7962624 | tf_op jit(solution)/shard_map/attend_back/pallas_call | solution.py:310
  761.0 4.2 convolution_convert_fusion.10
  766.0 4.2 convolution_convert_fusion.1
  770.2 13.4 %weight_grads.8 = bf16[1536,3072]{1,0:T(8,128)(2,1)} custom-call(bf16[1024,1536]{1,0:T(8,128)(2,1)} %get-tuple-element.90.refs_0_, bf16[1152,384]{1,0:T(8,128)(2,1)} %get-tuple-element.72.out_ref.refs_1_.refs_3_, bf16[128,1536]{1,0:T(8,128)(2,1)} %get-tuple-element.91.refs_2_, bf16[1152,384]{1,0:T(8,128)(2,1)} %get-tuple-element.72.out_ref.refs_1_.refs_3_, ...), custom_call_target="tpu_custom_call" | custom-call | flops 5435817984 | bytes 20054016 | tf_op jit(solution)/shard_map/weight_grads/pallas_call | solution.py:430
  787.4 5.9 collective-permute-done.76
  800.9 12.5 %collective-permute-done.77 = bf16[288,1536]{1,0:T(8,128)(2,1)S(1)} collective-permute-done((bf16[288,1536]{1,0:T(8,128)(2,1)S(1)}, bf16[288,1536]{1,0:T(8,128)(2,1)S(1)}, u32[]{:S(2)}, u32[]{:S(2)}) %collective-permute-start.77) | collective-permute-done | bytes 884768 | tf_op jit(solution)/shard_map/ppermute | solution.py:41
  823.4 17.4 %collective-permute-done.78.refs_1_ = bf16[288,1536]{1,0:T(8,128)(2,1)S(1)} collective-permute-done((bf16[288,1536]{1,0:T(8,128)(2,1)S(1)}, bf16[288,1536]{1,0:T(8,128)(2,1)S(1)}, u32[]{:S(2)}, u32[]{:S(2)}) %collective-permute-start.78) | collective-permute-done | bytes 884768 | tf_op jit(solution)/shard_map/ppermute | solution.py:41
  844.8 5.0 collective-permute-done.80.refs_3_
  855.2 12.6 %weight_grads.9 = bf16[1536,3072]{1,0:T(8,128)(2,1)} custom-call(bf16[1024,1536]{1,0:T(8,128)(2,1)} %get-tuple-element.98.refs_0_, bf16[1024,1536]{1,0:T(8,128)(2,1)} %get-tuple-element.429.refs_1_, bf16[128,1536]{1,0:T(8,128)(2,1)} %get-tuple-element.100.refs_2_, bf16[128,1536]{1,0:T(8,128)(2,1)} %copy-done.284), custom_call_target="tpu_custom_call" | custom-call | flops 5435817984 | bytes 16515072 | tf_op jit(solution)/shard_map/weight_grads/pallas_call | solution.py:430
  873.4 4.4 convert_reduce_fusion.5
  877.8 4.2 fusion.73
  882.1 11.8 convert_reduce_fusion
  898.2 12.6 %weight_grads.10 = bf16[1536,3072]{1,0:T(8,128)(2,1)} custom-call(bf16[1024,1536]{1,0:T(8,128)(2,1)} %get-tuple-element.67.refs_0_, bf16[1024,1536]{1,0:T(8,128)(2,1)} %copy-done.281, bf16[128,1536]{1,0:T(8,128)(2,1)} %get-tuple-element.68.refs_2_, bf16[128,1536]{1,0:T(8,128)(2,1)} %copy-done.286), custom_call_target="tpu_custom_call" | custom-call | flops 5435817984 | bytes 16515072 | tf_op jit(solution)/shard_map/weight_grads/pallas_call | solution.py:430
  917.7 5.1 collective-permute-done.84
  926.6 4.1 fusion.60
  933.1 9.8 collective-permute-done.85
  962.9 11.8 collective-permute-done.86.refs_1_
  996.7 33.6 %attend_back.3.refs_5_.refs_7_ = bf16[1152,1152]{1,0:T(8,128)(2,1)} custom-call(bf16[1152,1152]{1,0:T(8,128)(2,1)} %pad_maximum_fusion.1.columns_ref, bf16[1152,384]{1,0:T(8,128)(2,1)} %get-tuple-element.65.out_ref.refs_1_.refs_3_, f32[1152,128]{1,0:T(8,128)} %get-tuple-element.107.log_ref, bf16[1152,384]{1,0:T(8,128)(2,1)} %pad_maximum_fusion.29.grad_ref), custom_call_target="tpu_custom_call" | custom-call | flops 5096079360 | bytes 7962624 | tf_op jit(solution)/shard_map/attend_back/pallas_call | solution.py:310
  1033.6 13.4 %weight_grads.11 = bf16[1536,3072]{1,0:T(8,128)(2,1)} custom-call(bf16[1024,1536]{1,0:T(8,128)(2,1)} %get-tuple-element.109.refs_0_, bf16[1152,384]{1,0:T(8,128)(2,1)} %get-tuple-element.65.out_ref.refs_1_.refs_3_, bf16[128,1536]{1,0:T(8,128)(2,1)} %get-tuple-element.110.refs_2_, bf16[1152,384]{1,0:T(8,128)(2,1)} %get-tuple-element.65.out_ref.refs_1_.refs_3_, ...), custom_call_target="tpu_custom_call" | custom-call | flops 5435817984 | bytes 20054016 | tf_op jit(solution)/shard_map/weight_grads/pallas_call | solution.py:430
  1047.0 4.8 convolution_convert_fusion
  1069.3 4.3 convolution_convert_fusion.9
  1092.8 10.5 collective-permute-done.117
  1115.3 11.1 collective-permute-done.93
  1157.1 7.0 collective-permute-done.101
  (1304 shorter events, 499.7 us)
Async XLA Ops:
  7.2 140.6 %all-gather.11.cloned.1.call-start = ((), (), s32[]{:S(2)}) async-start(), calls=%async_computation.6 | async-start | bytes 10616832 | tf_op jit(solution)/shard_map/all_gather | solution.py:667
  12.8 246.4 %all-gather.15.cloned.1.call-start = ((), (), s32[]{:S(2)}) async-start(), calls=%async_computation.14 | async-start | bytes 10616832 | tf_op jit(solution)/shard_map/all_gather | solution.py:667
  16.1 282.9 %all-gather.17.cloned.1.call-start = ((), (), s32[]{:S(2)}) async-start(), calls=%async_computation.15 | async-start | bytes 10616832 | tf_op jit(solution)/shard_map/all_gather | solution.py:667
  19.4 371.7 %all-gather.13.cloned.1.call-start = ((), (), s32[]{:S(2)}) async-start(), calls=%async_computation.7 | async-start | bytes 10616832 | tf_op jit(solution)/shard_map/all_gather | solution.py:667
  21.8 507.9 %all-gather.19.cloned.1.call-start = ((), (), s32[]{:S(2)}) async-start(), calls=%async_computation.16 | async-start | bytes 10616832 | tf_op jit(solution)/shard_map/all_gather | solution.py:667
  21.9 17.6 %collective-permute-start = (s32[1]{0:T(128)}, s32[1]{0:T(128)}, u32[]{:S(2)}, u32[]{:S(2)}) collective-permute-start(s32[1]{0:T(128)} %param.16), channel_id=1, source_target_pairs={{0,4},{4,0},{8,12},{12,8},{16,20},{20,16},{24,28},{28,24},{1,5},{5... | collective-permute-start | bytes 20 | tf_op jit(solution)/shard_map/ppermute | solution.py:41
  22.4 17.2 %collective-permute-start.1 = (s32[1]{0:T(128)}, s32[1]{0:T(128)}, u32[]{:S(2)}, u32[]{:S(2)}) collective-permute-start(s32[1]{0:T(128)} %param.16), channel_id=1, source_target_pairs={{0,8},{4,12},{8,0},{12,4},{16,24},{20,28},{24,16},{28,20},{1,9},{5... | collective-permute-start | bytes 20 | tf_op jit(solution)/shard_map/ppermute | solution.py:41
  25.1 33.5 %collective-permute-start.22 = (bf16[1,4,672]{2,1,0:T(4,128)(2,1)S(1)}, bf16[1,4,672]{2,1,0:T(4,128)(2,1)}, u32[]{:S(2)}, u32[]{:S(2)}) collective-permute-start(bf16[1,4,672]{2,1,0:T(4,128)(2,1)S(1)} %reshape.427), channel_id=1, source_target_pairs={{0,3},{1,2},{2,1},{3,0},{4,7},{5,6},{6,5},{7,4},{8,11},{9,10},{10,... | collective-permute-start | bytes 16136 | tf_op jit(solution)/shard_map/ppermute | solution.py:41
  27.6 32.7 %collective-permute-start.21 = (bf16[1,4,672]{2,1,0:T(4,128)(2,1)S(1)}, bf16[1,4,672]{2,1,0:T(4,128)(2,1)}, u32[]{:S(2)}, u32[]{:S(2)}) collective-permute-start(bf16[1,4,672]{2,1,0:T(4,128)(2,1)S(1)} %reshape.427), channel_id=1, source_target_pairs={{0,2},{1,3},{2,0},{3,1},{4,6},{5,7},{6,4},{7,5},{8,10},{9,11},{10,... | collective-permute-start | bytes 16136 | tf_op jit(solution)/shard_map/ppermute | solution.py:41
  28.1 32.2 %collective-permute-start.20 = (bf16[1,4,672]{2,1,0:T(4,128)(2,1)S(1)}, bf16[1,4,672]{2,1,0:T(4,128)(2,1)}, u32[]{:S(2)}, u32[]{:S(2)}) collective-permute-start(bf16[1,4,672]{2,1,0:T(4,128)(2,1)S(1)} %reshape.427), channel_id=1, source_target_pairs={{0,1},{1,0},{2,3},{3,2},{4,5},{5,4},{6,7},{7,6},{8,9},{9,8},{10,11... | collective-permute-start | bytes 16136 | tf_op jit(solution)/shard_map/ppermute | solution.py:41
  52.2 28.0 %collective-permute-start.9 = (f32[6,9216]{1,0:T(8,128)S(1)}, f32[6,9216]{1,0:T(8,128)S(1)}, u32[]{:S(2)}, u32[]{:S(2)}) collective-permute-start(f32[6,9216]{1,0:T(8,128)S(1)} %get-tuple-element.296), channel_id=1, source_target_pairs={{0,3},{1,2},{2,1},{3,0},{4,7},{5,6},{6,5},{7,4},{8,11},{9,10},{10,... | collective-permute-start | bytes 663560 | tf_op jit(solution)/shard_map/ppermute | solution.py:41
  53.7 26.5 %collective-permute-start.8 = (f32[6,9216]{1,0:T(8,128)S(1)}, f32[6,9216]{1,0:T(8,128)S(1)}, u32[]{:S(2)}, u32[]{:S(2)}) collective-permute-start(f32[6,9216]{1,0:T(8,128)S(1)} %get-tuple-element.297), channel_id=1, source_target_pairs={{0,2},{1,3},{2,0},{3,1},{4,6},{5,7},{6,4},{7,5},{8,10},{9,11},{10,... | collective-permute-start | bytes 663560 | tf_op jit(solution)/shard_map/ppermute | solution.py:41
  58.6 21.6 %collective-permute-start.7 = (f32[6,9216]{1,0:T(8,128)S(1)}, f32[6,9216]{1,0:T(8,128)S(1)}, u32[]{:S(2)}, u32[]{:S(2)}) collective-permute-start(f32[6,9216]{1,0:T(8,128)S(1)} %get-tuple-element.295), channel_id=1, source_target_pairs={{0,1},{1,0},{2,3},{3,2},{4,5},{5,4},{6,7},{7,6},{8,9},{9,8},{10,11... | collective-permute-start | bytes 663560 | tf_op jit(solution)/shard_map/ppermute | solution.py:41
  109.0 20.9 %collective-permute-start.30 = (bf16[288,1536]{1,0:T(8,128)(2,1)S(1)}, bf16[288,1536]{1,0:T(8,128)(2,1)S(1)}, u32[]{:S(2)}, u32[]{:S(2)}) collective-permute-start(bf16[288,1536]{1,0:T(8,128)(2,1)S(1)} %pad_maximum_fusion.13.refs_0_), channel_id=1, source_target_pairs={{0,1},{1,0},{2,3},{3,2},{4,5},{5,4},{6,7},{7,6},{8,9},{9,8},{10,11... | collective-permute-start | bytes 2654216 | tf_op jit(solution)/shard_map/ppermute | solution.py:41
  110.3 21.4 %collective-permute-start.31 = (bf16[288,1536]{1,0:T(8,128)(2,1)S(1)}, bf16[288,1536]{1,0:T(8,128)(2,1)}, u32[]{:S(2)}, u32[]{:S(2)}) collective-permute-start(bf16[288,1536]{1,0:T(8,128)(2,1)S(1)} %pad_maximum_fusion.13.refs_0_), channel_id=1, source_target_pairs={{0,2},{1,3},{2,0},{3,1},{4,6},{5,7},{6,4},{7,5},{8,10},{9,11},{10,... | collective-permute-start | bytes 2654216 | tf_op jit(solution)/shard_map/ppermute | solution.py:41
  112.1 459.0 %all-gather.21.cloned.1.call-start = ((), (), s32[]{:S(2)}) async-start(), calls=%async_computation.17 | async-start | bytes 10616832 | tf_op jit(solution)/shard_map/all_gather | solution.py:667
  202.1 19.8 %collective-permute-start.37 = (bf16[288,1536]{1,0:T(8,128)(2,1)S(1)}, bf16[288,1536]{1,0:T(8,128)(2,1)S(1)}, u32[]{:S(2)}, u32[]{:S(2)}) collective-permute-start(bf16[288,1536]{1,0:T(8,128)(2,1)S(1)} %fusion.107), channel_id=1, source_target_pairs={{0,2},{1,3},{2,0},{3,1},{4,6},{5,7},{6,4},{7,5},{8,10},{9,11},{10,... | collective-permute-start | bytes 2654216 | tf_op jit(solution)/shard_map/ppermute | solution.py:41
  204.8 17.0 %collective-permute-start.35 = (bf16[288,1536]{1,0:T(8,128)(2,1)S(1)}, bf16[288,1536]{1,0:T(8,128)(2,1)S(1)}, u32[]{:S(2)}, u32[]{:S(2)}) collective-permute-start(bf16[288,1536]{1,0:T(8,128)(2,1)S(1)} %pad_maximum_fusion.14), channel_id=1, source_target_pairs={{0,1},{1,0},{2,3},{3,2},{4,5},{5,4},{6,7},{7,6},{8,9},{9,8},{10,11... | collective-permute-start | bytes 2654216 | tf_op jit(solution)/shard_map/ppermute | solution.py:41
  224.5 18.8 %collective-permute-start.38 = (bf16[288,1536]{1,0:T(8,128)(2,1)S(1)}, bf16[288,1536]{1,0:T(8,128)(2,1)S(1)}, u32[]{:S(2)}, u32[]{:S(2)}) collective-permute-start(bf16[288,1536]{1,0:T(8,128)(2,1)S(1)} %pad_maximum_fusion.15.refs_0_), channel_id=1, source_target_pairs={{0,1},{1,0},{2,3},{3,2},{4,5},{5,4},{6,7},{7,6},{8,9},{9,8},{10,11... | collective-permute-start | bytes 2654216 | tf_op jit(solution)/shard_map/ppermute | solution.py:41
  225.4 19.9 %collective-permute-start.39 = (bf16[288,1536]{1,0:T(8,128)(2,1)S(1)}, bf16[288,1536]{1,0:T(8,128)(2,1)S(1)}, u32[]{:S(2)}, u32[]{:S(2)}) collective-permute-start(bf16[288,1536]{1,0:T(8,128)(2,1)S(1)} %pad_maximum_fusion.15.refs_0_), channel_id=1, source_target_pairs={{0,2},{1,3},{2,0},{3,1},{4,6},{5,7},{6,4},{7,5},{8,10},{9,11},{10,... | collective-permute-start | bytes 2654216 | tf_op jit(solution)/shard_map/ppermute | solution.py:41
  326.0 21.3 %collective-permute-start.45 = (bf16[288,1536]{1,0:T(8,128)(2,1)S(1)}, bf16[288,1536]{1,0:T(8,128)(2,1)}, u32[]{:S(2)}, u32[]{:S(2)}) collective-permute-start(bf16[288,1536]{1,0:T(8,128)(2,1)S(1)} %fusion.109), channel_id=1, source_target_pairs={{0,2},{1,3},{2,0},{3,1},{4,6},{5,7},{6,4},{7,5},{8,10},{9,11},{10,... | collective-permute-start | bytes 2654216 | tf_op jit(solution)/shard_map/ppermute | solution.py:41
  328.7 21.2 %collective-permute-start.43 = (bf16[288,1536]{1,0:T(8,128)(2,1)}, bf16[288,1536]{1,0:T(8,128)(2,1)}, u32[]{:S(2)}, u32[]{:S(2)}) collective-permute-start(bf16[288,1536]{1,0:T(8,128)(2,1)} %pad_maximum_fusion.16), channel_id=1, source_target_pairs={{0,1},{1,0},{2,3},{3,2},{4,5},{5,4},{6,7},{7,6},{8,9},{9,8},{10,11... | collective-permute-start | bytes 2654216 | tf_op jit(solution)/shard_map/ppermute | solution.py:41
  330.1 543.2 %reduce-scatter.7.cloned.1.call-start = ((), (), s32[]{:S(2)}) async-start(), calls=%async_computation.8 | async-start | bytes 10616832 | tf_op jit(solution)/shard_map/reduce_scatter | solution.py:444
  354.7 20.1 %collective-permute-start.46 = (bf16[288,1536]{1,0:T(8,128)(2,1)S(1)}, bf16[288,1536]{1,0:T(8,128)(2,1)}, u32[]{:S(2)}, u32[]{:S(2)}) collective-permute-start(bf16[288,1536]{1,0:T(8,128)(2,1)S(1)} %pad_maximum_fusion.17.refs_0_), channel_id=1, source_target_pairs={{0,1},{1,0},{2,3},{3,2},{4,5},{5,4},{6,7},{7,6},{8,9},{9,8},{10,11... | collective-permute-start | bytes 2654216 | tf_op jit(solution)/shard_map/ppermute | solution.py:41
  356.1 20.5 %collective-permute-start.47 = (bf16[288,1536]{1,0:T(8,128)(2,1)S(1)}, bf16[288,1536]{1,0:T(8,128)(2,1)}, u32[]{:S(2)}, u32[]{:S(2)}) collective-permute-start(bf16[288,1536]{1,0:T(8,128)(2,1)S(1)} %pad_maximum_fusion.17.refs_0_), channel_id=1, source_target_pairs={{0,2},{1,3},{2,0},{3,1},{4,6},{5,7},{6,4},{7,5},{8,10},{9,11},{10,... | collective-permute-start | bytes 2654216 | tf_op jit(solution)/shard_map/ppermute | solution.py:41
  447.5 22.6 %collective-permute-start.53 = (bf16[288,1536]{1,0:T(8,128)(2,1)S(1)}, bf16[288,1536]{1,0:T(8,128)(2,1)S(1)}, u32[]{:S(2)}, u32[]{:S(2)}) collective-permute-start(bf16[288,1536]{1,0:T(8,128)(2,1)S(1)} %fusion.111), channel_id=1, source_target_pairs={{0,2},{1,3},{2,0},{3,1},{4,6},{5,7},{6,4},{7,5},{8,10},{9,11},{10,... | collective-permute-start | bytes 2654216 | tf_op jit(solution)/shard_map/ppermute | solution.py:41
  449.2 22.7 %collective-permute-start.51 = (bf16[288,1536]{1,0:T(8,128)(2,1)S(1)}, bf16[288,1536]{1,0:T(8,128)(2,1)S(1)}, u32[]{:S(2)}, u32[]{:S(2)}) collective-permute-start(bf16[288,1536]{1,0:T(8,128)(2,1)S(1)} %pad_maximum_fusion.18), channel_id=1, source_target_pairs={{0,1},{1,0},{2,3},{3,2},{4,5},{5,4},{6,7},{7,6},{8,9},{9,8},{10,11... | collective-permute-start | bytes 2654216 | tf_op jit(solution)/shard_map/ppermute | solution.py:41
  450.9 39.9 %collective-permute-start.62 = (bf16[288,1536]{1,0:T(8,128)(2,1)S(1)}, bf16[288,1536]{1,0:T(8,128)(2,1)S(1)}, u32[]{:S(2)}, u32[]{:S(2)}) collective-permute-start(bf16[288,1536]{1,0:T(8,128)(2,1)S(1)} %pad_maximum_fusion.21.refs_0_), channel_id=1, source_target_pairs={{0,1},{1,0},{2,3},{3,2},{4,5},{5,4},{6,7},{7,6},{8,9},{9,8},{10,11... | collective-permute-start | bytes 2654216 | tf_op jit(solution)/shard_map/ppermute | solution.py:41
  451.9 40.1 %collective-permute-start.63 = (bf16[288,1536]{1,0:T(8,128)(2,1)S(1)}, bf16[288,1536]{1,0:T(8,128)(2,1)S(1)}, u32[]{:S(2)}, u32[]{:S(2)}) collective-permute-start(bf16[288,1536]{1,0:T(8,128)(2,1)S(1)} %pad_maximum_fusion.21.refs_0_), channel_id=1, source_target_pairs={{0,2},{1,3},{2,0},{3,1},{4,6},{5,7},{6,4},{7,5},{8,10},{9,11},{10,... | collective-permute-start | bytes 2654216 | tf_op jit(solution)/shard_map/ppermute | solution.py:41
  474.8 35.0 %collective-permute-start.54 = (bf16[288,1536]{1,0:T(8,128)(2,1)S(1)}, bf16[288,1536]{1,0:T(8,128)(2,1)S(1)}, u32[]{:S(2)}, u32[]{:S(2)}) collective-permute-start(bf16[288,1536]{1,0:T(8,128)(2,1)S(1)} %pad_maximum_fusion.19.refs_0_), channel_id=1, source_target_pairs={{0,1},{1,0},{2,3},{3,2},{4,5},{5,4},{6,7},{7,6},{8,9},{9,8},{10,11... | collective-permute-start | bytes 2654216 | tf_op jit(solution)/shard_map/ppermute | solution.py:41
  476.3 35.5 %collective-permute-start.55 = (bf16[288,1536]{1,0:T(8,128)(2,1)S(1)}, bf16[288,1536]{1,0:T(8,128)(2,1)S(1)}, u32[]{:S(2)}, u32[]{:S(2)}) collective-permute-start(bf16[288,1536]{1,0:T(8,128)(2,1)S(1)} %pad_maximum_fusion.19.refs_0_), channel_id=1, source_target_pairs={{0,2},{1,3},{2,0},{3,1},{4,6},{5,7},{6,4},{7,5},{8,10},{9,11},{10,... | collective-permute-start | bytes 2654216 | tf_op jit(solution)/shard_map/ppermute | solution.py:41
  490.9 26.7 %collective-permute-start.64 = (bf16[144,1536]{1,0:T(8,128)(2,1)S(1)}, bf16[144,1536]{1,0:T(8,128)(2,1)S(1)}, u32[]{:S(2)}, u32[]{:S(2)}) collective-permute-start(bf16[144,1536]{1,0:T(8,128)(2,1)S(1)} %slice.1264), channel_id=1, source_target_pairs={{0,2},{1,3},{2,0},{3,1},{4,6},{5,7},{6,4},{7,5},{8,10},{9,11},{10,... | collective-permute-start | bytes 1327112 | tf_op jit(solution)/shard_map/ppermute | solution.py:41
  492.1 27.3 %collective-permute-start.65 = (bf16[144,1536]{1,0:T(8,128)(2,1)S(1)}, bf16[144,1536]{1,0:T(8,128)(2,1)}, u32[]{:S(2)}, u32[]{:S(2)}) collective-permute-start(bf16[144,1536]{1,0:T(8,128)(2,1)S(1)} %slice.1265), channel_id=1, source_target_pairs={{0,1},{1,0},{2,3},{3,2},{4,5},{5,4},{6,7},{7,6},{8,9},{9,8},{10,11... | collective-permute-start | bytes 1327112 | tf_op jit(solution)/shard_map/ppermute | solution.py:41
  510.6 13.8 %collective-permute-start.56 = (bf16[144,1536]{1,0:T(8,128)(2,1)}, bf16[144,1536]{1,0:T(8,128)(2,1)}, u32[]{:S(2)}, u32[]{:S(2)}) collective-permute-start(bf16[144,1536]{1,0:T(8,128)(2,1)} %slice.1243), channel_id=1, source_target_pairs={{0,2},{1,3},{2,0},{3,1},{4,6},{5,7},{6,4},{7,5},{8,10},{9,11},{10,... | collective-permute-start | bytes 1327112 | tf_op jit(solution)/shard_map/ppermute | solution.py:41
  557.9 372.8 %reduce-scatter.9.cloned.1.call-start = ((), (), s32[]{:S(2)}) async-start(), calls=%async_computation.9 | async-start | bytes 10616832 | tf_op jit(solution)/shard_map/reduce_scatter | solution.py:444
  611.2 333.4 %reduce-scatter.11.cloned.1.call-start = ((), (), s32[]{:S(2)}) async-start(), calls=%async_computation.10 | async-start | bytes 10616832 | tf_op jit(solution)/shard_map/reduce_scatter | solution.py:444
  613.0 17.7 %collective-permute-start.68 = (bf16[144,1536]{1,0:T(8,128)(2,1)S(1)}, bf16[144,1536]{1,0:T(8,128)(2,1)S(1)}, u32[]{:S(2)}, u32[]{:S(2)}) collective-permute-start(bf16[144,1536]{1,0:T(8,128)(2,1)S(1)} %get-tuple-element.305), channel_id=1, source_target_pairs={{0,1},{1,0},{2,3},{3,2},{4,5},{5,4},{6,7},{7,6},{8,9},{9,8},{10,11... | collective-permute-start | bytes 1327112 | tf_op jit(solution)/shard_map/ppermute | solution.py:41
  614.2 18.7 %collective-permute-start.66 = (bf16[144,1536]{1,0:T(8,128)(2,1)S(1)}, bf16[144,1536]{1,0:T(8,128)(2,1)S(1)}, u32[]{:S(2)}, u32[]{:S(2)}) collective-permute-start(bf16[144,1536]{1,0:T(8,128)(2,1)S(1)} %get-tuple-element.304), channel_id=1, source_target_pairs={{0,2},{1,3},{2,0},{3,1},{4,6},{5,7},{6,4},{7,5},{8,10},{9,11},{10,... | collective-permute-start | bytes 1327112 | tf_op jit(solution)/shard_map/ppermute | solution.py:41
  631.6 26.0 %collective-permute-start.69 = (bf16[288,1536]{1,0:T(8,128)(2,1)S(1)}, bf16[288,1536]{1,0:T(8,128)(2,1)S(1)}, u32[]{:S(2)}, u32[]{:S(2)}) collective-permute-start(bf16[288,1536]{1,0:T(8,128)(2,1)S(1)} %fusion.115), channel_id=1, source_target_pairs={{0,2},{1,3},{2,0},{3,1},{4,6},{5,7},{6,4},{7,5},{8,10},{9,11},{10,... | collective-permute-start | bytes 2654216 | tf_op jit(solution)/shard_map/ppermute | solution.py:41
  633.1 24.6 %collective-permute-start.67 = (bf16[288,1536]{1,0:T(8,128)(2,1)S(1)}, bf16[288,1536]{1,0:T(8,128)(2,1)S(1)}, u32[]{:S(2)}, u32[]{:S(2)}) collective-permute-start(bf16[288,1536]{1,0:T(8,128)(2,1)S(1)} %pad_maximum_fusion.22), channel_id=1, source_target_pairs={{0,1},{1,0},{2,3},{3,2},{4,5},{5,4},{6,7},{7,6},{8,9},{9,8},{10,11... | collective-permute-start | bytes 2654216 | tf_op jit(solution)/shard_map/ppermute | solution.py:41
  638.0 36.9 %collective-permute-start.61 = (bf16[288,1536]{1,0:T(8,128)(2,1)S(1)}, bf16[288,1536]{1,0:T(8,128)(2,1)S(1)}, u32[]{:S(2)}, u32[]{:S(2)}) collective-permute-start(bf16[288,1536]{1,0:T(8,128)(2,1)S(1)} %fusion.113), channel_id=1, source_target_pairs={{0,2},{1,3},{2,0},{3,1},{4,6},{5,7},{6,4},{7,5},{8,10},{9,11},{10,... | collective-permute-start | bytes 2654216 | tf_op jit(solution)/shard_map/ppermute | solution.py:41
  638.9 36.0 %collective-permute-start.59 = (bf16[288,1536]{1,0:T(8,128)(2,1)S(1)}, bf16[288,1536]{1,0:T(8,128)(2,1)S(1)}, u32[]{:S(2)}, u32[]{:S(2)}) collective-permute-start(bf16[288,1536]{1,0:T(8,128)(2,1)S(1)} %pad_maximum_fusion.20), channel_id=1, source_target_pairs={{0,1},{1,0},{2,3},{3,2},{4,5},{5,4},{6,7},{7,6},{8,9},{9,8},{10,11... | collective-permute-start | bytes 2654216 | tf_op jit(solution)/shard_map/ppermute | solution.py:41
  680.4 20.3 %collective-permute-start.70 = (bf16[288,1536]{1,0:T(8,128)(2,1)S(1)}, bf16[288,1536]{1,0:T(8,128)(2,1)S(1)}, u32[]{:S(2)}, u32[]{:S(2)}) collective-permute-start(bf16[288,1536]{1,0:T(8,128)(2,1)S(1)} %pad_maximum_fusion.23.refs_0_), channel_id=1, source_target_pairs={{0,1},{1,0},{2,3},{3,2},{4,5},{5,4},{6,7},{7,6},{8,9},{9,8},{10,11... | collective-permute-start | bytes 2654216 | tf_op jit(solution)/shard_map/ppermute | solution.py:41
  681.9 20.4 %collective-permute-start.71 = (bf16[288,1536]{1,0:T(8,128)(2,1)S(1)}, bf16[288,1536]{1,0:T(8,128)(2,1)S(1)}, u32[]{:S(2)}, u32[]{:S(2)}) collective-permute-start(bf16[288,1536]{1,0:T(8,128)(2,1)S(1)} %pad_maximum_fusion.23.refs_0_), channel_id=1, source_target_pairs={{0,2},{1,3},{2,0},{3,1},{4,6},{5,7},{6,4},{7,5},{8,10},{9,11},{10,... | collective-permute-start | bytes 2654216 | tf_op jit(solution)/shard_map/ppermute | solution.py:41
  783.6 352.4 %reduce-scatter.17.cloned.1.call-start = ((), (), s32[]{:S(2)}) async-start(), calls=%async_computation.13 | async-start | bytes 10616832 | tf_op jit(solution)/shard_map/reduce_scatter | solution.py:444
  793.5 19.9 %collective-permute-start.77 = (bf16[288,1536]{1,0:T(8,128)(2,1)S(1)}, bf16[288,1536]{1,0:T(8,128)(2,1)S(1)}, u32[]{:S(2)}, u32[]{:S(2)}) collective-permute-start(bf16[288,1536]{1,0:T(8,128)(2,1)S(1)} %fusion.117), channel_id=1, source_target_pairs={{0,2},{1,3},{2,0},{3,1},{4,6},{5,7},{6,4},{7,5},{8,10},{9,11},{10,... | collective-permute-start | bytes 2654216 | tf_op jit(solution)/shard_map/ppermute | solution.py:41
  797.4 16.0 %collective-permute-start.75 = (bf16[288,1536]{1,0:T(8,128)(2,1)S(1)}, bf16[288,1536]{1,0:T(8,128)(2,1)S(1)}, u32[]{:S(2)}, u32[]{:S(2)}) collective-permute-start(bf16[288,1536]{1,0:T(8,128)(2,1)S(1)} %pad_maximum_fusion.25), channel_id=1, source_target_pairs={{0,1},{1,0},{2,3},{3,2},{4,5},{5,4},{6,7},{7,6},{8,9},{9,8},{10,11... | collective-permute-start | bytes 2654216 | tf_op jit(solution)/shard_map/ppermute | solution.py:41
  821.4 19.5 %collective-permute-start.78 = (bf16[288,1536]{1,0:T(8,128)(2,1)S(1)}, bf16[288,1536]{1,0:T(8,128)(2,1)S(1)}, u32[]{:S(2)}, u32[]{:S(2)}) collective-permute-start(bf16[288,1536]{1,0:T(8,128)(2,1)S(1)} %pad_maximum_fusion.26.refs_0_), channel_id=1, source_target_pairs={{0,1},{1,0},{2,3},{3,2},{4,5},{5,4},{6,7},{7,6},{8,9},{9,8},{10,11... | collective-permute-start | bytes 2654216 | tf_op jit(solution)/shard_map/ppermute | solution.py:41
  822.2 19.1 %collective-permute-start.79 = (bf16[288,1536]{1,0:T(8,128)(2,1)S(1)}, bf16[288,1536]{1,0:T(8,128)(2,1)S(1)}, u32[]{:S(2)}, u32[]{:S(2)}) collective-permute-start(bf16[288,1536]{1,0:T(8,128)(2,1)S(1)} %pad_maximum_fusion.26.refs_0_), channel_id=1, source_target_pairs={{0,2},{1,3},{2,0},{3,1},{4,6},{5,7},{6,4},{7,5},{8,10},{9,11},{10,... | collective-permute-start | bytes 2654216 | tf_op jit(solution)/shard_map/ppermute | solution.py:41
  868.0 329.6 %reduce-scatter.15.cloned.1.call-start = ((), (), s32[]{:S(2)}) async-start(), calls=%async_computation.12 | async-start | bytes 10616832 | tf_op jit(solution)/shard_map/reduce_scatter | solution.py:444
  910.9 291.7 %reduce-scatter.13.cloned.1.call-start = ((), (), s32[]{:S(2)}) async-start(), calls=%async_computation.11 | async-start | bytes 10616832 | tf_op jit(solution)/shard_map/reduce_scatter | solution.py:444
  922.9 20.1 %collective-permute-start.85 = (bf16[288,1536]{1,0:T(8,128)(2,1)S(1)}, bf16[288,1536]{1,0:T(8,128)(2,1)}, u32[]{:S(2)}, u32[]{:S(2)}) collective-permute-start(bf16[288,1536]{1,0:T(8,128)(2,1)S(1)} %fusion.119), channel_id=1, source_target_pairs={{0,2},{1,3},{2,0},{3,1},{4,6},{5,7},{6,4},{7,5},{8,10},{9,11},{10,... | collective-permute-start | bytes 2654216 | tf_op jit(solution)/shard_map/ppermute | solution.py:41
  926.5 16.4 %collective-permute-start.83 = (bf16[288,1536]{1,0:T(8,128)(2,1)S(1)}, bf16[288,1536]{1,0:T(8,128)(2,1)S(1)}, u32[]{:S(2)}, u32[]{:S(2)}) collective-permute-start(bf16[288,1536]{1,0:T(8,128)(2,1)S(1)} %pad_maximum_fusion.27), channel_id=1, source_target_pairs={{0,1},{1,0},{2,3},{3,2},{4,5},{5,4},{6,7},{7,6},{8,9},{9,8},{10,11... | collective-permute-start | bytes 2654216 | tf_op jit(solution)/shard_map/ppermute | solution.py:41
  955.6 19.1 %collective-permute-start.86 = (bf16[288,1536]{1,0:T(8,128)(2,1)S(1)}, bf16[288,1536]{1,0:T(8,128)(2,1)}, u32[]{:S(2)}, u32[]{:S(2)}) collective-permute-start(bf16[288,1536]{1,0:T(8,128)(2,1)S(1)} %pad_maximum_fusion.28.refs_0_), channel_id=1, source_target_pairs={{0,1},{1,0},{2,3},{3,2},{4,5},{5,4},{6,7},{7,6},{8,9},{9,8},{10,11... | collective-permute-start | bytes 2654216 | tf_op jit(solution)/shard_map/ppermute | solution.py:41
  956.0 20.3 %collective-permute-start.87 = (bf16[288,1536]{1,0:T(8,128)(2,1)S(1)}, bf16[288,1536]{1,0:T(8,128)(2,1)S(1)}, u32[]{:S(2)}, u32[]{:S(2)}) collective-permute-start(bf16[288,1536]{1,0:T(8,128)(2,1)S(1)} %pad_maximum_fusion.28.refs_0_), channel_id=1, source_target_pairs={{0,2},{1,3},{2,0},{3,1},{4,6},{5,7},{6,4},{7,5},{8,10},{9,11},{10,... | collective-permute-start | bytes 2654216 | tf_op jit(solution)/shard_map/ppermute | solution.py:41
  1086.8 20.3 %collective-permute-start.92 = (bf16[144,1536]{1,0:T(8,128)(2,1)}, bf16[144,1536]{1,0:T(8,128)(2,1)}, u32[]{:S(2)}, u32[]{:S(2)}) collective-permute-start(bf16[144,1536]{1,0:T(8,128)(2,1)} %get-tuple-element.299), channel_id=1, source_target_pairs={{0,1},{1,0},{2,3},{3,2},{4,5},{5,4},{6,7},{7,6},{8,9},{9,8},{10,11... | collective-permute-start | bytes 1327112 | tf_op jit(solution)/shard_map/ppermute | solution.py:41
  1088.5 20.4 %collective-permute-start.90 = (bf16[144,1536]{1,0:T(8,128)(2,1)}, bf16[144,1536]{1,0:T(8,128)(2,1)}, u32[]{:S(2)}, u32[]{:S(2)}) collective-permute-start(bf16[144,1536]{1,0:T(8,128)(2,1)} %get-tuple-element.298), channel_id=1, source_target_pairs={{0,2},{1,3},{2,0},{3,1},{4,6},{5,7},{6,4},{7,5},{8,10},{9,11},{10,... | collective-permute-start | bytes 1327112 | tf_op jit(solution)/shard_map/ppermute | solution.py:41
  1089.2 14.1 %collective-permute-start.117 = (f32[8,4608]{1,0:T(8,128)S(1)}, f32[8,4608]{1,0:T(8,128)S(1)}, u32[]{:S(2)}, u32[]{:S(2)}) collective-permute-start(f32[8,4608]{1,0:T(8,128)S(1)} %concatenate.301), channel_id=1, source_target_pairs={{0,1},{1,0},{2,3},{3,2},{4,5},{5,4},{6,7},{7,6},{8,9},{9,8},{10,11... | collective-permute-start | bytes 442376 | tf_op jit(solution)/shard_map/ppermute | solution.py:41
  1090.7 16.5 %collective-permute-start.118 = (f32[8,4608]{1,0:T(8,128)S(1)}, f32[8,4608]{1,0:T(8,128)S(1)}, u32[]{:S(2)}, u32[]{:S(2)}) collective-permute-start(f32[8,4608]{1,0:T(8,128)S(1)} %concatenate.301), channel_id=1, source_target_pairs={{0,2},{1,3},{2,0},{3,1},{4,6},{5,7},{6,4},{7,5},{8,10},{9,11},{10,... | collective-permute-start | bytes 442376 | tf_op jit(solution)/shard_map/ppermute | solution.py:41
  1091.3 18.9 %collective-permute-start.119 = (f32[8,4608]{1,0:T(8,128)S(1)}, f32[8,4608]{1,0:T(8,128)S(1)}, u32[]{:S(2)}, u32[]{:S(2)}) collective-permute-start(f32[8,4608]{1,0:T(8,128)S(1)} %concatenate.301), channel_id=1, source_target_pairs={{0,3},{1,2},{2,1},{3,0},{4,7},{5,6},{6,5},{7,4},{8,11},{9,10},{10,... | collective-permute-start | bytes 442376 | tf_op jit(solution)/shard_map/ppermute | solution.py:41
  1108.4 17.9 %collective-permute-start.93 = (bf16[288,1536]{1,0:T(8,128)(2,1)S(1)}, bf16[288,1536]{1,0:T(8,128)(2,1)S(1)}, u32[]{:S(2)}, u32[]{:S(2)}) collective-permute-start(bf16[288,1536]{1,0:T(8,128)(2,1)S(1)} %fusion.121), channel_id=1, source_target_pairs={{0,2},{1,3},{2,0},{3,1},{4,6},{5,7},{6,4},{7,5},{8,10},{9,11},{10,... | collective-permute-start | bytes 2654216 | tf_op jit(solution)/shard_map/ppermute | solution.py:41
  1110.1 17.6 %collective-permute-start.91 = (bf16[288,1536]{1,0:T(8,128)(2,1)S(1)}, bf16[288,1536]{1,0:T(8,128)(2,1)S(1)}, u32[]{:S(2)}, u32[]{:S(2)}) collective-permute-start(bf16[288,1536]{1,0:T(8,128)(2,1)S(1)} %pad_maximum_fusion.30), channel_id=1, source_target_pairs={{0,1},{1,0},{2,3},{3,2},{4,5},{5,4},{6,7},{7,6},{8,9},{9,8},{10,11... | collective-permute-start | bytes 2654216 | tf_op jit(solution)/shard_map/ppermute | solution.py:41
  1148.9 18.2 %collective-permute-start.126 = (f32[4,4,672]{2,1,0:T(4,128)S(1)}, f32[4,4,672]{2,1,0:T(4,128)S(1)}, u32[]{:S(2)}, u32[]{:S(2)}) collective-permute-start(f32[4,4,672]{2,1,0:T(4,128)S(1)} %get-tuple-element.317), channel_id=1, source_target_pairs={{0,28},{4,24},{8,20},{12,16},{16,12},{20,8},{24,4},{28,0},{1,29},{... | collective-permute-start | bytes 129032 | tf_op jit(solution)/shard_map/ppermute | solution.py:41
  1150.1 18.5 %collective-permute-start.125 = (f32[4,4,672]{2,1,0:T(4,128)S(1)}, f32[4,4,672]{2,1,0:T(4,128)S(1)}, u32[]{:S(2)}, u32[]{:S(2)}) collective-permute-start(f32[4,4,672]{2,1,0:T(4,128)S(1)} %get-tuple-element.318), channel_id=1, source_target_pairs={{0,24},{4,28},{8,16},{12,20},{16,8},{20,12},{24,0},{28,4},{1,25},{... | collective-permute-start | bytes 129032 | tf_op jit(solution)/shard_map/ppermute | solution.py:41
  (379 other events, 2954.0 us)
Sparse Core Ops, SparseCore 0:
  13.0 103.7 all-gather.10
  118.9 89.1 all-gather.14
  209.8 89.1 all-gather.16
  300.4 89.1 all-gather.12
  391.1 89.2 all-gather.18
  481.9 89.1 all-gather.20
  573.4 97.9 reduce-scatter.6
  673.7 97.8 reduce-scatter.8
  783.7 98.0 reduce-scatter.10
  884.0 97.8 reduce-scatter.16
  984.2 97.8 reduce-scatter.14
  1084.3 106.9 reduce-scatter.12

commit v5 on v4

--- a/solution.py
+++ b/solution.py
@@ -201,45 +201,29 @@
     return chunks.reshape(LAYERS, 2, width)
 
 
-def row_block(rows):
-    for block in (384, 256, 128):
-        if rows % block == 0:
-            return block
-    return rows
-
-
-def attend_kernel(heads, block, columns_ref, out_ref, log_ref):
-    rows = columns_ref.shape[0]
+def attend_kernel(heads, columns_ref, out_ref, log_ref):
     for head in range(heads):
         base = head * 3 * HEAD_DIM
+        queries = columns_ref[:, base : base + HEAD_DIM]
         keys = columns_ref[:, base + HEAD_DIM : base + 2 * HEAD_DIM]
         values = columns_ref[:, base + 2 * HEAD_DIM : base + 3 * HEAD_DIM]
-
-        def step(index, carry):
-            place = pl.ds(pl.multiple_of(index * block, block), block)
-            queries = columns_ref[place, base : base + HEAD_DIM]
-            scores = lax.dot_general(
-                queries, keys, contract_columns, preferred_element_type=jnp.float32
-            )
-            row_max = jnp.max(scores, -1, keepdims=True)
-            weights = jnp.exp2((scores - row_max) * EXPONENT)
-            totals = jnp.sum(weights, -1, keepdims=True)
-            output = jnp.dot(
-                weights.astype(jnp.bfloat16), values, preferred_element_type=jnp.float32
-            )
-            out_ref[place, head * HEAD_DIM : (head + 1) * HEAD_DIM] = (output / totals).astype(
-                jnp.bfloat16
-            )
-            log_ref[place, head : head + 1] = row_max * EXPONENT + jnp.log2(totals)
-            return carry
-
-        lax.fori_loop(0, rows // block, step, 0)
+        scores = lax.dot_general(
+            queries, keys, contract_columns, preferred_element_type=jnp.float32
+        )
+        row_max = jnp.max(scores, -1, keepdims=True)
+        weights = jnp.exp2((scores - row_max) * EXPONENT)
+        totals = jnp.sum(weights, -1, keepdims=True)
+        output = jnp.dot(weights.astype(jnp.bfloat16), values, preferred_element_type=jnp.float32)
+        out_ref[:, head * HEAD_DIM : (head + 1) * HEAD_DIM] = (output / totals).astype(
+            jnp.bfloat16
+        )
+        log_ref[:, head : head + 1] = row_max * EXPONENT + jnp.log2(totals)
 
 
 def attend(columns, heads):
     rows = columns.shape[0]
     return pl.pallas_call(
-        functools.partial(attend_kernel, heads, row_block(rows)),
+        functools.partial(attend_kernel, heads),
         out_shape=(
             jax.ShapeDtypeStruct((rows, heads * HEAD_DIM), jnp.bfloat16),
             jax.ShapeDtypeStruct((rows, 128), jnp.float32),
@@ -253,54 +237,42 @@
     )(columns)
 
 
-def attend_back_kernel(
-    heads, block, columns_ref, out_ref, log_ref, grad_ref, result_ref, key_acc, value_acc
-):
-    rows = columns_ref.shape[0]
+def attend_back_kernel(heads, columns_ref, out_ref, log_ref, grad_ref, result_ref):
     for head in range(heads):
         base = head * 3 * HEAD_DIM
         part = slice(head * HEAD_DIM, (head + 1) * HEAD_DIM)
+        queries = columns_ref[:, base : base + HEAD_DIM]
         keys = columns_ref[:, base + HEAD_DIM : base + 2 * HEAD_DIM]
         values = columns_ref[:, base + 2 * HEAD_DIM : base + 3 * HEAD_DIM]
-        key_acc[...] = jnp.zeros_like(key_acc)
-        value_acc[...] = jnp.zeros_like(value_acc)
-
-        def step(index, carry):
-            place = pl.ds(pl.multiple_of(index * block, block), block)
-            queries = columns_ref[place, base : base + HEAD_DIM]
-            grad_out = grad_ref[place, part]
-            inner = jnp.sum(
-                grad_out.astype(jnp.float32) * out_ref[place, part].astype(jnp.float32),
-                -1,
-                keepdims=True,
-            )
-            scores = lax.dot_general(
-                queries, keys, contract_columns, preferred_element_type=jnp.float32
-            )
-            weights = jnp.exp2(scores * EXPONENT - log_ref[place, head : head + 1])
-            grad_weights = lax.dot_general(
-                grad_out, values, contract_columns, preferred_element_type=jnp.float32
-            )
-            grad_scores = (weights * (grad_weights - inner)).astype(jnp.bfloat16)
-            result_ref[place, base : base + HEAD_DIM] = (
-                jnp.dot(grad_scores, keys, preferred_element_type=jnp.float32) * SCALE
-            ).astype(jnp.bfloat16)
-            key_acc[...] += lax.dot_general(
-                grad_scores, queries, contract_rows, preferred_element_type=jnp.float32
-            )
-            value_acc[...] += lax.dot_general(
-                weights.astype(jnp.bfloat16),
-                grad_out,
-                contract_rows,
-                preferred_element_type=jnp.float32,
-            )
-            return carry
-
-        lax.fori_loop(0, rows // block, step, 0)
-        result_ref[:, base + HEAD_DIM : base + 2 * HEAD_DIM] = (key_acc[...] * SCALE).astype(
+        grad_out = grad_ref[:, part]
+        inner = jnp.sum(
+            grad_out.astype(jnp.float32) * out_ref[:, part].astype(jnp.float32),
+            -1,
+            keepdims=True,
+        )
+        scores = lax.dot_general(
+            queries, keys, contract_columns, preferred_element_type=jnp.float32
+        )
+        weights = jnp.exp2(scores * EXPONENT - log_ref[:, head : head + 1])
+        grad_weights = lax.dot_general(
+            grad_out, values, contract_columns, preferred_element_type=jnp.float32
+        )
+        grad_scores = (weights * (grad_weights - inner)).astype(jnp.bfloat16)
+        grad_queries = jnp.dot(grad_scores, keys, preferred_element_type=jnp.float32)
+        grad_keys = lax.dot_general(
+            grad_scores, queries, contract_rows, preferred_element_type=jnp.float32
+        )
+        grad_values = lax.dot_general(
+            weights.astype(jnp.bfloat16),
+            grad_out,
+            contract_rows,
+            preferred_element_type=jnp.float32,
+        )
+        result_ref[:, base : base + HEAD_DIM] = (grad_queries * SCALE).astype(jnp.bfloat16)
+        result_ref[:, base + HEAD_DIM : base + 2 * HEAD_DIM] = (grad_keys * SCALE).astype(
             jnp.bfloat16
         )
-        result_ref[:, base + 2 * HEAD_DIM : base + 3 * HEAD_DIM] = value_acc[...].astype(
+        result_ref[:, base + 2 * HEAD_DIM : base + 3 * HEAD_DIM] = grad_values.astype(
             jnp.bfloat16
         )
 
@@ -308,12 +280,8 @@
 def attend_back(columns, output, logsum, grad_output, heads):
     rows = columns.shape[0]
     return pl.pallas_call(
-        functools.partial(attend_back_kernel, heads, row_block(rows)),
+        functools.partial(attend_back_kernel, heads),
         out_shape=jax.ShapeDtypeStruct(columns.shape, jnp.bfloat16),
-        scratch_shapes=[
-            pltpu.VMEM((rows, HEAD_DIM), jnp.float32),
-            pltpu.VMEM((rows, HEAD_DIM), jnp.float32),
-        ],
         cost_estimate=pl.CostEstimate(
             flops=heads * rows * rows * HEAD_DIM * 10,
             bytes_accessed=columns.size * 6,
@@ -487,9 +455,8 @@
     hidden_sums = [jnp.sum(grad_preact[stream], 0, dtype=jnp.float32) for stream in range(2)]
     summed, started = scatter_streams(grad_preact, weights[2])
     behind = after(grad_preact, started)
-    grad_expansion = weight_grads(
-        [(joined_feed[stream], behind[stream], 0) for stream in range(2)]
-    )
+    factors = [(joined_feed[stream], behind[stream], 0) for stream in range(2)]
+    grad_expansion = weight_grads(factors)
     summed = after(summed, grad_expansion)
     grad_expansion = scatter_weights(grad_expansion)
     grad_middle, shift_feed, scale_feed = ([], [], [])
@@ -519,25 +486,22 @@
     ]
     text_place = split // attend_rows[1].shape[0]
 
-    def attention_grads(behind):
-        return weight_grads(
-            [
-                (attend_rows[0], attended, 0),
-                (attend_rows[1], attended, text_place),
-                (joined[0], behind, 0),
-                (joined[1], behind, text_place),
-            ]
-        )
+    def factors(columns):
+        return [
+            (attend_rows[0], attended, 0),
+            (attend_rows[1], attended, text_place),
+            (joined[0], columns, 0),
+            (joined[1], columns, text_place),
+        ]
 
     if pending:
-        grad_attention = attention_grads(grad_columns)
+        grad_attention = weight_grads(factors(grad_columns))
         column_rows = after(column_rows, grad_attention)
         summed, _ = scatter_streams(column_rows, weights[0])
     else:
         summed, started = scatter_streams(column_rows, weights[0])
-        grad_attention = attention_grads(after(grad_columns, started))
+        grad_attention = weight_grads(factors(after(grad_columns, started)))
         summed = after(summed, grad_attention)
-    computed = grad_attention
     grad_attention = scatter_weights(grad_attention)
     tensor_rank = lax.axis_index("tensor")
     width_local = heads_local * HEAD_DIM
@@ -588,7 +552,6 @@
         new_grads,
         layer_grads,
         pending,
-        computed,
         jnp.stack(bias_grads),
         jnp.stack(slot_grads),
     )
@@ -691,22 +654,21 @@
         owned_rows,
         precision=highest,
     )
-    weight_store, bias_store, slot_store, modulation_store, pending = ([], [], [], [], ())
+    weight_store, bias_store, slot_store, pending = ([], [], [], ())
     for tier in reversed(range(LAYERS)):
         weights, shifts, record = stored[tier]
-        gradients, layer_grads, pending, computed, bias_part, slot_grads = backward_layer(
+        gradients, layer_grads, pending, bias_part, slot_grads = backward_layer(
             gradients, record, weights, shifts, heads_local, pending
         )
         weight_store.insert(0, layer_grads)
         bias_store.insert(0, bias_part)
         slot_store.insert(0, slot_grads)
-    slot_store[1:], bias_store[1:] = after((slot_store[1:], bias_store[1:]), computed)
-    for slot_grads in slot_store:
-        modulation_store.append(
-            jnp.dot(slot_rows.T, gather_slots(slot_grads), precision=highest)
-            .reshape(shard_rows, 2, -1)
-            .transpose(1, 0, 2)
-        )
+    slot_sums = gather_slots(jnp.stack(slot_store, axis=1))
+    modulation_grad = (
+        jnp.dot(slot_rows.T, slot_sums, precision=highest)
+        .reshape(shard_rows, 2, LAYERS, -1)
+        .transpose(2, 1, 0, 3)
+    )
     stacked = [
         jnp.stack([entry[kind] for entry in weight_store]) for kind in range(4)
     ]
@@ -720,7 +682,7 @@
         stacked[1],
         stacked[2],
         stacked[3],
-        jnp.stack(modulation_store),
+        modulation_grad,
         biases_grad,
     )
 

time: 1230 us -> 1210 us (0.984)
  Pallas kernels: 235 us -> 199 us
  waiting for transfers between devices: 419 us -> 439 us
  local copies, waits for them, and re-layouts: 95.8 us -> 114 us
    pallas_call x4, Pallas kernels: 122 us -> 85.7 us  [the longest x2 56.5 us: attend_back(): pl.pallas_call(functools.partial(attend_back_kernel, heads), out_shape=ja...]
    all_gather x6, waiting for transfers between devices: 41 us -> 66.6 us  [on_device(): lax.all_gather(matrix, 'dp', axis=1, tiled=True)]
    reshape x2, local copies, waits for them, and re-layouts: 2.28 us -> 20.2 us  [on_device(): modulation_grad = jnp.dot(slot_rows.T, slot_sums, precision=highest).resh...]
    ppermute x130 -> x117, starting transfers between devices: 153 us -> 140 us  [exchange(): lax.ppermute(values, axis, [(rank, rank ^ step) for rank in range(size)])]
    ppermute x130 -> x117, waiting for transfers between devices: 377 us -> 372 us  [exchange(): lax.ppermute(values, axis, [(rank, rank ^ step) for rank in range(size)])]
    unnamed x646 -> x582, local copies, waits for them, and re-layouts: 24 us -> 26.8 us
  transfers between devices with their start and end apart: 142 -> 129, of which waited for: 66 -> 63; matrix products, arithmetic and copies ran while one was open for 29% -> 31% of each run, Pallas kernels for 19% -> 17%
where the time goes in v5:
time: 1210 us; the launch traced here: 1200 us
  waiting for transfers between devices  439 us (36%)
  matrix products  204 us (17%)
  Pallas kernels  199 us (16%)
  starting transfers between devices  142 us (12%)
  local copies, waits for them, and re-layouts  114 us (9%)
  other arithmetic  84.5 us (7%)
  between operations  20.1 us (2%)
    ppermute x117, waiting for transfers between devices, exchange(): lax.ppermute(values, axis, [(rank, rank ^ step) for rank in range(size)])  372 us
    ppermute x117, starting transfers between devices, exchange(): lax.ppermute(values, axis, [(rank, rank ^ step) for rank in range(size)])  140 us
    dot_general x32, matrix products, product(): lax.dot_general(left[stream][start * counts[stream]:stop * counts[stream]...  96.1 us
    pallas_call x6, Pallas kernels, weight_grads(): pl.pallas_call(functools.partial(weight_grads_kernel, len(pairs)), grid=(...  77.2 us
    all_gather x6, waiting for transfers between devices, on_device(): lax.all_gather(matrix, 'dp', axis=1, tiled=True)  66.6 us
    pallas_call x2, Pallas kernels, attend_back(): pl.pallas_call(functools.partial(attend_back_kernel, heads), out_shape=ja...  56.5 us
    dot_general x4, matrix products, backward_layer(): jnp.dot(branch_rows[stream], feed_weights[stream], preferred_element_type...  32.4 us
    pallas_call x8, Pallas kernels, assemble(): pl.pallas_call(functools.partial(assemble_kernel, counts[0]), out_shape=[...  32.2 us
  transfers between devices with their start and end apart: 129, of which 63 were waited for; matrix products, arithmetic and copies ran while one was open for 31% of the time, Pallas kernels for 17%

profile of v5, /device:TPU:0, one launch (start us, length us, event | category | flops | bytes accessed | tf_op | source)
XLA Modules:
  0.0 1201.8 jit_solution(16974519490587454084)
XLA Ops:
  48.0 4.3 collective-permute-start.6
  54.1 4.5 concatenate.226
  63.9 4.7 collective-permute-done.24
  74.5 4.8 collective-permute-start.28
  112.6 17.2 %collective-permute-done.30.refs_1_ = bf16[288,1536]{1,0:T(8,128)(2,1)S(1)} collective-permute-done((bf16[288,1536]{1,0:T(8,128)(2,1)S(1)}, bf16[288,1536]{1,0:T(8,128)(2,1)S(1)}, u32[]{:S(2)}, u32[]{:S(2)}) %collective-permute-start.30) | collective-permute-done | bytes 884768 | tf_op jit(solution)/shard_map/ppermute | solution.py:41
  150.8 6.5 add_convert_fusion.1
  159.1 14.6 %attend.2 = (bf16[1152,384]{1,0:T(8,128)(2,1)}, f32[1152,128]{1,0:T(8,128)}) custom-call(bf16[1152,1152]{1,0:T(8,128)(2,1)} %pad_maximum_fusion.columns_ref), custom_call_target="tpu_custom_call" | custom-call | flops 2038431744 | bytes 3981312 | tf_op jit(solution)/shard_map/attend/pallas_call | solution.py:225
  182.3 6.8 collective-permute-done.36
  197.2 12.1 %collective-permute-done.37 = bf16[288,1536]{1,0:T(8,128)(2,1)S(1)} collective-permute-done((bf16[288,1536]{1,0:T(8,128)(2,1)S(1)}, bf16[288,1536]{1,0:T(8,128)(2,1)S(1)}, u32[]{:S(2)}, u32[]{:S(2)}) %collective-permute-start.37) | collective-permute-done | bytes 884768 | tf_op jit(solution)/shard_map/ppermute | solution.py:41
  214.3 16.9 %collective-permute-done.38.refs_1_ = bf16[288,1536]{1,0:T(8,128)(2,1)S(1)} collective-permute-done((bf16[288,1536]{1,0:T(8,128)(2,1)S(1)}, bf16[288,1536]{1,0:T(8,128)(2,1)S(1)}, u32[]{:S(2)}, u32[]{:S(2)}) %collective-permute-start.38) | collective-permute-done | bytes 884768 | tf_op jit(solution)/shard_map/ppermute | solution.py:41
  236.4 4.7 collective-permute-done.40.refs_3_
  246.7 11.6 multiply_convert_fusion.1
  258.3 40.6 %all-gather.17.cloned.1.call-done = bf16[1,2,1536,1536]{3,2,1,0:T(8,128)(2,1)} async-done(((bf16[1,2,192,1536]{3,2,1,0:T(8,128)(2,1)}), bf16[1,2,1536,1536]{3,2,1,0:T(8,128)(2,1)}) %all-gather.17.cloned.1.call-update) | async-done | bytes 9437200 | tf_op jit(solution)/shard_map/all_gather | solution.py:630
  299.0 5.6 fusion.57
  316.6 9.3 collective-permute-done.44
  334.3 13.0 %collective-permute-done.45 = bf16[288,1536]{1,0:T(8,128)(2,1)} collective-permute-done((bf16[288,1536]{1,0:T(8,128)(2,1)S(1)}, bf16[288,1536]{1,0:T(8,128)(2,1)}, u32[]{:S(2)}, u32[]{:S(2)}) %collective-permute-start.45) | collective-permute-done | bytes 884768 | tf_op jit(solution)/shard_map/ppermute | solution.py:41
  358.2 16.4 %collective-permute-done.46.refs_1_ = bf16[288,1536]{1,0:T(8,128)(2,1)} collective-permute-done((bf16[288,1536]{1,0:T(8,128)(2,1)S(1)}, bf16[288,1536]{1,0:T(8,128)(2,1)}, u32[]{:S(2)}, u32[]{:S(2)}) %collective-permute-start.46) | collective-permute-done | bytes 884768 | tf_op jit(solution)/shard_map/ppermute | solution.py:41
  380.0 5.4 collective-permute-done.48.refs_3_
  387.1 4.2 assemble.10
  394.3 6.9 add_convert_fusion
  403.0 14.6 %attend.3 = (bf16[1152,384]{1,0:T(8,128)(2,1)}, f32[1152,128]{1,0:T(8,128)}) custom-call(bf16[1152,1152]{1,0:T(8,128)(2,1)} %pad_maximum_fusion.1.columns_ref), custom_call_target="tpu_custom_call" | custom-call | flops 2038431744 | bytes 3981312 | tf_op jit(solution)/shard_map/attend/pallas_call | solution.py:225
  426.6 7.9 collective-permute-done.52
  441.8 15.6 %collective-permute-done.53 = bf16[288,1536]{1,0:T(8,128)(2,1)S(1)} collective-permute-done((bf16[288,1536]{1,0:T(8,128)(2,1)S(1)}, bf16[288,1536]{1,0:T(8,128)(2,1)S(1)}, u32[]{:S(2)}, u32[]{:S(2)}) %collective-permute-start.53) | collective-permute-done | bytes 884768 | tf_op jit(solution)/shard_map/ppermute | solution.py:41
  464.1 14.0 %collective-permute-done.62.refs_1_ = bf16[288,1536]{1,0:T(8,128)(2,1)S(1)} collective-permute-done((bf16[288,1536]{1,0:T(8,128)(2,1)S(1)}, bf16[288,1536]{1,0:T(8,128)(2,1)S(1)}, u32[]{:S(2)}, u32[]{:S(2)}) %collective-permute-start.62) | collective-permute-done | bytes 884768 | tf_op jit(solution)/shard_map/ppermute | solution.py:41
  480.3 16.7 %collective-permute-done.54.refs_1_ = bf16[288,1536]{1,0:T(8,128)(2,1)S(1)} collective-permute-done((bf16[288,1536]{1,0:T(8,128)(2,1)S(1)}, bf16[288,1536]{1,0:T(8,128)(2,1)S(1)}, u32[]{:S(2)}, u32[]{:S(2)}) %collective-permute-start.54) | collective-permute-done | bytes 884768 | tf_op jit(solution)/shard_map/ppermute | solution.py:41
  516.9 4.6 multiply_convert_fusion.6
  521.4 10.8 multiply_convert_fusion
  532.3 12.6 %weight_grads.6 = bf16[1536,3072]{1,0:T(8,128)(2,1)} custom-call(bf16[1024,1536]{1,0:T(8,128)(2,1)} %get-tuple-element.77.refs_0_, bf16[1024,1536]{1,0:T(8,128)(2,1)} %get-tuple-element.424.refs_1_, bf16[128,1536]{1,0:T(8,128)(2,1)} %get-tuple-element.79.refs_2_, bf16[128,1536]{1,0:T(8,128)(2,1)} %get-tuple-element.426.refs_3_), custom_call_target="tpu_custom_call" | custom-call | flops 5435817984 | bytes 16515072 | tf_op jit(solution)/shard_map/weight_grads/pallas_call | solution.py:398
  545.2 25.9 %all-gather.21.cloned.1.call-done = bf16[1,2,1536,1536]{3,2,1,0:T(8,128)(2,1)} async-done(((bf16[1,2,192,1536]{3,2,1,0:T(8,128)(2,1)}), bf16[1,2,1536,1536]{3,2,1,0:T(8,128)(2,1)}) %all-gather.21.cloned.1.call-update) | async-done | bytes 9437200 | tf_op jit(solution)/shard_map/all_gather | solution.py:630
  571.1 4.6 convert_reduce_fusion.5
  575.7 4.7 fusion.72
  581.1 11.5 convert_reduce_fusion
  598.6 12.5 %weight_grads.7 = bf16[1536,3072]{1,0:T(8,128)(2,1)} custom-call(bf16[1024,1536]{1,0:T(8,128)(2,1)} %get-tuple-element.72.refs_0_, bf16[1024,1536]{1,0:T(8,128)(2,1)} %copy-done.251, bf16[128,1536]{1,0:T(8,128)(2,1)} %get-tuple-element.73.refs_2_, bf16[128,1536]{1,0:T(8,128)(2,1)} %copy-done.255), custom_call_target="tpu_custom_call" | custom-call | flops 5435817984 | bytes 16515072 | tf_op jit(solution)/shard_map/weight_grads/pallas_call | solution.py:398
  615.7 5.8 fusion.56
  640.1 17.5 %collective-permute-done.69 = bf16[288,1536]{1,0:T(8,128)(2,1)S(1)} collective-permute-done((bf16[288,1536]{1,0:T(8,128)(2,1)S(1)}, bf16[288,1536]{1,0:T(8,128)(2,1)S(1)}, u32[]{:S(2)}, u32[]{:S(2)}) %collective-permute-start.69) | collective-permute-done | bytes 884768 | tf_op jit(solution)/shard_map/ppermute | solution.py:41
  661.3 13.6 %collective-permute-done.61 = bf16[288,1536]{1,0:T(8,128)(2,1)S(1)} collective-permute-done((bf16[288,1536]{1,0:T(8,128)(2,1)S(1)}, bf16[288,1536]{1,0:T(8,128)(2,1)S(1)}, u32[]{:S(2)}, u32[]{:S(2)}) %collective-permute-start.61) | collective-permute-done | bytes 884768 | tf_op jit(solution)/shard_map/ppermute | solution.py:41
  682.3 18.5 %collective-permute-done.70.refs_1_ = bf16[288,1536]{1,0:T(8,128)(2,1)S(1)} collective-permute-done((bf16[288,1536]{1,0:T(8,128)(2,1)S(1)}, bf16[288,1536]{1,0:T(8,128)(2,1)S(1)}, u32[]{:S(2)}, u32[]{:S(2)}) %collective-permute-start.70) | collective-permute-done | bytes 884768 | tf_op jit(solution)/shard_map/ppermute | solution.py:41
  703.6 8.0 collective-permute-done.72.refs_3_
  718.5 4.2 convolution_convert_fusion.15
  723.6 28.4 %attend_back.2.refs_5_.refs_7_ = bf16[1152,1152]{1,0:T(8,128)(2,1)} custom-call(bf16[1152,1152]{1,0:T(8,128)(2,1)} %pad_maximum_fusion.1.columns_ref, bf16[1152,384]{1,0:T(8,128)(2,1)} %get-tuple-element.70.out_ref.refs_1_.refs_3_, f32[1152,128]{1,0:T(8,128)} %get-tuple-element.86.log_ref, bf16[1152,384]{1,0:T(8,128)(2,1)} %pad_maximum_fusion.23.grad_ref), custom_call_target="tpu_custom_call" | custom-call | flops 5096079360 | bytes 7962624 | tf_op jit(solution)/shard_map/attend_back/pallas_call | solution.py:282
  760.4 4.3 convolution_convert_fusion.1
  764.7 13.4 %weight_grads.8 = bf16[1536,3072]{1,0:T(8,128)(2,1)} custom-call(bf16[1024,1536]{1,0:T(8,128)(2,1)} %get-tuple-element.88.refs_0_, bf16[1152,384]{1,0:T(8,128)(2,1)} %get-tuple-element.70.out_ref.refs_1_.refs_3_, bf16[128,1536]{1,0:T(8,128)(2,1)} %get-tuple-element.89.refs_2_, bf16[1152,384]{1,0:T(8,128)(2,1)} %get-tuple-element.70.out_ref.refs_1_.refs_3_, ...), custom_call_target="tpu_custom_call" | custom-call | flops 5435817984 | bytes 20054016 | tf_op jit(solution)/shard_map/weight_grads/pallas_call | solution.py:398
  782.1 5.7 collective-permute-done.76
  795.4 12.4 %collective-permute-done.77 = bf16[288,1536]{1,0:T(8,128)(2,1)S(1)} collective-permute-done((bf16[288,1536]{1,0:T(8,128)(2,1)S(1)}, bf16[288,1536]{1,0:T(8,128)(2,1)S(1)}, u32[]{:S(2)}, u32[]{:S(2)}) %collective-permute-start.77) | collective-permute-done | bytes 884768 | tf_op jit(solution)/shard_map/ppermute | solution.py:41
  818.0 17.4 %collective-permute-done.78.refs_1_ = bf16[288,1536]{1,0:T(8,128)(2,1)S(1)} collective-permute-done((bf16[288,1536]{1,0:T(8,128)(2,1)S(1)}, bf16[288,1536]{1,0:T(8,128)(2,1)S(1)}, u32[]{:S(2)}, u32[]{:S(2)}) %collective-permute-start.78) | collective-permute-done | bytes 884768 | tf_op jit(solution)/shard_map/ppermute | solution.py:41
  839.4 4.8 collective-permute-done.80.refs_3_
  849.7 12.6 %weight_grads.9 = bf16[1536,3072]{1,0:T(8,128)(2,1)} custom-call(bf16[1024,1536]{1,0:T(8,128)(2,1)} %get-tuple-element.96.refs_0_, bf16[1024,1536]{1,0:T(8,128)(2,1)} %get-tuple-element.422.refs_1_, bf16[128,1536]{1,0:T(8,128)(2,1)} %get-tuple-element.98.refs_2_, bf16[128,1536]{1,0:T(8,128)(2,1)} %copy-done.252), custom_call_target="tpu_custom_call" | custom-call | flops 5435817984 | bytes 16515072 | tf_op jit(solution)/shard_map/weight_grads/pallas_call | solution.py:398
  868.8 4.5 convert_reduce_fusion.6
  877.5 11.8 convert_reduce_fusion.1
  893.6 12.6 %weight_grads.10 = bf16[1536,3072]{1,0:T(8,128)(2,1)} custom-call(bf16[1024,1536]{1,0:T(8,128)(2,1)} %get-tuple-element.65.refs_0_, bf16[1024,1536]{1,0:T(8,128)(2,1)} %copy-done.250, bf16[128,1536]{1,0:T(8,128)(2,1)} %get-tuple-element.66.refs_2_, bf16[128,1536]{1,0:T(8,128)(2,1)} %copy-done.254), custom_call_target="tpu_custom_call" | custom-call | flops 5435817984 | bytes 16515072 | tf_op jit(solution)/shard_map/weight_grads/pallas_call | solution.py:398
  912.2 5.0 collective-permute-done.84
  927.7 9.7 collective-permute-done.85
  957.5 11.5 collective-permute-done.86.refs_1_
  990.9 28.1 %attend_back.3.refs_5_.refs_7_ = bf16[1152,1152]{1,0:T(8,128)(2,1)} custom-call(bf16[1152,1152]{1,0:T(8,128)(2,1)} %pad_maximum_fusion.columns_ref, bf16[1152,384]{1,0:T(8,128)(2,1)} %get-tuple-element.63.out_ref.refs_1_.refs_3_, f32[1152,128]{1,0:T(8,128)} %get-tuple-element.105.log_ref, bf16[1152,384]{1,0:T(8,128)(2,1)} %pad_maximum_fusion.28.grad_ref), custom_call_target="tpu_custom_call" | custom-call | flops 5096079360 | bytes 7962624 | tf_op jit(solution)/shard_map/attend_back/pallas_call | solution.py:282
  1022.3 13.4 %weight_grads.11 = bf16[1536,3072]{1,0:T(8,128)(2,1)} custom-call(bf16[1024,1536]{1,0:T(8,128)(2,1)} %get-tuple-element.107.refs_0_, bf16[1152,384]{1,0:T(8,128)(2,1)} %get-tuple-element.63.out_ref.refs_1_.refs_3_, bf16[128,1536]{1,0:T(8,128)(2,1)} %get-tuple-element.108.refs_2_, bf16[1152,384]{1,0:T(8,128)(2,1)} %get-tuple-element.63.out_ref.refs_1_.refs_3_, ...), custom_call_target="tpu_custom_call" | custom-call | flops 5435817984 | bytes 20054016 | tf_op jit(solution)/shard_map/weight_grads/pallas_call | solution.py:398
  1035.7 4.6 convolution_convert_fusion
  1050.2 7.0 collective-permute-done.92
  1069.3 8.4 collective-permute-done.93
  1133.2 6.4 collective-permute-done.101
  1143.8 6.3 collective-permute-done.104
  1150.1 5.6 collective-permute-done.105
  1155.7 7.7 fusion.284
  1163.5 10.1 reshape.425
  1173.6 10.1 copy.36
  (1206 shorter events, 486.3 us)
Async XLA Ops:
  7.2 140.6 %all-gather.11.cloned.1.call-start = ((), (), s32[]{:S(2)}) async-start(), calls=%async_computation.6 | async-start | bytes 10616832 | tf_op jit(solution)/shard_map/all_gather | solution.py:630
  12.8 233.9 %all-gather.15.cloned.1.call-start = ((), (), s32[]{:S(2)}) async-start(), calls=%async_computation.14 | async-start | bytes 10616832 | tf_op jit(solution)/shard_map/all_gather | solution.py:630
  16.1 282.9 %all-gather.17.cloned.1.call-start = ((), (), s32[]{:S(2)}) async-start(), calls=%async_computation.15 | async-start | bytes 10616832 | tf_op jit(solution)/shard_map/all_gather | solution.py:630
  19.4 371.9 %all-gather.13.cloned.1.call-start = ((), (), s32[]{:S(2)}) async-start(), calls=%async_computation.7 | async-start | bytes 10616832 | tf_op jit(solution)/shard_map/all_gather | solution.py:630
  21.9 494.9 %all-gather.19.cloned.1.call-start = ((), (), s32[]{:S(2)}) async-start(), calls=%async_computation.16 | async-start | bytes 10616832 | tf_op jit(solution)/shard_map/all_gather | solution.py:630
  22.0 17.6 %collective-permute-start = (s32[1]{0:T(128)}, s32[1]{0:T(128)}, u32[]{:S(2)}, u32[]{:S(2)}) collective-permute-start(s32[1]{0:T(128)} %param.16), channel_id=1, source_target_pairs={{0,4},{4,0},{8,12},{12,8},{16,20},{20,16},{24,28},{28,24},{1,5},{5... | collective-permute-start | bytes 20 | tf_op jit(solution)/shard_map/ppermute | solution.py:41
  22.5 17.1 %collective-permute-start.1 = (s32[1]{0:T(128)}, s32[1]{0:T(128)}, u32[]{:S(2)}, u32[]{:S(2)}) collective-permute-start(s32[1]{0:T(128)} %param.16), channel_id=1, source_target_pairs={{0,8},{4,12},{8,0},{12,4},{16,24},{20,28},{24,16},{28,20},{1,9},{5... | collective-permute-start | bytes 20 | tf_op jit(solution)/shard_map/ppermute | solution.py:41
  25.2 33.5 %collective-permute-start.22 = (bf16[1,4,672]{2,1,0:T(4,128)(2,1)S(1)}, bf16[1,4,672]{2,1,0:T(4,128)(2,1)}, u32[]{:S(2)}, u32[]{:S(2)}) collective-permute-start(bf16[1,4,672]{2,1,0:T(4,128)(2,1)S(1)} %reshape.421), channel_id=1, source_target_pairs={{0,3},{1,2},{2,1},{3,0},{4,7},{5,6},{6,5},{7,4},{8,11},{9,10},{10,... | collective-permute-start | bytes 16136 | tf_op jit(solution)/shard_map/ppermute | solution.py:41
  27.7 32.7 %collective-permute-start.21 = (bf16[1,4,672]{2,1,0:T(4,128)(2,1)S(1)}, bf16[1,4,672]{2,1,0:T(4,128)(2,1)}, u32[]{:S(2)}, u32[]{:S(2)}) collective-permute-start(bf16[1,4,672]{2,1,0:T(4,128)(2,1)S(1)} %reshape.421), channel_id=1, source_target_pairs={{0,2},{1,3},{2,0},{3,1},{4,6},{5,7},{6,4},{7,5},{8,10},{9,11},{10,... | collective-permute-start | bytes 16136 | tf_op jit(solution)/shard_map/ppermute | solution.py:41
  28.2 32.2 %collective-permute-start.20 = (bf16[1,4,672]{2,1,0:T(4,128)(2,1)S(1)}, bf16[1,4,672]{2,1,0:T(4,128)(2,1)}, u32[]{:S(2)}, u32[]{:S(2)}) collective-permute-start(bf16[1,4,672]{2,1,0:T(4,128)(2,1)S(1)} %reshape.421), channel_id=1, source_target_pairs={{0,1},{1,0},{2,3},{3,2},{4,5},{5,4},{6,7},{7,6},{8,9},{9,8},{10,11... | collective-permute-start | bytes 16136 | tf_op jit(solution)/shard_map/ppermute | solution.py:41
  52.2 27.9 %collective-permute-start.9 = (f32[6,9216]{1,0:T(8,128)S(1)}, f32[6,9216]{1,0:T(8,128)S(1)}, u32[]{:S(2)}, u32[]{:S(2)}) collective-permute-start(f32[6,9216]{1,0:T(8,128)S(1)} %get-tuple-element.292), channel_id=1, source_target_pairs={{0,3},{1,2},{2,1},{3,0},{4,7},{5,6},{6,5},{7,4},{8,11},{9,10},{10,... | collective-permute-start | bytes 663560 | tf_op jit(solution)/shard_map/ppermute | solution.py:41
  53.7 26.5 %collective-permute-start.8 = (f32[6,9216]{1,0:T(8,128)S(1)}, f32[6,9216]{1,0:T(8,128)S(1)}, u32[]{:S(2)}, u32[]{:S(2)}) collective-permute-start(f32[6,9216]{1,0:T(8,128)S(1)} %get-tuple-element.293), channel_id=1, source_target_pairs={{0,2},{1,3},{2,0},{3,1},{4,6},{5,7},{6,4},{7,5},{8,10},{9,11},{10,... | collective-permute-start | bytes 663560 | tf_op jit(solution)/shard_map/ppermute | solution.py:41
  58.6 21.5 %collective-permute-start.7 = (f32[6,9216]{1,0:T(8,128)S(1)}, f32[6,9216]{1,0:T(8,128)S(1)}, u32[]{:S(2)}, u32[]{:S(2)}) collective-permute-start(f32[6,9216]{1,0:T(8,128)S(1)} %get-tuple-element.291), channel_id=1, source_target_pairs={{0,1},{1,0},{2,3},{3,2},{4,5},{5,4},{6,7},{7,6},{8,9},{9,8},{10,11... | collective-permute-start | bytes 663560 | tf_op jit(solution)/shard_map/ppermute | solution.py:41
  109.0 20.9 %collective-permute-start.30 = (bf16[288,1536]{1,0:T(8,128)(2,1)S(1)}, bf16[288,1536]{1,0:T(8,128)(2,1)S(1)}, u32[]{:S(2)}, u32[]{:S(2)}) collective-permute-start(bf16[288,1536]{1,0:T(8,128)(2,1)S(1)} %pad_maximum_fusion.12.refs_0_), channel_id=1, source_target_pairs={{0,1},{1,0},{2,3},{3,2},{4,5},{5,4},{6,7},{7,6},{8,9},{9,8},{10,11... | collective-permute-start | bytes 2654216 | tf_op jit(solution)/shard_map/ppermute | solution.py:41
  110.3 21.3 %collective-permute-start.31 = (bf16[288,1536]{1,0:T(8,128)(2,1)S(1)}, bf16[288,1536]{1,0:T(8,128)(2,1)}, u32[]{:S(2)}, u32[]{:S(2)}) collective-permute-start(bf16[288,1536]{1,0:T(8,128)(2,1)S(1)} %pad_maximum_fusion.12.refs_0_), channel_id=1, source_target_pairs={{0,2},{1,3},{2,0},{3,1},{4,6},{5,7},{6,4},{7,5},{8,10},{9,11},{10,... | collective-permute-start | bytes 2654216 | tf_op jit(solution)/shard_map/ppermute | solution.py:41
  112.0 459.0 %all-gather.21.cloned.1.call-start = ((), (), s32[]{:S(2)}) async-start(), calls=%async_computation.17 | async-start | bytes 10616832 | tf_op jit(solution)/shard_map/all_gather | solution.py:630
  189.3 20.0 %collective-permute-start.37 = (bf16[288,1536]{1,0:T(8,128)(2,1)S(1)}, bf16[288,1536]{1,0:T(8,128)(2,1)S(1)}, u32[]{:S(2)}, u32[]{:S(2)}) collective-permute-start(bf16[288,1536]{1,0:T(8,128)(2,1)S(1)} %fusion.107), channel_id=1, source_target_pairs={{0,2},{1,3},{2,0},{3,1},{4,6},{5,7},{6,4},{7,5},{8,10},{9,11},{10,... | collective-permute-start | bytes 2654216 | tf_op jit(solution)/shard_map/ppermute | solution.py:41
  192.6 16.7 %collective-permute-start.35 = (bf16[288,1536]{1,0:T(8,128)(2,1)S(1)}, bf16[288,1536]{1,0:T(8,128)(2,1)S(1)}, u32[]{:S(2)}, u32[]{:S(2)}) collective-permute-start(bf16[288,1536]{1,0:T(8,128)(2,1)S(1)} %pad_maximum_fusion.13), channel_id=1, source_target_pairs={{0,1},{1,0},{2,3},{3,2},{4,5},{5,4},{6,7},{7,6},{8,9},{9,8},{10,11... | collective-permute-start | bytes 2654216 | tf_op jit(solution)/shard_map/ppermute | solution.py:41
  212.1 19.1 %collective-permute-start.38 = (bf16[288,1536]{1,0:T(8,128)(2,1)S(1)}, bf16[288,1536]{1,0:T(8,128)(2,1)S(1)}, u32[]{:S(2)}, u32[]{:S(2)}) collective-permute-start(bf16[288,1536]{1,0:T(8,128)(2,1)S(1)} %pad_maximum_fusion.14.refs_0_), channel_id=1, source_target_pairs={{0,1},{1,0},{2,3},{3,2},{4,5},{5,4},{6,7},{7,6},{8,9},{9,8},{10,11... | collective-permute-start | bytes 2654216 | tf_op jit(solution)/shard_map/ppermute | solution.py:41
  212.7 20.0 %collective-permute-start.39 = (bf16[288,1536]{1,0:T(8,128)(2,1)S(1)}, bf16[288,1536]{1,0:T(8,128)(2,1)S(1)}, u32[]{:S(2)}, u32[]{:S(2)}) collective-permute-start(bf16[288,1536]{1,0:T(8,128)(2,1)S(1)} %pad_maximum_fusion.14.refs_0_), channel_id=1, source_target_pairs={{0,2},{1,3},{2,0},{3,1},{4,6},{5,7},{6,4},{7,5},{8,10},{9,11},{10,... | collective-permute-start | bytes 2654216 | tf_op jit(solution)/shard_map/ppermute | solution.py:41
  326.0 21.3 %collective-permute-start.45 = (bf16[288,1536]{1,0:T(8,128)(2,1)S(1)}, bf16[288,1536]{1,0:T(8,128)(2,1)}, u32[]{:S(2)}, u32[]{:S(2)}) collective-permute-start(bf16[288,1536]{1,0:T(8,128)(2,1)S(1)} %fusion.109), channel_id=1, source_target_pairs={{0,2},{1,3},{2,0},{3,1},{4,6},{5,7},{6,4},{7,5},{8,10},{9,11},{10,... | collective-permute-start | bytes 2654216 | tf_op jit(solution)/shard_map/ppermute | solution.py:41
  328.6 21.2 %collective-permute-start.43 = (bf16[288,1536]{1,0:T(8,128)(2,1)}, bf16[288,1536]{1,0:T(8,128)(2,1)}, u32[]{:S(2)}, u32[]{:S(2)}) collective-permute-start(bf16[288,1536]{1,0:T(8,128)(2,1)} %pad_maximum_fusion.15), channel_id=1, source_target_pairs={{0,1},{1,0},{2,3},{3,2},{4,5},{5,4},{6,7},{7,6},{8,9},{9,8},{10,11... | collective-permute-start | bytes 2654216 | tf_op jit(solution)/shard_map/ppermute | solution.py:41
  330.1 538.6 %reduce-scatter.7.cloned.1.call-start = ((), (), s32[]{:S(2)}) async-start(), calls=%async_computation.8 | async-start | bytes 10616832 | tf_op jit(solution)/shard_map/reduce_scatter | solution.py:412
  354.6 20.1 %collective-permute-start.46 = (bf16[288,1536]{1,0:T(8,128)(2,1)S(1)}, bf16[288,1536]{1,0:T(8,128)(2,1)}, u32[]{:S(2)}, u32[]{:S(2)}) collective-permute-start(bf16[288,1536]{1,0:T(8,128)(2,1)S(1)} %pad_maximum_fusion.16.refs_0_), channel_id=1, source_target_pairs={{0,1},{1,0},{2,3},{3,2},{4,5},{5,4},{6,7},{7,6},{8,9},{9,8},{10,11... | collective-permute-start | bytes 2654216 | tf_op jit(solution)/shard_map/ppermute | solution.py:41
  356.1 20.6 %collective-permute-start.47 = (bf16[288,1536]{1,0:T(8,128)(2,1)S(1)}, bf16[288,1536]{1,0:T(8,128)(2,1)}, u32[]{:S(2)}, u32[]{:S(2)}) collective-permute-start(bf16[288,1536]{1,0:T(8,128)(2,1)S(1)} %pad_maximum_fusion.16.refs_0_), channel_id=1, source_target_pairs={{0,2},{1,3},{2,0},{3,1},{4,6},{5,7},{6,4},{7,5},{8,10},{9,11},{10,... | collective-permute-start | bytes 2654216 | tf_op jit(solution)/shard_map/ppermute | solution.py:41
  434.7 22.7 %collective-permute-start.53 = (bf16[288,1536]{1,0:T(8,128)(2,1)S(1)}, bf16[288,1536]{1,0:T(8,128)(2,1)S(1)}, u32[]{:S(2)}, u32[]{:S(2)}) collective-permute-start(bf16[288,1536]{1,0:T(8,128)(2,1)S(1)} %fusion.111), channel_id=1, source_target_pairs={{0,2},{1,3},{2,0},{3,1},{4,6},{5,7},{6,4},{7,5},{8,10},{9,11},{10,... | collective-permute-start | bytes 2654216 | tf_op jit(solution)/shard_map/ppermute | solution.py:41
  436.4 22.7 %collective-permute-start.51 = (bf16[288,1536]{1,0:T(8,128)(2,1)S(1)}, bf16[288,1536]{1,0:T(8,128)(2,1)S(1)}, u32[]{:S(2)}, u32[]{:S(2)}) collective-permute-start(bf16[288,1536]{1,0:T(8,128)(2,1)S(1)} %pad_maximum_fusion.17), channel_id=1, source_target_pairs={{0,1},{1,0},{2,3},{3,2},{4,5},{5,4},{6,7},{7,6},{8,9},{9,8},{10,11... | collective-permute-start | bytes 2654216 | tf_op jit(solution)/shard_map/ppermute | solution.py:41
  438.1 39.9 %collective-permute-start.62 = (bf16[288,1536]{1,0:T(8,128)(2,1)S(1)}, bf16[288,1536]{1,0:T(8,128)(2,1)S(1)}, u32[]{:S(2)}, u32[]{:S(2)}) collective-permute-start(bf16[288,1536]{1,0:T(8,128)(2,1)S(1)} %pad_maximum_fusion.20.refs_0_), channel_id=1, source_target_pairs={{0,1},{1,0},{2,3},{3,2},{4,5},{5,4},{6,7},{7,6},{8,9},{9,8},{10,11... | collective-permute-start | bytes 2654216 | tf_op jit(solution)/shard_map/ppermute | solution.py:41
  439.1 40.3 %collective-permute-start.63 = (bf16[288,1536]{1,0:T(8,128)(2,1)S(1)}, bf16[288,1536]{1,0:T(8,128)(2,1)S(1)}, u32[]{:S(2)}, u32[]{:S(2)}) collective-permute-start(bf16[288,1536]{1,0:T(8,128)(2,1)S(1)} %pad_maximum_fusion.20.refs_0_), channel_id=1, source_target_pairs={{0,2},{1,3},{2,0},{3,1},{4,6},{5,7},{6,4},{7,5},{8,10},{9,11},{10,... | collective-permute-start | bytes 2654216 | tf_op jit(solution)/shard_map/ppermute | solution.py:41
  462.0 35.0 %collective-permute-start.54 = (bf16[288,1536]{1,0:T(8,128)(2,1)S(1)}, bf16[288,1536]{1,0:T(8,128)(2,1)S(1)}, u32[]{:S(2)}, u32[]{:S(2)}) collective-permute-start(bf16[288,1536]{1,0:T(8,128)(2,1)S(1)} %pad_maximum_fusion.18.refs_0_), channel_id=1, source_target_pairs={{0,1},{1,0},{2,3},{3,2},{4,5},{5,4},{6,7},{7,6},{8,9},{9,8},{10,11... | collective-permute-start | bytes 2654216 | tf_op jit(solution)/shard_map/ppermute | solution.py:41
  463.6 35.5 %collective-permute-start.55 = (bf16[288,1536]{1,0:T(8,128)(2,1)S(1)}, bf16[288,1536]{1,0:T(8,128)(2,1)S(1)}, u32[]{:S(2)}, u32[]{:S(2)}) collective-permute-start(bf16[288,1536]{1,0:T(8,128)(2,1)S(1)} %pad_maximum_fusion.18.refs_0_), channel_id=1, source_target_pairs={{0,2},{1,3},{2,0},{3,1},{4,6},{5,7},{6,4},{7,5},{8,10},{9,11},{10,... | collective-permute-start | bytes 2654216 | tf_op jit(solution)/shard_map/ppermute | solution.py:41
  478.1 26.7 %collective-permute-start.64 = (bf16[144,1536]{1,0:T(8,128)(2,1)S(1)}, bf16[144,1536]{1,0:T(8,128)(2,1)S(1)}, u32[]{:S(2)}, u32[]{:S(2)}) collective-permute-start(bf16[144,1536]{1,0:T(8,128)(2,1)S(1)} %slice.1264), channel_id=1, source_target_pairs={{0,2},{1,3},{2,0},{3,1},{4,6},{5,7},{6,4},{7,5},{8,10},{9,11},{10,... | collective-permute-start | bytes 1327112 | tf_op jit(solution)/shard_map/ppermute | solution.py:41
  479.4 27.2 %collective-permute-start.65 = (bf16[144,1536]{1,0:T(8,128)(2,1)S(1)}, bf16[144,1536]{1,0:T(8,128)(2,1)}, u32[]{:S(2)}, u32[]{:S(2)}) collective-permute-start(bf16[144,1536]{1,0:T(8,128)(2,1)S(1)} %slice.1265), channel_id=1, source_target_pairs={{0,1},{1,0},{2,3},{3,2},{4,5},{5,4},{6,7},{7,6},{8,9},{9,8},{10,11... | collective-permute-start | bytes 1327112 | tf_op jit(solution)/shard_map/ppermute | solution.py:41
  497.8 13.8 %collective-permute-start.56 = (bf16[144,1536]{1,0:T(8,128)(2,1)}, bf16[144,1536]{1,0:T(8,128)(2,1)}, u32[]{:S(2)}, u32[]{:S(2)}) collective-permute-start(bf16[144,1536]{1,0:T(8,128)(2,1)} %slice.1243), channel_id=1, source_target_pairs={{0,2},{1,3},{2,0},{3,1},{4,6},{5,7},{6,4},{7,5},{8,10},{9,11},{10,... | collective-permute-start | bytes 1327112 | tf_op jit(solution)/shard_map/ppermute | solution.py:41
  544.9 380.4 %reduce-scatter.9.cloned.1.call-start = ((), (), s32[]{:S(2)}) async-start(), calls=%async_computation.9 | async-start | bytes 10616832 | tf_op jit(solution)/shard_map/reduce_scatter | solution.py:412
  611.2 327.8 %reduce-scatter.11.cloned.1.call-start = ((), (), s32[]{:S(2)}) async-start(), calls=%async_computation.10 | async-start | bytes 10616832 | tf_op jit(solution)/shard_map/reduce_scatter | solution.py:412
  613.0 17.7 %collective-permute-start.68 = (bf16[144,1536]{1,0:T(8,128)(2,1)S(1)}, bf16[144,1536]{1,0:T(8,128)(2,1)S(1)}, u32[]{:S(2)}, u32[]{:S(2)}) collective-permute-start(bf16[144,1536]{1,0:T(8,128)(2,1)S(1)} %get-tuple-element.301), channel_id=1, source_target_pairs={{0,1},{1,0},{2,3},{3,2},{4,5},{5,4},{6,7},{7,6},{8,9},{9,8},{10,11... | collective-permute-start | bytes 1327112 | tf_op jit(solution)/shard_map/ppermute | solution.py:41
  614.2 18.8 %collective-permute-start.66 = (bf16[144,1536]{1,0:T(8,128)(2,1)S(1)}, bf16[144,1536]{1,0:T(8,128)(2,1)S(1)}, u32[]{:S(2)}, u32[]{:S(2)}) collective-permute-start(bf16[144,1536]{1,0:T(8,128)(2,1)S(1)} %get-tuple-element.300), channel_id=1, source_target_pairs={{0,2},{1,3},{2,0},{3,1},{4,6},{5,7},{6,4},{7,5},{8,10},{9,11},{10,... | collective-permute-start | bytes 1327112 | tf_op jit(solution)/shard_map/ppermute | solution.py:41
  631.6 26.1 %collective-permute-start.69 = (bf16[288,1536]{1,0:T(8,128)(2,1)S(1)}, bf16[288,1536]{1,0:T(8,128)(2,1)S(1)}, u32[]{:S(2)}, u32[]{:S(2)}) collective-permute-start(bf16[288,1536]{1,0:T(8,128)(2,1)S(1)} %fusion.115), channel_id=1, source_target_pairs={{0,2},{1,3},{2,0},{3,1},{4,6},{5,7},{6,4},{7,5},{8,10},{9,11},{10,... | collective-permute-start | bytes 2654216 | tf_op jit(solution)/shard_map/ppermute | solution.py:41
  633.1 24.6 %collective-permute-start.67 = (bf16[288,1536]{1,0:T(8,128)(2,1)S(1)}, bf16[288,1536]{1,0:T(8,128)(2,1)S(1)}, u32[]{:S(2)}, u32[]{:S(2)}) collective-permute-start(bf16[288,1536]{1,0:T(8,128)(2,1)S(1)} %pad_maximum_fusion.21), channel_id=1, source_target_pairs={{0,1},{1,0},{2,3},{3,2},{4,5},{5,4},{6,7},{7,6},{8,9},{9,8},{10,11... | collective-permute-start | bytes 2654216 | tf_op jit(solution)/shard_map/ppermute | solution.py:41
  638.0 36.9 %collective-permute-start.61 = (bf16[288,1536]{1,0:T(8,128)(2,1)S(1)}, bf16[288,1536]{1,0:T(8,128)(2,1)S(1)}, u32[]{:S(2)}, u32[]{:S(2)}) collective-permute-start(bf16[288,1536]{1,0:T(8,128)(2,1)S(1)} %fusion.113), channel_id=1, source_target_pairs={{0,2},{1,3},{2,0},{3,1},{4,6},{5,7},{6,4},{7,5},{8,10},{9,11},{10,... | collective-permute-start | bytes 2654216 | tf_op jit(solution)/shard_map/ppermute | solution.py:41
  638.9 36.0 %collective-permute-start.59 = (bf16[288,1536]{1,0:T(8,128)(2,1)S(1)}, bf16[288,1536]{1,0:T(8,128)(2,1)S(1)}, u32[]{:S(2)}, u32[]{:S(2)}) collective-permute-start(bf16[288,1536]{1,0:T(8,128)(2,1)S(1)} %pad_maximum_fusion.19), channel_id=1, source_target_pairs={{0,1},{1,0},{2,3},{3,2},{4,5},{5,4},{6,7},{7,6},{8,9},{9,8},{10,11... | collective-permute-start | bytes 2654216 | tf_op jit(solution)/shard_map/ppermute | solution.py:41
  680.4 20.4 %collective-permute-start.70 = (bf16[288,1536]{1,0:T(8,128)(2,1)S(1)}, bf16[288,1536]{1,0:T(8,128)(2,1)S(1)}, u32[]{:S(2)}, u32[]{:S(2)}) collective-permute-start(bf16[288,1536]{1,0:T(8,128)(2,1)S(1)} %pad_maximum_fusion.22.refs_0_), channel_id=1, source_target_pairs={{0,1},{1,0},{2,3},{3,2},{4,5},{5,4},{6,7},{7,6},{8,9},{9,8},{10,11... | collective-permute-start | bytes 2654216 | tf_op jit(solution)/shard_map/ppermute | solution.py:41
  682.0 20.4 %collective-permute-start.71 = (bf16[288,1536]{1,0:T(8,128)(2,1)S(1)}, bf16[288,1536]{1,0:T(8,128)(2,1)S(1)}, u32[]{:S(2)}, u32[]{:S(2)}) collective-permute-start(bf16[288,1536]{1,0:T(8,128)(2,1)S(1)} %pad_maximum_fusion.22.refs_0_), channel_id=1, source_target_pairs={{0,2},{1,3},{2,0},{3,1},{4,6},{5,7},{6,4},{7,5},{8,10},{9,11},{10,... | collective-permute-start | bytes 2654216 | tf_op jit(solution)/shard_map/ppermute | solution.py:41
  778.2 324.6 %reduce-scatter.17.cloned.1.call-start = ((), (), s32[]{:S(2)}) async-start(), calls=%async_computation.13 | async-start | bytes 10616832 | tf_op jit(solution)/shard_map/reduce_scatter | solution.py:412
  788.0 19.9 %collective-permute-start.77 = (bf16[288,1536]{1,0:T(8,128)(2,1)S(1)}, bf16[288,1536]{1,0:T(8,128)(2,1)S(1)}, u32[]{:S(2)}, u32[]{:S(2)}) collective-permute-start(bf16[288,1536]{1,0:T(8,128)(2,1)S(1)} %fusion.117), channel_id=1, source_target_pairs={{0,2},{1,3},{2,0},{3,1},{4,6},{5,7},{6,4},{7,5},{8,10},{9,11},{10,... | collective-permute-start | bytes 2654216 | tf_op jit(solution)/shard_map/ppermute | solution.py:41
  791.9 15.9 %collective-permute-start.75 = (bf16[288,1536]{1,0:T(8,128)(2,1)S(1)}, bf16[288,1536]{1,0:T(8,128)(2,1)S(1)}, u32[]{:S(2)}, u32[]{:S(2)}) collective-permute-start(bf16[288,1536]{1,0:T(8,128)(2,1)S(1)} %pad_maximum_fusion.24), channel_id=1, source_target_pairs={{0,1},{1,0},{2,3},{3,2},{4,5},{5,4},{6,7},{7,6},{8,9},{9,8},{10,11... | collective-permute-start | bytes 2654216 | tf_op jit(solution)/shard_map/ppermute | solution.py:41
  815.9 19.5 %collective-permute-start.78 = (bf16[288,1536]{1,0:T(8,128)(2,1)S(1)}, bf16[288,1536]{1,0:T(8,128)(2,1)S(1)}, u32[]{:S(2)}, u32[]{:S(2)}) collective-permute-start(bf16[288,1536]{1,0:T(8,128)(2,1)S(1)} %pad_maximum_fusion.25.refs_0_), channel_id=1, source_target_pairs={{0,1},{1,0},{2,3},{3,2},{4,5},{5,4},{6,7},{7,6},{8,9},{9,8},{10,11... | collective-permute-start | bytes 2654216 | tf_op jit(solution)/shard_map/ppermute | solution.py:41
  816.7 18.9 %collective-permute-start.79 = (bf16[288,1536]{1,0:T(8,128)(2,1)S(1)}, bf16[288,1536]{1,0:T(8,128)(2,1)S(1)}, u32[]{:S(2)}, u32[]{:S(2)}) collective-permute-start(bf16[288,1536]{1,0:T(8,128)(2,1)S(1)} %pad_maximum_fusion.25.refs_0_), channel_id=1, source_target_pairs={{0,2},{1,3},{2,0},{3,1},{4,6},{5,7},{6,4},{7,5},{8,10},{9,11},{10,... | collective-permute-start | bytes 2654216 | tf_op jit(solution)/shard_map/ppermute | solution.py:41
  862.5 321.1 %reduce-scatter.15.cloned.1.call-start = ((), (), s32[]{:S(2)}) async-start(), calls=%async_computation.12 | async-start | bytes 10616832 | tf_op jit(solution)/shard_map/reduce_scatter | solution.py:412
  906.3 282.5 %reduce-scatter.13.cloned.1.call-start = ((), (), s32[]{:S(2)}) async-start(), calls=%async_computation.11 | async-start | bytes 10616832 | tf_op jit(solution)/shard_map/reduce_scatter | solution.py:412
  917.3 20.0 %collective-permute-start.85 = (bf16[288,1536]{1,0:T(8,128)(2,1)S(1)}, bf16[288,1536]{1,0:T(8,128)(2,1)}, u32[]{:S(2)}, u32[]{:S(2)}) collective-permute-start(bf16[288,1536]{1,0:T(8,128)(2,1)S(1)} %fusion.119), channel_id=1, source_target_pairs={{0,2},{1,3},{2,0},{3,1},{4,6},{5,7},{6,4},{7,5},{8,10},{9,11},{10,... | collective-permute-start | bytes 2654216 | tf_op jit(solution)/shard_map/ppermute | solution.py:41
  921.1 16.3 %collective-permute-start.83 = (bf16[288,1536]{1,0:T(8,128)(2,1)S(1)}, bf16[288,1536]{1,0:T(8,128)(2,1)S(1)}, u32[]{:S(2)}, u32[]{:S(2)}) collective-permute-start(bf16[288,1536]{1,0:T(8,128)(2,1)S(1)} %pad_maximum_fusion.26), channel_id=1, source_target_pairs={{0,1},{1,0},{2,3},{3,2},{4,5},{5,4},{6,7},{7,6},{8,9},{9,8},{10,11... | collective-permute-start | bytes 2654216 | tf_op jit(solution)/shard_map/ppermute | solution.py:41
  950.0 19.0 %collective-permute-start.86 = (bf16[288,1536]{1,0:T(8,128)(2,1)S(1)}, bf16[288,1536]{1,0:T(8,128)(2,1)}, u32[]{:S(2)}, u32[]{:S(2)}) collective-permute-start(bf16[288,1536]{1,0:T(8,128)(2,1)S(1)} %pad_maximum_fusion.27.refs_0_), channel_id=1, source_target_pairs={{0,1},{1,0},{2,3},{3,2},{4,5},{5,4},{6,7},{7,6},{8,9},{9,8},{10,11... | collective-permute-start | bytes 2654216 | tf_op jit(solution)/shard_map/ppermute | solution.py:41
  950.4 20.1 %collective-permute-start.87 = (bf16[288,1536]{1,0:T(8,128)(2,1)S(1)}, bf16[288,1536]{1,0:T(8,128)(2,1)S(1)}, u32[]{:S(2)}, u32[]{:S(2)}) collective-permute-start(bf16[288,1536]{1,0:T(8,128)(2,1)S(1)} %pad_maximum_fusion.27.refs_0_), channel_id=1, source_target_pairs={{0,2},{1,3},{2,0},{3,1},{4,6},{5,7},{6,4},{7,5},{8,10},{9,11},{10,... | collective-permute-start | bytes 2654216 | tf_op jit(solution)/shard_map/ppermute | solution.py:41
  1058.2 19.5 %collective-permute-start.93 = (bf16[288,1536]{1,0:T(8,128)(2,1)}, bf16[288,1536]{1,0:T(8,128)(2,1)}, u32[]{:S(2)}, u32[]{:S(2)}) collective-permute-start(bf16[288,1536]{1,0:T(8,128)(2,1)} %fusion.121), channel_id=1, source_target_pairs={{0,2},{1,3},{2,0},{3,1},{4,6},{5,7},{6,4},{7,5},{8,10},{9,11},{10,... | collective-permute-start | bytes 2654216 | tf_op jit(solution)/shard_map/ppermute | solution.py:41
  1060.1 17.6 %collective-permute-start.91 = (bf16[288,1536]{1,0:T(8,128)(2,1)S(1)}, bf16[288,1536]{1,0:T(8,128)(2,1)}, u32[]{:S(2)}, u32[]{:S(2)}) collective-permute-start(bf16[288,1536]{1,0:T(8,128)(2,1)S(1)} %pad_maximum_fusion.29), channel_id=1, source_target_pairs={{0,1},{1,0},{2,3},{3,2},{4,5},{5,4},{6,7},{7,6},{8,9},{9,8},{10,11... | collective-permute-start | bytes 2654216 | tf_op jit(solution)/shard_map/ppermute | solution.py:41
  1084.5 22.5 %collective-permute-start.96 = (f32[1,9216]{1,0:T(1,128)}, f32[1,9216]{1,0:T(1,128)}, u32[]{:S(2)}, u32[]{:S(2)}) collective-permute-start(f32[1,9216]{1,0:T(1,128)} %get-tuple-element.363), channel_id=1, source_target_pairs={{0,3},{1,2},{2,1},{3,0},{4,7},{5,6},{6,5},{7,4},{8,11},{9,10},{10,... | collective-permute-start | bytes 110600 | tf_op jit(solution)/shard_map/ppermute | solution.py:41
  1086.2 23.3 %collective-permute-start.95 = (f32[1,9216]{1,0:T(1,128)}, f32[1,9216]{1,0:T(1,128)}, u32[]{:S(2)}, u32[]{:S(2)}) collective-permute-start(f32[1,9216]{1,0:T(1,128)} %get-tuple-element.364), channel_id=1, source_target_pairs={{0,2},{1,3},{2,0},{3,1},{4,6},{5,7},{6,4},{7,5},{8,10},{9,11},{10,... | collective-permute-start | bytes 110600 | tf_op jit(solution)/shard_map/ppermute | solution.py:41
  1086.5 25.3 %collective-permute-start.94 = (f32[1,9216]{1,0:T(1,128)}, f32[1,9216]{1,0:T(1,128)}, u32[]{:S(2)}, u32[]{:S(2)}) collective-permute-start(f32[1,9216]{1,0:T(1,128)} %get-tuple-element.362), channel_id=1, source_target_pairs={{0,1},{1,0},{2,3},{3,2},{4,5},{5,4},{6,7},{7,6},{8,9},{9,8},{10,11... | collective-permute-start | bytes 110600 | tf_op jit(solution)/shard_map/ppermute | solution.py:41
  1097.9 13.9 %collective-permute-start.113 = (f32[4,4,672]{2,1,0:T(4,128)S(1)}, f32[4,4,672]{2,1,0:T(4,128)S(1)}, u32[]{:S(2)}, u32[]{:S(2)}) collective-permute-start(f32[4,4,672]{2,1,0:T(4,128)S(1)} %get-tuple-element.313), channel_id=1, source_target_pairs={{0,28},{4,24},{8,20},{12,16},{16,12},{20,8},{24,4},{28,0},{1,29},{... | collective-permute-start | bytes 129032 | tf_op jit(solution)/shard_map/ppermute | solution.py:41
  1097.9 13.9 %collective-permute-start.112 = (f32[4,4,672]{2,1,0:T(4,128)S(1)}, f32[4,4,672]{2,1,0:T(4,128)}, u32[]{:S(2)}, u32[]{:S(2)}) collective-permute-start(f32[4,4,672]{2,1,0:T(4,128)S(1)} %get-tuple-element.314), channel_id=1, source_target_pairs={{0,24},{4,28},{8,16},{12,20},{16,8},{20,12},{24,0},{28,4},{1,25},{... | collective-permute-start | bytes 129032 | tf_op jit(solution)/shard_map/ppermute | solution.py:41
  1114.7 16.1 %collective-permute-start.97 = (f32[1,9216]{1,0:T(1,128)S(1)}, f32[1,9216]{1,0:T(1,128)S(1)}, u32[]{:S(2)}, u32[]{:S(2)}) collective-permute-start(f32[1,9216]{1,0:T(1,128)S(1)} %fusion.205), channel_id=1, source_target_pairs={{0,4},{4,0},{8,12},{12,8},{16,20},{20,16},{24,28},{28,24},{1,5},{5... | collective-permute-start | bytes 110600 | tf_op jit(solution)/shard_map/ppermute | solution.py:41
  1140.2 15.5 %collective-permute-start.105 = (f32[8,9216]{1,0:T(8,128)S(1)}, f32[8,9216]{1,0:T(8,128)S(1)}, u32[]{:S(2)}, u32[]{:S(2)}) collective-permute-start(f32[8,9216]{1,0:T(8,128)S(1)} %concatenate.295), channel_id=1, source_target_pairs={{0,2},{1,3},{2,0},{3,1},{4,6},{5,7},{6,4},{7,5},{8,10},{9,11},{10,... | collective-permute-start | bytes 884744 | tf_op jit(solution)/shard_map/ppermute | solution.py:41
  (334 other events, 2728.2 us)
Sparse Core Ops, SparseCore 0:
  13.0 103.7 all-gather.10
  119.0 89.1 all-gather.14
  209.8 89.1 all-gather.16
  300.4 89.1 all-gather.12
  391.1 89.2 all-gather.18
  481.9 89.1 all-gather.20
  573.4 97.9 reduce-scatter.6
  673.7 97.8 reduce-scatter.8
  778.3 97.9 reduce-scatter.10
  878.5 97.8 reduce-scatter.16
  978.7 97.8 reduce-scatter.14
  1078.7 108.9 reduce-scatter.12
